TPU v7x, 128 devices: a whole 4x4x4 slice. The times are simulated.
128 devices in a mesh: row: 8 (over y, core), col: 16 (over z, x).
Axes of the slice: x: 4, y: 4, z: 4, core: 2. Of those that a mesh axis runs over, the one named last changes fastest.
Arguments:
- hidden_states: bfloat16 [1024, 2048], P('col', 'row'), may hold values from -20 to 20
- input_gain: float32 [2, 2048], P(None, 'row'), may hold values from 0.25 to 1.75
- inner_weight: bfloat16 [2, 2048, 2, 4096], P(None, 'row', None, 'col'), may hold values from -0.125 to 0.125
- proj_weight: bfloat16 [2, 2048, 256], P(None, 'row'), may hold values from -0.125 to 0.125
- step_weight: bfloat16 [2, 2048, 64], P(None, 'row', 'col'), may hold values from -0.125 to 0.125
- inner_kernel: float32 [2, 4, 4096], P(None, None, 'col'), may hold values from -3 to 3
- proj_kernel: float32 [2, 4, 256], replicated, may hold values from -3 to 3
- step_bias: float32 [2, 64], P(None, 'col'), may hold values from -5 to -1
- decay_log: float32 [2, 64], P(None, 'col'), may hold values from -2 to 1
- skip_gain: float32 [2, 64], P(None, 'col'), may hold values from 0.5 to 1.5
- norm_gain: float32 [2, 4096], P(None, 'col'), may hold values from 0.25 to 1.75
- out_weight: bfloat16 [2, 4096, 2048], P(None, 'col', 'row'), may hold values from -0.09375 to 0.09375
- inner_cache: bfloat16 [2, 64, 3, 4096], P(None, 'row', None, 'col'), may hold values from -6 to 6
- proj_cache: bfloat16 [2, 64, 3, 256], P(None, 'row'), may hold values from -6 to 6
- state_cache: float32 [2, 64, 64, 64, 128], P(None, 'row', 'col'), may hold values from -1.2 to 1.2
- accepted: int32 [64], P('row'), may hold values from 1 to 16
- owners: int32 [64], P('row'), may hold values from 0 to 15, as said below
- tenant_ranges: int32 [4, 2], replicated, may hold values from 0 to 64, as said below
Outputs:
- hidden_output: bfloat16 [1024, 2048], P('col', 'row')
- step_states: bfloat16 [2, 64, 16, 64, 64, 128], P(None, 'row', None, 'col')
- owned_states: bfloat16 [8, 16, 2, 2, 64, 64, 128], P('row', 'col')
Inputs may be any that keep to these rules, and one draw needn't show every extreme that they name: `owners`: within the requests of one index of row (aligned blocks of 8) no owner appears more than 2 times, and in every block some owner appears exactly 2 times. `tenant_ranges`: the ranges are in order, disjoint and not empty; exactly 8 requests lie in no range.
All inputs are finite; a program needn't handle non-finite values.
Results may differ from a plain program's by a relative error of at most 0.024.
Values may be sent and summed in bfloat16 or wider, within the bound.
No kernel may reach another device: no remote copies, remote signals or barrier semaphores. Data moves between devices by JAX's collectives and lax.ppermute only.
A program may use at most 128 MiB of HBM per device.

v0:
```python
import jax
import jax.numpy as jnp
from jax import lax
from jax.sharding import PartitionSpec as P

S = 16
SEND_CAP = 2


EPSILON = 1e-05


def conv_silu(prefix, incoming, kernel):
    joined = jnp.concatenate([prefix, incoming], axis=1)
    length = incoming.shape[1]
    summed = joined[:, 0:length, :] * kernel[0]
    for offset in range(1, kernel.shape[0]):
        summed = summed + joined[:, offset : offset + length, :] * kernel[offset]
    return jax.nn.silu(summed)


def ssm_scan(decays, deltas, inner_values, b_values, c_values, skip_values, start_state):

    def advance(carried, packed):
        decay_now, delta_now, value_now, b_now, c_now = packed
        updated = (
            decay_now[:, :, None, None] * carried
            + (delta_now[:, :, None] * value_now)[:, :, :, None] * b_now[:, None, None, :]
        )
        output = (
            jnp.einsum("rhpn,rn->rhp", updated, c_now, precision=lax.Precision.HIGHEST)
            + skip_values[None, :, None] * value_now
        )
        return (updated, (output, updated.astype(jnp.bfloat16)))

    time_major = tuple(
        (
            jnp.moveaxis(member, 1, 0)
            for member in (decays, deltas, inner_values, b_values, c_values)
        )
    )
    last_state, (outputs, states) = lax.scan(advance, start_state, time_major)
    return (jnp.moveaxis(outputs, 0, 1), jnp.moveaxis(states, 0, 1))


def local(
    hidden_states,
    input_gain,
    inner_weight,
    proj_weight,
    step_weight,
    inner_kernel,
    proj_kernel,
    step_bias,
    decay_log,
    skip_gain,
    norm_gain,
    out_weight,
    inner_cache,
    proj_cache,
    state_cache,
    accepted,
    owners,
    tenant_ranges,
):
    layer_count = inner_weight.shape[0]
    row_width = inner_weight.shape[1]
    inner_local = inner_weight.shape[3]
    heads_local = step_weight.shape[2]
    head_size = inner_local // heads_local
    state_size = proj_weight.shape[2] // 2
    requests_local = state_cache.shape[1]
    draft_steps = S
    row_count = lax.axis_size("row")
    col_count = lax.axis_size("col")
    model_width = row_width * row_count
    inner_width = inner_local * col_count
    token_rows = requests_local * draft_steps
    local_ids = jnp.arange(requests_local, dtype=jnp.int32)
    request_ids = lax.axis_index("row") * requests_local + local_ids
    live_mask = jnp.any(
        (request_ids[:, None] >= tenant_ranges[None, :, 0])
        & (request_ids[:, None] < tenant_ranges[None, :, 1]),
        axis=1,
    )
    earlier = (owners[:, None] == owners[None, :]) & (local_ids[None, :] < local_ids[:, None])
    slot_ranks = jnp.sum(earlier.astype(jnp.int32), axis=1)
    slot_ids = owners * SEND_CAP + slot_ranks
    slot_grid = jnp.arange(col_count * SEND_CAP, dtype=jnp.int32)
    step_grid = jnp.arange(draft_steps, dtype=jnp.int32)
    picker = (
        (slot_grid[:, None, None] == slot_ids[None, :, None])
        & (step_grid[None, None, :] == accepted[None, :, None] - 1)
        & live_mask[None, :, None]
    )
    picker = picker.astype(jnp.bfloat16).reshape(col_count * SEND_CAP, token_rows)
    hidden = hidden_states
    step_outputs = []
    chosen_layers = []
    for layer_index in range(layer_count):
        all_tokens = lax.all_gather(hidden, "col", axis=0, tiled=True)
        tokens_f = all_tokens.astype(jnp.float32)
        scaled = (tokens_f * input_gain[layer_index]).astype(jnp.bfloat16)
        square_part = jnp.sum(tokens_f * tokens_f, axis=1)
        inner_part = jnp.dot(
            scaled,
            inner_weight[layer_index].reshape(row_width, 2 * inner_local),
            preferred_element_type=jnp.float32,
        )
        step_part = jnp.dot(scaled, step_weight[layer_index], preferred_element_type=jnp.float32)
        proj_part = jnp.dot(scaled, proj_weight[layer_index], preferred_element_type=jnp.float32)
        inner_sum, step_sum, proj_sum, square_sum = (
            lax.psum_scatter(inner_part, "row", scatter_dimension=0, tiled=True),
            lax.psum_scatter(step_part, "row", scatter_dimension=0, tiled=True),
            lax.psum_scatter(proj_part, "row", scatter_dimension=0, tiled=True),
            lax.psum_scatter(square_part, "row", scatter_dimension=0, tiled=True),
        )
        inverse_rms = lax.rsqrt(square_sum / model_width + EPSILON)
        inner_vals = inner_sum * inverse_rms[:, None]
        gate_vals = inner_vals[:, :inner_local]
        raw_inner = inner_vals[:, inner_local:].reshape(requests_local, draft_steps, inner_local)
        raw_proj = (proj_sum * inverse_rms[:, None]).reshape(
            requests_local, draft_steps, 2 * state_size
        )
        conv_inner = conv_silu(
            inner_cache[layer_index].astype(jnp.float32), raw_inner, inner_kernel[layer_index]
        )
        conv_proj = conv_silu(
            proj_cache[layer_index].astype(jnp.float32), raw_proj, proj_kernel[layer_index]
        )
        deltas = jax.nn.softplus(
            (step_sum * inverse_rms[:, None]).reshape(requests_local, draft_steps, heads_local)
            + step_bias[layer_index]
        )
        decays = jnp.exp(-deltas * jnp.exp(decay_log[layer_index]))
        outputs, states = ssm_scan(
            decays,
            deltas,
            conv_inner.reshape(requests_local, draft_steps, heads_local, head_size),
            conv_proj[..., :state_size],
            conv_proj[..., state_size:],
            skip_gain[layer_index],
            state_cache[layer_index],
        )
        step_outputs.append(states)
        gated_raw = outputs.reshape(token_rows, inner_local) * jax.nn.silu(gate_vals)
        gate_square = lax.psum(jnp.sum(gated_raw * gated_raw, axis=1), "col")
        gated = (
            gated_raw
            * norm_gain[layer_index]
            * lax.rsqrt(gate_square / inner_width + EPSILON)[:, None]
        ).astype(jnp.bfloat16)
        layer_weight = out_weight[layer_index]
        partial_out = jnp.dot(
            lax.all_gather(gated, "row", axis=0, tiled=True),
            layer_weight,
            preferred_element_type=jnp.float32,
        )
        out_sum = lax.psum_scatter(
            partial_out.astype(jnp.bfloat16), "col", scatter_dimension=0, tiled=True
        ).astype(jnp.float32)
        hidden = (hidden.astype(jnp.float32) + out_sum).astype(jnp.bfloat16)
        chosen = jnp.dot(
            picker,
            states.reshape(token_rows, heads_local * head_size * state_size),
            preferred_element_type=jnp.float32,
        )
        chosen = chosen.astype(jnp.bfloat16).reshape(
            col_count, SEND_CAP, heads_local, head_size, state_size
        )
        chosen_layers.append(chosen)
    gathered = lax.all_to_all(
        jnp.stack(chosen_layers, axis=2), "col", split_axis=0, concat_axis=3, tiled=True
    )
    owned_block = gathered[None]
    step_all = jnp.stack(step_outputs, axis=0)
    return (hidden, step_all, owned_block)


def solution(mesh):
    placed = (
        P("col", "row"),
        P(None, "row"),
        P(None, "row", None, "col"),
        P(None, "row", None),
        P(None, "row", "col"),
        P(None, None, "col"),
        P(),
        P(None, "col"),
        P(None, "col"),
        P(None, "col"),
        P(None, "col"),
        P(None, "col", "row"),
        P(None, "row", None, "col"),
        P(None, "row", None, None),
        P(None, "row", "col", None, None),
        P("row"),
        P("row"),
        P(),
    )
    return jax.shard_map(
        local,
        mesh=mesh,
        in_specs=placed,
        out_specs=(
            P("col", "row"),
            P(None, "row", None, "col", None, None),
            P("row", "col", None, None, None, None, None),
        ),
        check_vma=False,
    )
```

profile of v0, /device:TPU:32, one launch (start us, length us, event | category | flops | bytes accessed | tf_op | source)
XLA Modules:
  0.0 788.0 jit_solution(10721165272953729870)
XLA Ops:
  8.6 24.6 %all_gather.12 = bf16[1024,256]{1,0:T(8,128)(2,1)S(1)} all-gather(bf16[64,256]{1,0:T(8,128)(2,1)} %param.22), channel_id=1, replica_groups=mesh['row'=8,'col'=16] {'col'}, dimensions={0}, use_global_device_ids=true | all-gather | bytes 557056 | tf_op jit(solution)/shard_map/all_gather | solution.py:101
  42.1 12.5 %all-reduce = f32[1024]{0:T(1024)S(1)} all-reduce(f32[1024]{0:T(1024)S(1)} %fusion.5), channel_id=3, replica_groups=mesh['row'=8,'col'=16] {'row'}, use_global_device_ids=true, to_apply=%region_2.0.clone | all-reduce | flops 1024 | bytes 8192
  59.9 6.1 reduce-scatter.25.cloned.1.call-done
  68.5 31.3 %reduce-scatter.15.cloned.1.call-done = f32[128,256]{1,0:T(8,128)} async-done(((f32[1024,256]{1,0:T(8,128)}), f32[128,256]{1,0:T(8,128)}) %reduce-scatter.15.cloned.1.call-update) | async-done | bytes 131088 | tf_op jit(solution)/shard_map/reduce_scatter | solution.py:115
  101.6 33.8 %reduce-scatter.13.cloned.1.call-done = f32[128,512]{1,0:T(8,128)} async-done(((f32[1024,512]{1,0:T(8,128)}), f32[128,512]{1,0:T(8,128)}) %reduce-scatter.13.cloned.1.call-update) | async-done | bytes 262160 | tf_op jit(solution)/shard_map/reduce_scatter | solution.py:113
  136.9 5.4 broadcast.153.clone2
  142.3 103.3 %while.28 = (s32[]{:T(128)}, f32[8,4,64,128]{3,2,1,0:T(8,128)S(1)}, f32[16,8,4,64]{3,2,1,0:T(4,128)S(1)}, bf16[16,8,4,64,128]{4,3,2,0,1:T(8,128)(2,1)}, f32[16,8...) while((s32[]{:T(128)}, f32[8,4,64,128]{3,2,1,0:T(8,128)S(1)}, ...), condition=%wide.region_6.0_spmd, body=%wide.region_5.0_spmd.sunk | while | flops 4200450 | bytes 3777949 | solution.py:42
  145.4 2.5 fusion.99
  151.9 2.5 fusion.99
  171.3 2.5 fusion.99
  177.7 2.5 fusion.99
  190.6 2.5 fusion.99
  203.6 2.5 fusion.99
  210.0 2.5 fusion.99
  216.5 2.5 fusion.99
  222.9 2.5 fusion.99
  229.4 2.5 fusion.99
  235.8 2.5 fusion.99
  242.3 2.5 fusion.99
  246.0 34.4 %psum.14 = f32[128]{0:T(128)S(1)} all-reduce(f32[128]{0:T(128)S(1)} %get-tuple-element.179), channel_id=1, replica_groups=mesh['row'=8,'col'=16] {'col'}, use_global_device_ids=true, to_apply=%region_8.9 | all-reduce | flops 128 | bytes 1024 | tf_op jit(solution)/shard_map/psum | solution.py:147
  281.2 13.1 %all_gather.13 = bf16[1024,256]{1,0:T(8,128)(2,1)S(1)} all-gather(bf16[128,256]{1,0:T(8,128)(2,1)S(1)} %multiply_convert_fusion.1), channel_id=1, replica_groups=mesh['row'=8,'col'=16] {'row'}, dimensions={0}, use_global_device_ids=true | all-gather | bytes 589824 | tf_op jit(solution)/shard_map/all_gather | solution.py:155
  296.4 73.0 %reduce-scatter.17.cloned.1.call-done = bf16[64,256]{1,0:T(8,128)(2,1)} async-done(((bf16[1024,256]{1,0:T(8,128)(2,1)}), bf16[64,256]{1,0:T(8,128)(2,1)}) %reduce-scatter.17.cloned.1.call-update) | async-done | bytes 32784 | tf_op jit(solution)/shard_map/reduce_scatter | solution.py:159
  370.1 22.3 %all_gather.14 = bf16[1024,256]{1,0:T(8,128)(2,1)S(1)} all-gather(bf16[64,256]{1,0:T(8,128)(2,1)S(1)} %add_convert_fusion.1), channel_id=1, replica_groups=mesh['row'=8,'col'=16] {'col'}, dimensions={0}, use_global_device_ids=true | all-gather | bytes 557056 | tf_op jit(solution)/shard_map/all_gather | solution.py:101
  398.8 13.3 %reshape.291 = bf16[128,32768]{1,0:T(8,128)(2,1)} reshape(bf16[8,16,4,64,128]{4,3,2,1,0:T(8,128)(2,1)} %bitcast.249) | data formatting | bytes 16777216 | tf_op jit(solution)/shard_map/reshape | solution.py:165
  412.1 4.7 fusion.2
  418.8 12.6 %all-reduce.1 = f32[1024]{0:T(1024)S(1)} all-reduce(f32[1024]{0:T(1024)S(1)} %fusion.7), channel_id=8, replica_groups=mesh['row'=8,'col'=16] {'row'}, use_global_device_ids=true, to_apply=%region_12.13.clone | all-reduce | flops 1024 | bytes 8192
  432.8 25.6 %reduce-scatter.21.cloned.1.call-done = f32[128,256]{1,0:T(8,128)} async-done(((f32[1024,256]{1,0:T(8,128)}), f32[128,256]{1,0:T(8,128)}) %reduce-scatter.21.cloned.1.call-update) | async-done | bytes 131088 | tf_op jit(solution)/shard_map/reduce_scatter | solution.py:115
  459.6 34.4 %reduce-scatter.19.cloned.1.call-done = f32[128,512]{1,0:T(8,128)} async-done(((f32[1024,512]{1,0:T(8,128)}), f32[128,512]{1,0:T(8,128)}) %reduce-scatter.19.cloned.1.call-update) | async-done | bytes 262160 | tf_op jit(solution)/shard_map/reduce_scatter | solution.py:113
  495.5 5.4 broadcast.153.clone
  500.9 70.9 %while.29 = (s32[]{:T(128)}, f32[8,4,64,128]{3,2,1,0:T(8,128)S(1)}, f32[16,8,4,64]{3,2,1,0:T(4,128)S(1)}, bf16[16,8,4,64,128]{4,3,2,0,1:T(8,128)(2,1)}, f32[16,8...) while((s32[]{:T(128)}, f32[8,4,64,128]{3,2,1,0:T(8,128)S(1)}, ...), condition=%wide.region_16.17_spmd, body=%wide.region_15.16_spmd.sunk | while | flops 4200450 | bytes 3778445 | solution.py:42
  502.7 2.5 fusion.102
  507.1 2.5 fusion.102
  511.6 2.5 fusion.102
  516.0 2.5 fusion.102
  524.9 2.5 fusion.102
  529.3 2.5 fusion.102
  533.7 2.5 fusion.102
  556.0 2.5 fusion.102
  560.4 2.5 fusion.102
  564.8 2.5 fusion.102
  571.9 13.3 %reshape.292 = bf16[128,32768]{1,0:T(8,128)(2,1)} reshape(bf16[8,16,4,64,128]{4,3,2,1,0:T(8,128)(2,1)} %bitcast.247) | data formatting | bytes 16777216 | tf_op jit(solution)/shard_map/reshape | solution.py:165
  585.1 4.8 fusion.3
  592.8 7.4 all-to-all-start
  600.6 77.6 %psum.15 = f32[128]{0:T(128)S(1)} all-reduce(f32[128]{0:T(128)S(1)} %get-tuple-element.177), channel_id=1, replica_groups=mesh['row'=8,'col'=16] {'col'}, use_global_device_ids=true, to_apply=%region_18.19 | all-reduce | flops 128 | bytes 1024 | tf_op jit(solution)/shard_map/psum | solution.py:147
  678.4 19.8 %all_gather.15 = bf16[1024,256]{1,0:T(8,128)(2,1)S(1)} all-gather(bf16[128,256]{1,0:T(8,128)(2,1)S(1)} %multiply_convert_fusion), channel_id=1, replica_groups=mesh['row'=8,'col'=16] {'row'}, dimensions={0}, use_global_device_ids=true | all-gather | bytes 589824 | tf_op jit(solution)/shard_map/all_gather | solution.py:155
  699.3 13.8 %pad_maximum_fusion = bf16[2,8,16,4,64,128]{5,4,3,2,1,0:T(8,128)(2,1)} fusion(bf16[1,8,16,4,64,128]{5,4,3,2,1,0:T(8,128)(2,1)} %bitcast.248, bf16[1,8,16,4,64,128]{5,4,3,2,1,0:T(8,128)(2,1)} %bitcast.250), kind=kLoop, calls=%fused_computation.22 | loop fusion | flops 8388608 | bytes 33554432 | tf_op jit(solution)/shard_map/stack | solution.py:176
  713.1 60.7 %reduce-scatter.23.cloned.1.call-done = bf16[64,256]{1,0:T(8,128)(2,1)} async-done(((bf16[1024,256]{1,0:T(8,128)(2,1)}), bf16[64,256]{1,0:T(8,128)(2,1)}) %reduce-scatter.23.cloned.1.call-update) | async-done | bytes 32784 | tf_op jit(solution)/shard_map/reduce_scatter | solution.py:159
  775.2 6.0 copy.143
  (423 shorter events, 160.6 us)
Async XLA Ops:
  7.2 33.4 %copy-start.28 = (u32[128]{0:T(128)S(1)}, u32[128]{0:T(128)}, u32[]{:S(2)}) copy-start(u32[128]{0:T(128)} %constant.80) | copy-start | bytes 1540
  7.2 47.4 %copy-start.22 = (f32[2,4]{1,0:T(2,128)S(1)}, f32[2,4]{1,0:T(2,128)}, u32[]{:S(2)}) copy-start(f32[2,4]{1,0:T(2,128)} %param.31) | copy-start | bytes 100
  7.2 48.0 %copy-start.21 = (f32[2,256]{1,0:T(2,128)S(1)}, f32[2,256]{1,0:T(2,128)}, u32[]{:S(2)}) copy-start(f32[2,256]{1,0:T(2,128)} %param.32) | copy-start | bytes 6148
  7.2 48.6 %copy-start.25 = (f32[2,4]{1,0:T(2,128)S(1)}, f32[2,4]{1,0:T(2,128)}, u32[]{:S(2)}) copy-start(f32[2,4]{1,0:T(2,128)} %param.30) | copy-start | bytes 100
  7.2 48.6 %copy-start.24 = (f32[2,4]{1,0:T(2,128)S(1)}, f32[2,4]{1,0:T(2,128)}, u32[]{:S(2)}) copy-start(f32[2,4]{1,0:T(2,128)} %param.29) | copy-start | bytes 100
  7.2 49.1 %copy-start.8 = (f32[2,4,256]{2,1,0:T(4,128)S(1)}, f32[2,4,256]{2,1,0:T(4,128)}, u32[]{:S(2)}) copy-start(f32[2,4,256]{2,1,0:T(4,128)} %param.27) | copy-start | bytes 24580
  7.2 49.7 %copy-start.9 = (f32[2,4,256]{2,1,0:T(4,128)S(1)}, f32[2,4,256]{2,1,0:T(4,128)}, u32[]{:S(2)}) copy-start(f32[2,4,256]{2,1,0:T(4,128)} %param.28) | copy-start | bytes 24580
  7.2 50.3 %copy-start.5 = (bf16[2,8,3,256]{3,1,2,0:T(8,128)(2,1)S(1)}, bf16[2,8,3,256]{3,1,2,0:T(8,128)(2,1)}, u32[]{:S(2)}) copy-start(bf16[2,8,3,256]{3,1,2,0:T(8,128)(2,1)} %param.34) | copy-start | bytes 73732
  7.3 50.3 %copy-start.6 = (bf16[2,8,3,256]{3,1,2,0:T(8,128)(2,1)S(1)}, bf16[2,8,3,256]{3,1,2,0:T(8,128)(2,1)}, u32[]{:S(2)}) copy-start(bf16[2,8,3,256]{3,1,2,0:T(8,128)(2,1)} %param.35) | copy-start | bytes 73732
  7.3 58.8 %reduce-scatter.25.cloned.1.call-start = ((), (), s32[]{:S(2)}) async-start(), calls=%async_computation.15 | async-start | bytes 589824
  35.0 64.9 %reduce-scatter.15.cloned.1.call-start = ((), (), s32[]{:S(2)}) async-start(), calls=%async_computation.10 | async-start | bytes 1179648 | tf_op jit(solution)/shard_map/reduce_scatter | solution.py:115
  37.3 98.2 %reduce-scatter.13.cloned.1.call-start = ((), (), s32[]{:S(2)}) async-start(), calls=%async_computation.9 | async-start | bytes 2359296 | tf_op jit(solution)/shard_map/reduce_scatter | solution.py:113
  40.5 328.8 %reduce-scatter.17.cloned.1.call-start = ((), (), s32[]{:S(2)}) async-start(), calls=%async_computation.11 | async-start | bytes 557056 | tf_op jit(solution)/shard_map/reduce_scatter | solution.py:159
  142.3 227.1 %copy-start.3 = (bf16[64,256]{1,0:T(8,128)(2,1)S(1)}, bf16[64,256]{1,0:T(8,128)(2,1)}, u32[]{:S(2)}) copy-start(bf16[64,256]{1,0:T(8,128)(2,1)} %param.22) | copy-start | bytes 98308
  142.3 252.0 %copy-start.1 = (bf16[2,256,256]{2,1,0:T(8,128)(2,1)S(1)}, bf16[2,256,256]{2,1,0:T(8,128)(2,1)}, u32[]{:S(2)}) copy-start(bf16[2,256,256]{2,1,0:T(8,128)(2,1)} %param.25) | copy-start | bytes 786436
  245.6 150.8 %copy-start.7 = (f32[1,256]{1,0:T(1,128)S(1)}, f32[1,256]{1,0:T(1,128)}, u32[]{:S(2)}) copy-start(f32[1,256]{1,0:T(1,128)} %get-tuple-element.219) | copy-start | bytes 3076
  245.6 152.6 %copy-start.27 = (s32[8]{0:T(128)S(1)}, s32[8]{0:T(128)}, u32[]{:S(2)}) copy-start(s32[8]{0:T(128)} %param.38) | copy-start | bytes 100
  245.6 152.8 %copy-start.23 = (s32[4,2]{0,1:T(2,128)S(1)}, s32[4,2]{0,1:T(2,128)}, u32[]{:S(2)}) copy-start(s32[4,2]{0,1:T(2,128)} %param.39) | copy-start | bytes 100
  245.6 152.9 %copy-start.26 = (s32[8]{0:T(128)S(1)}, s32[8]{0:T(128)}, u32[]{:S(2)}) copy-start(s32[8]{0:T(128)} %param.37) | copy-start | bytes 100
  296.3 135.2 %reduce-scatter.27.cloned.1.call-start = ((), (), s32[]{:S(2)}) async-start(), calls=%async_computation.16 | async-start | bytes 589824
  394.2 64.2 %reduce-scatter.21.cloned.1.call-start = ((), (), s32[]{:S(2)}) async-start(), calls=%async_computation.13 | async-start | bytes 1179648 | tf_op jit(solution)/shard_map/reduce_scatter | solution.py:115
  396.3 97.8 %reduce-scatter.19.cloned.1.call-start = ((), (), s32[]{:S(2)}) async-start(), calls=%async_computation.12 | async-start | bytes 2359296 | tf_op jit(solution)/shard_map/reduce_scatter | solution.py:113
  412.0 20.5 %copy-start.19 = (f32[4]{0:T(128)S(1)}, f32[4]{0:T(128)}, u32[]{:S(2)}) copy-start(f32[4]{0:T(128)} %get-tuple-element.225) | copy-start | bytes 52
  412.0 20.5 %copy-start.20 = (f32[4]{0:T(128)S(1)}, f32[4]{0:T(128)}, u32[]{:S(2)}) copy-start(f32[4]{0:T(128)} %get-tuple-element.229) | copy-start | bytes 52
  412.1 47.5 %copy-start.4 = (f32[8,3,256]{2,0,1:T(8,128)S(1)}, f32[8,3,256]{2,0,1:T(8,128)}, u32[]{:S(2)}) copy-start(f32[8,3,256]{2,0,1:T(8,128)} %get-tuple-element.193) | copy-start | bytes 73732
  412.1 47.5 %copy-start.14 = (f32[1,1,256]{2,1,0:T(1,128)S(1)}, f32[1,1,256]{2,1,0:T(1,128)}, u32[]{:S(2)}) copy-start(f32[1,1,256]{2,1,0:T(1,128)} %get-tuple-element.201) | copy-start | bytes 3076
  412.1 47.5 %copy-start.15 = (f32[1,1,256]{2,1,0:T(1,128)S(1)}, f32[1,1,256]{2,1,0:T(1,128)}, u32[]{:S(2)}) copy-start(f32[1,1,256]{2,1,0:T(1,128)} %get-tuple-element.202) | copy-start | bytes 3076
  412.1 47.5 %copy-start.16 = (f32[1,1,256]{2,1,0:T(1,128)S(1)}, f32[1,1,256]{2,1,0:T(1,128)}, u32[]{:S(2)}) copy-start(f32[1,1,256]{2,1,0:T(1,128)} %get-tuple-element.207) | copy-start | bytes 3076
  412.1 47.5 %copy-start.17 = (f32[1,1,256]{2,1,0:T(1,128)S(1)}, f32[1,1,256]{2,1,0:T(1,128)}, u32[]{:S(2)}) copy-start(f32[1,1,256]{2,1,0:T(1,128)} %get-tuple-element.208) | copy-start | bytes 3076
  412.1 83.1 %copy-start.10 = (f32[1,1,256]{2,1,0:T(1,128)S(1)}, f32[1,1,256]{2,1,0:T(1,128)}, u32[]{:S(2)}) copy-start(f32[1,1,256]{2,1,0:T(1,128)} %get-tuple-element.209) | copy-start | bytes 3076
  412.1 83.1 %copy-start.11 = (f32[1,1,256]{2,1,0:T(1,128)S(1)}, f32[1,1,256]{2,1,0:T(1,128)}, u32[]{:S(2)}) copy-start(f32[1,1,256]{2,1,0:T(1,128)} %get-tuple-element.210) | copy-start | bytes 3076
  412.1 83.1 %copy-start.12 = (f32[1,1,256]{2,1,0:T(1,128)S(1)}, f32[1,1,256]{2,1,0:T(1,128)}, u32[]{:S(2)}) copy-start(f32[1,1,256]{2,1,0:T(1,128)} %get-tuple-element.215) | copy-start | bytes 3076
  412.1 83.1 %copy-start.13 = (f32[1,1,256]{2,1,0:T(1,128)S(1)}, f32[1,1,256]{2,1,0:T(1,128)}, u32[]{:S(2)}) copy-start(f32[1,1,256]{2,1,0:T(1,128)} %get-tuple-element.216) | copy-start | bytes 3076
  585.1 5.3 copy-start
  590.4 87.8 %copy-start.18 = (f32[1,256]{1,0:T(1,128)S(1)}, f32[1,256]{1,0:T(1,128)}, u32[]{:S(2)}) copy-start(f32[1,256]{1,0:T(1,128)} %get-tuple-element.217) | copy-start | bytes 3076
  590.4 107.7 %copy-start.2 = (bf16[2,256,256]{2,1,0:T(8,128)(2,1)S(1)}, bf16[2,256,256]{2,1,0:T(8,128)(2,1)}, u32[]{:S(2)}) copy-start(bf16[2,256,256]{2,1,0:T(8,128)(2,1)} %param.33) | copy-start | bytes 786436
  592.8 182.4 %all-to-all-start = ((bf16[16,2,2,4,64,128]{5,4,3,1,2,0:T(8,128)(2,1)}), bf16[16,2,2,4,64,128]{5,4,3,1,2,0:T(8,128)(2,1)}, u32[]{:S(2)}, u32[]{:S(2)}) async-start(bf16[16,2,2,4,64,128]{5,4,3,1,2,0:T(8,128)(2,1)} %pad_maximum_fusion.1), calls=%async_computation.6 | async-start | bytes 8388608 | tf_op jit(solution)/shard_map/all_to_all | solution.py:172
  600.2 173.6 %reduce-scatter.23.cloned.1.call-start = ((), (), s32[]{:S(2)}) async-start(), calls=%async_computation.14 | async-start | bytes 557056 | tf_op jit(solution)/shard_map/reduce_scatter | solution.py:159
Sparse Core Ops, SparseCore 0:
  35.1 30.8 reduce-scatter.24
  69.1 30.6 reduce-scatter.14
  103.0 32.4 reduce-scatter.12
  296.4 72.8 reduce-scatter.16
  394.4 30.9 reduce-scatter.26
  427.7 30.6 reduce-scatter.20
  461.5 32.4 reduce-scatter.18
  699.4 74.3 reduce-scatter.22
where the time goes:
time: 792 us; the launch traced here: 788 us
  waiting for transfers between devices  265 us (33%)
  blocking collectives  217 us (27%)
  matrix products  105 us (13%)
  other arithmetic  90.8 us (11%)
  local copies, waits for them, and re-layouts  86.9 us (11%)
  between operations  15.4 us (2%)
    reduce_scatter x2, waiting for transfers between devices, local(): lax.psum_scatter(partial_out.astype(jnp.bfloat16), 'col', scatter_dimensi...  134 us
    psum x2, blocking collectives, local(): gate_square = lax.psum(jnp.sum(gated_raw * gated_raw, axis=1), 'col')  112 us
    dot_general x32, matrix products, advance(): jnp.einsum('rhpn,rn->rhp', updated, c_now, precision=lax.Precision.HIGHEST)  80.9 us
    reduce_scatter x2, waiting for transfers between devices, local(): lax.psum_scatter(inner_part, 'row', scatter_dimension=0, tiled=True)  68.2 us
    dynamic_update_slice x64, other arithmetic, ssm_scan(): last_state, (outputs, states) = lax.scan(advance, start_state, time_major)  62.7 us
    reduce_scatter x2, waiting for transfers between devices, local(): lax.psum_scatter(proj_part, 'row', scatter_dimension=0, tiled=True)  56.9 us
    all_gather x2, blocking collectives, local(): all_tokens = lax.all_gather(hidden, 'col', axis=0, tiled=True)  46.9 us
    all_gather x2, blocking collectives, local(): lax.all_gather(gated, 'row', axis=0, tiled=True)  32.9 us
  transfers between devices with their start and end apart: 9, of which 7 were waited for; matrix products, arithmetic and copies ran while one was open for 8% of the time, Pallas kernels for 0%

commit v1 on v0

v1 whole, which is shorter than its diff:
```python
import jax
import jax.numpy as jnp
from jax import lax
from jax.experimental import pallas as pl
from jax.experimental.pallas import tpu as pltpu
from jax.sharding import PartitionSpec as P

S = 16
SEND_CAP = 2
EPSILON = 1e-05
ROWS = 8
COLS = 16
BF = jnp.bfloat16
F32 = jnp.float32
SUM_ROWS = 16


def silu(v):
    return v / (1.0 + jnp.exp(-v))


def softplus(v):
    return jnp.maximum(v, 0.0) + jnp.log1p(jnp.exp(-jnp.abs(v)))


def mixer_body(
    layer,
    slots_ref,
    accepted_ref,
    bias_ref,
    decay_log_ref,
    skip_ref,
    hidden_ref,
    weight_ref,
    out_weight_ref,
    inner_kernel_ref,
    proj_kernel_ref,
    norm_gain_ref,
    inner_cache_ref,
    proj_cache_ref,
    state_ref,
    *rest,
):
    (
        steps_ref,
        send_ref,
        part_ref,
        z_s,
        x_pad,
        p_pad,
        x_s,
        dx_s,
        b_s,
        c_s,
        dec_s,
        ydiag_s,
        ecum_s,
        yg_s,
        g2_s,
    ) = rest[-15:]
    q = pl.program_id(0)
    requests = x_pad.shape[0]
    tokens = requests * S
    width = z_s.shape[1]
    state_size = b_s.shape[1]
    heads = dec_s.shape[1] // 128
    model_width = ROWS * hidden_ref.shape[2]
    block_tokens = hidden_ref.shape[1]
    lane = lax.broadcasted_iota(jnp.int32, (1, 128), 1)

    def spread(pieces):
        return jnp.concatenate(
            [jnp.where(lane < 64, pieces[2 * k], pieces[2 * k + 1]) for k in range(heads // 2)],
            axis=1,
        )

    @pl.when(q == 0)
    def _first():
        send_ref[...] = jnp.zeros(send_ref.shape, BF)
        total = jnp.zeros((tokens, weight_ref.shape[2]), F32)
        squares = jnp.zeros((tokens, 128), F32)
        for r in range(ROWS):
            rows_r = jnp.concatenate([hidden_ref[r], hidden_ref[ROWS + r]], axis=0)
            total = total + jnp.dot(rows_r, weight_ref[r], preferred_element_type=F32)
            wide = rows_r.astype(F32)
            wide = wide * wide
            squares = squares + wide[:, :128] + wide[:, 128:]
        inverse = lax.rsqrt(jnp.sum(squares, axis=1, keepdims=True) / model_width + EPSILON)
        total = total * inverse
        z_s[...] = total[:, :width]
        x_pad[:, 8:24, :] = total[:, width : 2 * width].reshape(requests, S, width)
        p_pad[:, 8:24, :] = total[:, 2 * width : 2 * width + 2 * state_size].reshape(
            requests, S, 2 * state_size
        )
        x_pad[:, 5:8, :] = inner_cache_ref[...].astype(F32)
        p_pad[:, 5:8, :] = proj_cache_ref[...].astype(F32)
        conv_x = x_pad[:, 5 : 5 + S, :] * inner_kernel_ref[0:1, :]
        conv_p = p_pad[:, 5 : 5 + S, :] * proj_kernel_ref[0:1, :]
        for i in range(1, 4):
            conv_x = conv_x + x_pad[:, 5 + i : 5 + i + S, :] * inner_kernel_ref[i : i + 1, :]
            conv_p = conv_p + p_pad[:, 5 + i : 5 + i + S, :] * proj_kernel_ref[i : i + 1, :]
        x_conv = silu(conv_x).reshape(tokens, width)
        p_conv = silu(conv_p).reshape(tokens, 2 * state_size)
        b_conv = p_conv[:, :state_size]
        c_conv = p_conv[:, state_size:]
        x_s[...] = x_conv
        b_s[...] = b_conv
        c_s[...] = c_conv.astype(BF)
        step_raw = total[:, 2 * width + 2 * state_size :]
        t_now = lax.broadcasted_iota(jnp.int32, (tokens, tokens), 0)
        t_then = lax.broadcasted_iota(jnp.int32, (tokens, tokens), 1)
        causal = (t_now // S == t_then // S) & (t_then <= t_now)
        lower = causal.astype(F32)
        scores = lax.dot_general(
            c_conv.astype(BF), b_conv.astype(BF), (((1,), (1,)), ((), ())),
            preferred_element_type=F32,
        )
        deltas = []
        cums = []
        mixes = []
        for h in range(heads):
            raw = jnp.broadcast_to(step_raw[:, h : h + 1], (tokens, 128))
            delta = softplus(raw + bias_ref[layer, h])
            rate = jnp.exp(jnp.full((1, 128), decay_log_ref[layer, h], F32))
            log_decay = -delta * rate
            dec_s[:, h * 128 : (h + 1) * 128] = jnp.exp(log_decay)
            cum = jnp.dot(
                lower, log_decay, precision=lax.Precision.HIGHEST, preferred_element_type=F32
            )
            gap = jnp.where(causal, cum - cum.T, 0.0)
            mixes.append((jnp.where(causal, jnp.exp(gap), 0.0) * scores).astype(BF))
            deltas.append(delta)
            cums.append(jnp.exp(cum))
        dx = x_conv * spread(deltas)
        dx_s[...] = dx
        ecum_s[...] = spread(cums)
        for k in range(heads // 2):
            dx_k = dx[:, 128 * k : 128 * (k + 1)].astype(BF)
            first = jnp.dot(mixes[2 * k], dx_k, preferred_element_type=F32)
            second = jnp.dot(mixes[2 * k + 1], dx_k, preferred_element_type=F32)
            ydiag_s[:, 128 * k : 128 * (k + 1)] = jnp.where(lane < 64, first, second)

    rows = pl.ds(pl.multiple_of(q * S, S), S)
    start = state_ref[...]
    flat = start.reshape(heads * start.shape[1], state_size)
    y_off = lax.dot_general(
        c_s[rows, :], flat.astype(BF), (((1,), (1,)), ((), ())), preferred_element_type=F32
    )
    skip = spread([jnp.full((1, 128), skip_ref[layer, h], F32) for h in range(heads)])
    y = ydiag_s[rows, :] + ecum_s[rows, :] * y_off + skip * x_s[rows, :]
    g = y * silu(z_s[rows, :])
    yg_s[rows, :] = (g * norm_gain_ref[layer : layer + 1, :]).astype(BF)
    g2_s[rows, :] = (g * g).astype(BF)

    dx_t = dx_s[rows, :].T
    b_q = b_s[rows, :]
    dec_q = dec_s[rows, :]
    head_size = start.shape[1]
    for h in range(heads):
        state = start[h]
        columns = dx_t[h * head_size : (h + 1) * head_size, :]
        for t in range(S):
            state = (
                state * dec_q[t : t + 1, h * 128 : (h + 1) * 128]
                + columns[:, t : t + 1] * b_q[t : t + 1, :]
            )
            steps_ref[t, h] = state.astype(BF)

    @pl.when(slots_ref[q] >= 0)
    def _choose():
        send_ref[slots_ref[q]] = steps_ref[accepted_ref[q] - 1]

    @pl.when(q == requests - 1)
    def _last():
        yg = yg_s[...]
        g2 = g2_s[...]
        ones = jnp.ones((SUM_ROWS, width), BF)
        sums = [
            lax.dot_general(
                ones,
                g2[b * block_tokens : (b + 1) * block_tokens, :],
                (((1,), (1,)), ((), ())),
                preferred_element_type=F32,
            ).astype(BF)
            for b in range(2)
        ]
        for r in range(ROWS):
            part = jnp.dot(yg, out_weight_ref[r], preferred_element_type=F32).astype(BF)
            for b in range(2):
                part_ref[b * ROWS + r, 0:block_tokens, :] = part[
                    b * block_tokens : (b + 1) * block_tokens, :
                ]
                part_ref[b * ROWS + r, block_tokens:, :] = jnp.zeros((SUM_ROWS, width), BF)
                part_ref[b * ROWS + r, block_tokens:, 0:block_tokens] = sums[b]


def mixer(layer, slots, accepted, bias, decay_log, skip, hidden, weight, out_weight,
          inner_kernel, proj_kernel, norm_gain, inner_cache, proj_cache, state, previous):
    layers, requests, heads, head_size, state_size = state.shape
    width = heads * head_size
    tokens = requests * S
    block_tokens = hidden.shape[1]
    smem = pl.BlockSpec(memory_space=pltpu.SMEM)

    def whole(shape):
        return pl.BlockSpec(shape, lambda q: (0,) * len(shape))

    in_specs = [
        smem, smem, smem, smem, smem,
        whole(hidden.shape),
        whole(weight.shape),
        pl.BlockSpec((ROWS, None) + out_weight.shape[2:], lambda q: (0, layer, 0, 0)),
        pl.BlockSpec((None,) + inner_kernel.shape[1:], lambda q: (layer, 0, 0)),
        pl.BlockSpec((None,) + proj_kernel.shape[1:], lambda q: (layer, 0, 0)),
        whole(norm_gain.shape),
        pl.BlockSpec((None,) + inner_cache.shape[1:], lambda q: (layer, 0, 0, 0)),
        pl.BlockSpec((None,) + proj_cache.shape[1:], lambda q: (layer, 0, 0, 0)),
        pl.BlockSpec((None, None, heads, head_size, state_size), lambda q: (layer, q, 0, 0, 0)),
    ]
    operands = [slots, accepted, bias, decay_log, skip, hidden, weight, out_weight,
                inner_kernel, proj_kernel, norm_gain, inner_cache, proj_cache, state]
    aliases = {}
    if previous is not None:
        in_specs.append(pl.BlockSpec(memory_space=pl.ANY))
        aliases = {len(operands): 0}
        operands.append(previous)
    return pl.pallas_call(
        lambda *refs: mixer_body(layer, *refs),
        name="mixer%d" % layer,
        grid=(requests,),
        in_specs=in_specs,
        out_specs=[
            pl.BlockSpec(
                (None, None, S, heads, head_size, state_size),
                lambda q: (layer, q, 0, 0, 0, 0),
            ),
            whole((COLS * SEND_CAP, heads, head_size, state_size)),
            whole((COLS, block_tokens + SUM_ROWS, width)),
        ],
        out_shape=[
            jax.ShapeDtypeStruct((layers, requests, S, heads, head_size, state_size), BF),
            jax.ShapeDtypeStruct((COLS * SEND_CAP, heads, head_size, state_size), BF),
            jax.ShapeDtypeStruct((COLS, block_tokens + SUM_ROWS, width), BF),
        ],
        scratch_shapes=[
            pltpu.VMEM((tokens, width), F32),
            pltpu.VMEM((requests, 24, width), F32),
            pltpu.VMEM((requests, 24, 2 * state_size), F32),
            pltpu.VMEM((tokens, width), F32),
            pltpu.VMEM((tokens, width), F32),
            pltpu.VMEM((tokens, state_size), F32),
            pltpu.VMEM((tokens, state_size), BF),
            pltpu.VMEM((tokens, heads * 128), F32),
            pltpu.VMEM((tokens, width), F32),
            pltpu.VMEM((tokens, width), F32),
            pltpu.VMEM((tokens, width), BF),
            pltpu.VMEM((tokens, width), BF),
        ],
        input_output_aliases=aliases,
        compiler_params=pltpu.CompilerParams(
            dimension_semantics=("arbitrary",), vmem_limit_bytes=48 * 1024 * 1024
        ),
    )(*operands)


def update_body(inner_width, received_ref, hidden_ref, out_ref):
    rows = hidden_ref.shape[0]
    total = received_ref[0].astype(F32)
    for c in range(1, COLS):
        total = total + received_ref[c].astype(F32)
    sums = total[rows:, 0:128].T[:rows, 0:1]
    scale = lax.rsqrt(sums / inner_width + EPSILON)
    fresh = (hidden_ref[...].astype(F32) + total[:rows, :] * scale).astype(BF)
    if len(out_ref.shape) == 3:
        for c in range(COLS):
            out_ref[c] = fresh
    else:
        out_ref[...] = fresh


def update(inner_width, received, hidden, spread):
    shape = ((COLS,) if spread else ()) + hidden.shape
    return pl.pallas_call(
        lambda *refs: update_body(inner_width, *refs),
        name="update_spread" if spread else "update_last",
        out_shape=jax.ShapeDtypeStruct(shape, BF),
    )(received, hidden)


def swap(x):
    return lax.all_to_all(x, "col", 0, 0, tiled=True)


def local(
    hidden_states,
    input_gain,
    inner_weight,
    proj_weight,
    step_weight,
    inner_kernel,
    proj_kernel,
    step_bias,
    decay_log,
    skip_gain,
    norm_gain,
    out_weight,
    inner_cache,
    proj_cache,
    state_cache,
    accepted,
    owners,
    tenant_ranges,
):
    layer_count = inner_weight.shape[0]
    row_width = inner_weight.shape[1]
    inner_local = inner_weight.shape[3]
    heads_local = step_weight.shape[2]
    requests_local = state_cache.shape[1]
    inner_width = inner_local * COLS
    local_ids = jnp.arange(requests_local, dtype=jnp.int32)
    request_ids = lax.axis_index("row") * requests_local + local_ids
    live_mask = jnp.any(
        (request_ids[:, None] >= tenant_ranges[None, :, 0])
        & (request_ids[:, None] < tenant_ranges[None, :, 1]),
        axis=1,
    )
    earlier = (owners[:, None] == owners[None, :]) & (local_ids[None, :] < local_ids[:, None])
    slot_ranks = jnp.sum(earlier.astype(jnp.int32), axis=1)
    slots = jnp.where(live_mask, owners * SEND_CAP + slot_ranks, -1)

    there = []
    for r in range(ROWS):
        for c in range(COLS):
            there.append((r * COLS + c, (c // 2) * COLS + (c % 2) * ROWS + r))
    back = [(b, a) for a, b in there]

    def packed(layer):
        joined = jnp.concatenate(
            [
                inner_weight[layer].reshape(row_width, 2 * inner_local),
                proj_weight[layer],
                jnp.pad(step_weight[layer], ((0, 0), (0, 128 - heads_local))),
            ],
            axis=1,
        )
        return (joined.astype(F32) * input_gain[layer][:, None]).astype(BF)

    weights = [lax.all_gather(packed(0), "row", axis=0)]
    out_all = lax.all_gather(out_weight, "row", axis=0)
    weights.append(lax.all_gather(packed(1), "row", axis=0))

    block = lax.ppermute(hidden_states, ("row", "col"), there)
    spread = jnp.broadcast_to(block[None], (COLS,) + block.shape)
    steps = None
    owned = []
    for layer in range(layer_count):
        everything = swap(spread)
        steps, send, part = mixer(
            layer, slots, accepted, step_bias, decay_log, skip_gain, everything,
            weights[layer], out_all, inner_kernel, proj_kernel, norm_gain,
            inner_cache, proj_cache, state_cache, steps,
        )
        received = swap(part)
        last = layer == layer_count - 1
        fresh = update(inner_width, received, block, not last)
        if not last:
            spread = fresh
            block = fresh[0]
        owned.append(swap(send.reshape((COLS, SEND_CAP) + send.shape[1:])))
    hidden = lax.ppermute(fresh, ("row", "col"), back)
    stacked = jnp.stack(owned, axis=0)
    stacked = jnp.transpose(stacked, (2, 0, 1, 3, 4, 5))
    owned_block = stacked.reshape(
        (1, 1, SEND_CAP, layer_count, COLS * heads_local) + stacked.shape[4:]
    )
    return (hidden, steps, owned_block)


def solution(mesh):
    placed = (
        P("col", "row"),
        P(None, "row"),
        P(None, "row", None, "col"),
        P(None, "row", None),
        P(None, "row", "col"),
        P(None, None, "col"),
        P(),
        P(None, "col"),
        P(None, "col"),
        P(None, "col"),
        P(None, "col"),
        P(None, "col", "row"),
        P(None, "row", None, "col"),
        P(None, "row", None, None),
        P(None, "row", "col", None, None),
        P("row"),
        P("row"),
        P(),
    )
    return jax.shard_map(
        local,
        mesh=mesh,
        in_specs=placed,
        out_specs=(
            P("col", "row"),
            P(None, "row", None, "col", None, None),
            P("row", "col", None, None, None, None, None),
        ),
        check_vma=False,
    )
```

time: 792 us -> 225 us (0.28)
  waiting for transfers between devices: 265 us -> 67.6 us
  blocking collectives: 217 us -> 63.3 us
  matrix products: 105 us -> 0 us
  other arithmetic: 90.8 us -> 4.08 us
  local copies, waits for them, and re-layouts: 86.9 us -> 13.4 us
  Pallas kernels: 0 us -> 29.7 us
  starting transfers between devices: 7.69 us -> 28.4 us
    reduce_scatter x6 -> x0, waiting for transfers between devices: 259 us -> none  [the longest x2 134 us: local(): lax.psum_scatter(partial_out.astype(jnp.bfloat16), 'col', scatter_dimensi...]
    psum x2 -> x0, blocking collectives: 112 us -> none  [local(): gate_square = lax.psum(jnp.sum(gated_raw * gated_raw, axis=1), 'col')]
    dot_general x40 -> x0, matrix products: 101 us -> none  [the longest x32 80.9 us: advance(): jnp.einsum('rhpn,rn->rhp', updated, c_now, precision=lax.Precision.HIGHEST)]
    all_gather x4 -> x0, blocking collectives: 79.8 us -> none  [the longest x2 46.9 us: local(): all_tokens = lax.all_gather(hidden, 'col', axis=0, tiled=True)]
    all_to_all x0 -> x3, blocking collectives: none -> 63.3 us  [swap(): return lax.all_to_all(x, 'col', 0, 0, tiled=True)]
    dynamic_update_slice x64 -> x0, other arithmetic: 62.7 us -> none  [ssm_scan(): last_state, (outputs, states) = lax.scan(advance, start_state, time_major)]
    all_to_all x1 -> x3, waiting for transfers between devices: 0.01 us -> 30.8 us  [swap(): return lax.all_to_all(x, 'col', 0, 0, tiled=True)]
    pallas_call x0 -> x4, Pallas kernels: none -> 29.7 us  [the longest x2 25.7 us: mixer(): pl.pallas_call(lambda *refs: mixer_body(layer, *refs), name='mixer%d' % l...]
  transfers between devices with their start and end apart: 9 -> 8, of which waited for: 7 -> 6; matrix products, arithmetic and copies ran while one was open for 8% -> 4% of each run, Pallas kernels for 0% -> 8%
where the time goes in v1:
time: 225 us; the launch traced here: 220 us
  waiting for transfers between devices  67.6 us (30%)
  blocking collectives  63.3 us (28%)
  Pallas kernels  29.7 us (13%)
  starting transfers between devices  28.4 us (13%)
  between operations  14 us (6%)
  local copies, waits for them, and re-layouts  13.4 us (6%)
  other arithmetic  4.08 us (2%)
    all_to_all x3, blocking collectives, swap(): return lax.all_to_all(x, 'col', 0, 0, tiled=True)  63.3 us
    all_to_all x3, waiting for transfers between devices, swap(): return lax.all_to_all(x, 'col', 0, 0, tiled=True)  30.8 us
    all_gather x1, waiting for transfers between devices, local(): weights = [lax.all_gather(packed(0), 'row', axis=0)]  26.9 us
    pallas_call x2, Pallas kernels, mixer(): pl.pallas_call(lambda *refs: mixer_body(layer, *refs), name='mixer%d' % l...  25.7 us
    all_to_all x3, starting transfers between devices, swap(): return lax.all_to_all(x, 'col', 0, 0, tiled=True)  22.1 us
    ppermute x1, waiting for transfers between devices, local(): block = lax.ppermute(hidden_states, ('row', 'col'), there)  5.15 us
  transfers between devices with their start and end apart: 8, of which 6 were waited for; matrix products, arithmetic and copies ran while one was open for 4% of the time, Pallas kernels for 8%

profile of v1, /device:TPU:32, one launch (start us, length us, event | category | flops | bytes accessed | tf_op | source)
XLA Modules:
  0.0 220.5 jit_solution(1582789765024279520)
XLA Ops:
  7.2 0.0 all-gather.9.cloned.1.call-start
  7.2 0.7 all-gather.9.cloned.1.call-update
  7.9 0.0 all-gather.5.cloned.1.call-start
  8.0 0.7 fusion.3
  8.7 0.1 copy.43
  8.8 0.0 copy-start.14
  8.8 0.0 copy-start.5
  8.9 0.0 copy-start.6
  8.9 0.0 copy-start.9
  8.9 1.4 fusion.1
  10.4 0.2 concatenate.28
  10.6 0.8 fusion.4
  11.3 1.0 fusion.2
  12.3 0.9 multiply_convert_fusion.1
  13.2 0.0 all-gather.5.cloned.1.call-update
  13.3 0.0 all-gather.7.cloned.1.call-start
  13.3 0.1 copy.44
  13.5 0.2 concatenate.31
  13.7 0.9 multiply_convert_fusion
  14.6 0.0 all-gather.7.cloned.1.call-update
  14.6 3.0 %collective-permute-start = (bf16[64,256]{1,0:T(8,128)(2,1)S(1)}, bf16[64,256]{1,0:T(8,128)(2,1)S(1)}, u32[]{:S(2)}, u32[]{:S(2)}) collective-permute-start(bf16[64,256]{1,0:T(8,128)(2,1)S(1)} %copy-done.17), channel_id=1, source_target_pairs={{0,0},{1,8},{2,16},{3,24},{4,32},{5,40},{6,48},{7,56},{8,64},{9,72... | collective-permute-start | bytes 98312 | tf_op jit(solution)/shard_map/ppermute | solution.py:352
  17.7 5.1 %collective-permute-done.refs_1_ = bf16[64,256]{1,0:T(8,128)(2,1)S(1)} collective-permute-done((bf16[64,256]{1,0:T(8,128)(2,1)S(1)}, bf16[64,256]{1,0:T(8,128)(2,1)S(1)}, u32[]{:S(2)}, u32[]{:S(2)}) %collective-permute-start) | collective-permute-done | bytes 32800 | tf_op jit(solution)/shard_map/ppermute | solution.py:352
  22.8 0.8 broadcast_in_dim.6
  23.7 10.5 %all-to-all-start = ((bf16[16,64,256]{2,1,0:T(8,128)(2,1)}), bf16[16,64,256]{2,1,0:T(8,128)(2,1)S(1)}, u32[]{:S(2)}, u32[]{:S(2)}) async-start(bf16[16,64,256]{2,1,0:T(8,128)(2,1)} %broadcast_in_dim.6), calls=%async_computation | async-start | bytes 1048576 | tf_op jit(solution)/shard_map/all_to_all | solution.py:291
  34.2 0.2 convert_reduce_fusion
  34.4 0.1 and_reduce_fusion
  34.5 8.1 %all-to-all-done.refs_5_ = bf16[16,64,256]{2,1,0:T(8,128)(2,1)S(1)} async-done(((bf16[16,64,256]{2,1,0:T(8,128)(2,1)}), bf16[16,64,256]{2,1,0:T(8,128)(2,1)S(1)}, u32[]{:S(2)}, u32[]{:S(2)}) %all-to-all-start) | async-done | bytes 524320 | tf_op jit(solution)/shard_map/all_to_all | solution.py:291
  42.6 26.9 %all-gather.5.cloned.1.call-done.refs_6_ = bf16[8,256,896]{2,1,0:T(8,128)(2,1)} async-done(((bf16[1,256,896]{2,1,0:T(8,128)(2,1)}), bf16[8,256,896]{2,1,0:T(8,128)(2,1)}) %all-gather.5.cloned.1.call-update) | async-done | bytes 3670032 | tf_op jit(solution)/shard_map/all_gather | solution.py:348
  69.5 1.6 copy-done
  71.1 12.8 %mixer0.1 = (bf16[2,8,16,4,64,128]{5,4,3,2,1,0:T(8,128)(2,1)}, bf16[32,4,64,128]{3,2,1,0:T(8,128)(2,1)S(1)}, bf16[16,80,256]{2,1,0:T(8,128)(2,1)S(1)}) custom-call(s32[8]{0:T(128)S(1)} %add_select_fusion.refs_0_, s32[8]{0:T(128)S(1)} %copy-done.11, f32[2,4]{1,0:T(2,128)S(1)} %copy-done.8, f32[2,4]{1,0:T(2,128)S(1)} %copy-done.9, f32[2,4]{1,0:T(2,128)S(1)} %copy-done.10, ...), custom_call_target="tpu_custom_call" | custom-call | tf_op jit(solution)/shard_map/mixer0/pallas_call | solution.py:227
  83.9 1.3 copy-done.2
  85.2 19.0 %all_to_all.30.refs_0_ = bf16[16,80,256]{2,1,0:T(8,128)(2,1)} all-to-all(bf16[16,80,256]{2,1,0:T(8,128)(2,1)S(1)} %get-tuple-element.9), channel_id=1, replica_groups=mesh['row'=8,'col'=16] {'col'}, dimensions={0} | all-to-all | bytes 1310720 | tf_op jit(solution)/shard_map/all_to_all | solution.py:291
  104.3 2.1 update_spread.1
  106.4 5.1 %all-to-all-start.2 = ((bf16[16,64,256]{2,1,0:T(8,128)(2,1)}), bf16[16,64,256]{2,1,0:T(8,128)(2,1)S(1)}, u32[]{:S(2)}, u32[]{:S(2)}) async-start(bf16[16,64,256]{2,1,0:T(8,128)(2,1)} %update_spread.1), calls=%async_computation.2 | async-start | bytes 1048576 | tf_op jit(solution)/shard_map/all_to_all | solution.py:291
  111.5 0.0 all-gather.7.cloned.1.call-done.refs_6_
  111.5 8.7 %all-to-all-done.2.refs_5_ = bf16[16,64,256]{2,1,0:T(8,128)(2,1)S(1)} async-done(((bf16[16,64,256]{2,1,0:T(8,128)(2,1)}), bf16[16,64,256]{2,1,0:T(8,128)(2,1)S(1)}, u32[]{:S(2)}, u32[]{:S(2)}) %all-to-all-start.2) | async-done | bytes 524320 | tf_op jit(solution)/shard_map/all_to_all | solution.py:291
  120.3 12.9 %mixer1.1 = (bf16[2,8,16,4,64,128]{5,4,3,2,1,0:T(8,128)(2,1)}, bf16[32,4,64,128]{3,2,1,0:T(8,128)(2,1)S(1)}, bf16[16,80,256]{2,1,0:T(8,128)(2,1)S(1)}) custom-call(s32[8]{0:T(128)S(1)} %add_select_fusion.refs_0_, s32[8]{0:T(128)S(1)} %copy-done.11, f32[2,4]{1,0:T(2,128)S(1)} %copy-done.8, f32[2,4]{1,0:T(2,128)S(1)} %copy-done.9, ...), custom_call_target="tpu_custom_call", output_to_operand_aliasing={{0}: (14, {})} | custom-call | tf_op jit(solution)/shard_map/mixer1/pallas_call | solution.py:227
  133.2 15.7 %all_to_all.31.refs_0_ = bf16[16,80,256]{2,1,0:T(8,128)(2,1)} all-to-all(bf16[16,80,256]{2,1,0:T(8,128)(2,1)S(1)} %get-tuple-element.11), channel_id=1, replica_groups=mesh['row'=8,'col'=16] {'col'}, dimensions={0} | all-to-all | bytes 1310720 | tf_op jit(solution)/shard_map/all_to_all | solution.py:291
  148.9 28.5 %all_to_all.32 = bf16[16,2,4,64,128]{4,3,2,1,0:T(8,128)(2,1)S(1)} all-to-all(bf16[16,2,4,64,128]{4,3,2,1,0:T(8,128)(2,1)S(1)} %bitcast.24), channel_id=1, replica_groups=mesh['row'=8,'col'=16] {'col'}, dimensions={0} | all-to-all | bytes 4194304 | tf_op jit(solution)/shard_map/all_to_all | solution.py:291
  177.5 6.4 %all-to-all-start.5 = ((bf16[16,2,4,64,128]{4,3,2,1,0:T(8,128)(2,1)}), bf16[16,2,4,64,128]{4,3,2,1,0:T(8,128)(2,1)}, u32[]{:S(2)}, u32[]{:S(2)}) async-start(bf16[16,2,4,64,128]{4,3,2,1,0:T(8,128)(2,1)} %bitcast.25), calls=%async_computation.5 | async-start | bytes 4194304 | tf_op jit(solution)/shard_map/all_to_all | solution.py:291
  183.9 1.4 slice_bitcast_fusion.refs_1_
  185.3 1.9 update_last.1
  187.1 3.2 %collective-permute-start.1 = (bf16[64,256]{1,0:T(8,128)(2,1)}, bf16[64,256]{1,0:T(8,128)(2,1)S(1)}, u32[]{:S(2)}, u32[]{:S(2)}) collective-permute-start(bf16[64,256]{1,0:T(8,128)(2,1)} %update_last.1), channel_id=1, source_target_pairs={{0,0},{8,1},{16,2},{24,3},{32,4},{40,5},{48,6},{56,7},{64,8},{72,9... | collective-permute-start | bytes 98312 | tf_op jit(solution)/shard_map/ppermute | solution.py:370
  190.3 4.0 %collective-permute-done.1 = bf16[64,256]{1,0:T(8,128)(2,1)S(1)} collective-permute-done((bf16[64,256]{1,0:T(8,128)(2,1)}, bf16[64,256]{1,0:T(8,128)(2,1)S(1)}, u32[]{:S(2)}, u32[]{:S(2)}) %collective-permute-start.1) | collective-permute-done | bytes 32800 | tf_op jit(solution)/shard_map/ppermute | solution.py:370
  194.3 14.1 %all-to-all-done.5 = bf16[16,2,4,64,128]{4,3,2,1,0:T(8,128)(2,1)} async-done(((bf16[16,2,4,64,128]{4,3,2,1,0:T(8,128)(2,1)}), bf16[16,2,4,64,128]{4,3,2,1,0:T(8,128)(2,1)}, u32[]{:S(2)}, u32[]{:S(2)}) %all-to-all-start.5) | async-done | bytes 2097184 | tf_op jit(solution)/shard_map/all_to_all | solution.py:291
  208.4 2.0 maximum_bitcast_fusion
  210.4 3.0 %copy.42 = bf16[2,2,16,4,64,128]{5,4,3,2,1,0:T(8,128)(2,1)} copy(bf16[2,2,16,4,64,128]{5,4,3,0,2,1:T(8,128)(2,1)S(1)} %maximum_bitcast_fusion) | data formatting | bytes 8388608 | tf_op jit(solution)/shard_map/transpose | solution.py:372
  213.3 0.6 copy.47
  (38 shorter events, 0.1 us)
Async XLA Ops:
  7.2 7.4 %copy-start.17 = (bf16[64,256]{1,0:T(8,128)(2,1)S(1)}, bf16[64,256]{1,0:T(8,128)(2,1)}, u32[]{:S(2)}) copy-start(bf16[64,256]{1,0:T(8,128)(2,1)} %param.18) | copy-start | bytes 98308
  7.2 10.5 %copy-start.15 = (s32[4,2]{0,1:T(2,128)S(1)}, s32[4,2]{0,1:T(2,128)}, u32[]{:S(2)}) copy-start(s32[4,2]{0,1:T(2,128)} %param.35) | copy-start | bytes 100
  7.2 35.4 %all-gather.9.cloned.1.call-start = ((), (), s32[]{:S(2)}) async-start(), calls=%async_computation.8 | async-start | bytes 2359296 | tf_op jit(solution)/shard_map/all_gather | solution.py:349
  7.9 61.6 %all-gather.5.cloned.1.call-start = ((), (), s32[]{:S(2)}) async-start(), calls=%async_computation.6 | async-start | bytes 4128768 | tf_op jit(solution)/shard_map/all_gather | solution.py:348
  8.8 25.3 %copy-start.13 = (bf16[2,8,3,256]{3,1,2,0:T(8,128)(2,1)S(1)}, bf16[2,8,3,256]{3,1,2,0:T(8,128)(2,1)}, u32[]{:S(2)}) copy-start(bf16[2,8,3,256]{3,1,2,0:T(8,128)(2,1)} %param.30) | copy-start | bytes 73732
  8.8 25.4 %copy-start.14 = (bf16[2,8,3,256]{3,1,2,0:T(8,128)(2,1)S(1)}, bf16[2,8,3,256]{3,1,2,0:T(8,128)(2,1)}, u32[]{:S(2)}) copy-start(bf16[2,8,3,256]{3,1,2,0:T(8,128)(2,1)} %param.31) | copy-start | bytes 73732
  8.8 25.4 %copy-start.16 = (s32[8]{0:T(128)S(1)}, s32[8]{0:T(128)}, u32[]{:S(2)}) copy-start(s32[8]{0:T(128)} %param.34) | copy-start | bytes 100
  8.8 60.6 %copy-start.5 = (f32[2,4,256]{2,1,0:T(4,128)S(1)}, f32[2,4,256]{2,1,0:T(4,128)}, u32[]{:S(2)}) copy-start(f32[2,4,256]{2,1,0:T(4,128)} %refs_8_.3) | copy-start | bytes 24580
  8.9 60.6 %copy-start.6 = (f32[2,4,256]{2,1,0:T(4,128)S(1)}, f32[2,4,256]{2,1,0:T(4,128)}, u32[]{:S(2)}) copy-start(f32[2,4,256]{2,1,0:T(4,128)} %refs_9_.3) | copy-start | bytes 24580
  8.9 60.6 %copy-start.7 = (f32[2,256]{1,0:T(2,128)S(1)}, f32[2,256]{1,0:T(2,128)}, u32[]{:S(2)}) copy-start(f32[2,256]{1,0:T(2,128)} %refs_10_.3) | copy-start | bytes 6148
  8.9 60.6 %copy-start.8 = (f32[2,4]{1,0:T(2,128)S(1)}, f32[2,4]{1,0:T(2,128)}, u32[]{:S(2)}) copy-start(f32[2,4]{1,0:T(2,128)} %refs_2_.3) | copy-start | bytes 100
  8.9 60.6 %copy-start.9 = (f32[2,4]{1,0:T(2,128)S(1)}, f32[2,4]{1,0:T(2,128)}, u32[]{:S(2)}) copy-start(f32[2,4]{1,0:T(2,128)} %refs_3_.3) | copy-start | bytes 100
  8.9 60.6 %copy-start.10 = (f32[2,4]{1,0:T(2,128)S(1)}, f32[2,4]{1,0:T(2,128)}, u32[]{:S(2)}) copy-start(f32[2,4]{1,0:T(2,128)} %refs_4_.3) | copy-start | bytes 100
  8.9 60.6 %copy-start.11 = (s32[8]{0:T(128)S(1)}, s32[8]{0:T(128)}, u32[]{:S(2)}) copy-start(s32[8]{0:T(128)} %refs_1_.3) | copy-start | bytes 100
  13.3 98.3 %all-gather.7.cloned.1.call-start = ((), (), s32[]{:S(2)}) async-start(), calls=%async_computation.7 | async-start | bytes 4128768 | tf_op jit(solution)/shard_map/all_gather | solution.py:350
  14.6 8.2 %collective-permute-start = (bf16[64,256]{1,0:T(8,128)(2,1)S(1)}, bf16[64,256]{1,0:T(8,128)(2,1)S(1)}, u32[]{:S(2)}, u32[]{:S(2)}) collective-permute-start(bf16[64,256]{1,0:T(8,128)(2,1)S(1)} %copy-done.17), channel_id=1, source_target_pairs={{0,0},{1,8},{2,16},{3,24},{4,32},{5,40},{6,48},{7,56},{8,64},{9,72... | collective-permute-start | bytes 98312 | tf_op jit(solution)/shard_map/ppermute | solution.py:352
  22.8 61.1 %copy-start.12 = (bf16[64,256]{1,0:T(8,128)(2,1)}, bf16[64,256]{1,0:T(8,128)(2,1)S(1)}, u32[]{:S(2)}) copy-start(bf16[64,256]{1,0:T(8,128)(2,1)S(1)} %collective-permute-done.refs_1_) | copy-start | bytes 98308
  23.7 18.9 %all-to-all-start = ((bf16[16,64,256]{2,1,0:T(8,128)(2,1)}), bf16[16,64,256]{2,1,0:T(8,128)(2,1)S(1)}, u32[]{:S(2)}, u32[]{:S(2)}) async-start(bf16[16,64,256]{2,1,0:T(8,128)(2,1)} %broadcast_in_dim.6), calls=%async_computation | async-start | bytes 1048576 | tf_op jit(solution)/shard_map/all_to_all | solution.py:291
  69.5 1.6 copy-start
  83.9 1.3 copy-start.2
  85.2 35.0 %copy-start.1 = (bf16[16,256,256]{2,1,0:T(8,128)(2,1)S(1)}, bf16[16,256,256]{2,1,0:T(8,128)(2,1)}, u32[]{:S(2)}) copy-start(bf16[16,256,256]{2,1,0:T(8,128)(2,1)} %all-gather.9.cloned.1.call-done) | copy-start | bytes 6291460
  106.4 13.9 %all-to-all-start.2 = ((bf16[16,64,256]{2,1,0:T(8,128)(2,1)}), bf16[16,64,256]{2,1,0:T(8,128)(2,1)S(1)}, u32[]{:S(2)}, u32[]{:S(2)}) async-start(bf16[16,64,256]{2,1,0:T(8,128)(2,1)} %update_spread.1), calls=%async_computation.2 | async-start | bytes 1048576 | tf_op jit(solution)/shard_map/all_to_all | solution.py:291
  120.3 28.7 %copy-start.3 = (bf16[32,4,64,128]{3,2,1,0:T(8,128)(2,1)S(1)}, bf16[32,4,64,128]{3,2,1,0:T(8,128)(2,1)}, u32[]{:S(2)}) copy-start(bf16[32,4,64,128]{3,2,1,0:T(8,128)(2,1)} %copy-done.2) | copy-start | bytes 6291460
  133.2 44.3 %copy-start.4 = (bf16[32,4,64,128]{3,2,1,0:T(8,128)(2,1)}, bf16[32,4,64,128]{3,2,1,0:T(8,128)(2,1)S(1)}, u32[]{:S(2)}) copy-start(bf16[32,4,64,128]{3,2,1,0:T(8,128)(2,1)S(1)} %get-tuple-element.14) | copy-start | bytes 6291460
  177.5 30.9 %all-to-all-start.5 = ((bf16[16,2,4,64,128]{4,3,2,1,0:T(8,128)(2,1)}), bf16[16,2,4,64,128]{4,3,2,1,0:T(8,128)(2,1)}, u32[]{:S(2)}, u32[]{:S(2)}) async-start(bf16[16,2,4,64,128]{4,3,2,1,0:T(8,128)(2,1)} %bitcast.25), calls=%async_computation.5 | async-start | bytes 4194304 | tf_op jit(solution)/shard_map/all_to_all | solution.py:291
  187.1 7.2 %collective-permute-start.1 = (bf16[64,256]{1,0:T(8,128)(2,1)}, bf16[64,256]{1,0:T(8,128)(2,1)S(1)}, u32[]{:S(2)}, u32[]{:S(2)}) collective-permute-start(bf16[64,256]{1,0:T(8,128)(2,1)} %update_last.1), channel_id=1, source_target_pairs={{0,0},{8,1},{16,2},{24,3},{32,4},{40,5},{48,6},{56,7},{64,8},{72,9... | collective-permute-start | bytes 98312 | tf_op jit(solution)/shard_map/ppermute | solution.py:370
Sparse Core Ops, SparseCore 0:
  9.7 27.1 all-gather.8
  39.2 30.2 all-gather.4
  71.2 29.8 all-gather.6

commit v2 on v0

v2 whole, which is shorter than its diff:
```python
import jax
import jax.numpy as jnp
from jax import lax
from jax.experimental import pallas as pl
from jax.experimental.pallas import tpu as pltpu
from jax.sharding import PartitionSpec as P

S = 16
SEND_CAP = 2
EPSILON = 1e-05
ROWS = 8
COLS = 16
BF = jnp.bfloat16
F32 = jnp.float32
SUM_ROWS = 16


def silu(v):
    return v / (1.0 + jnp.exp(-v))


def softplus(v):
    return jnp.maximum(v, 0.0) + jnp.log1p(jnp.exp(-jnp.abs(v)))


def route(q, ints_ref, requests):
    owners, ranges = 1 + requests, 1 + 2 * requests
    request = ints_ref[0] + q
    live = (request >= ints_ref[ranges]) & (request < ints_ref[ranges + 1])
    for k in range(ranges + 2, ints_ref.shape[0], 2):
        live = live | ((request >= ints_ref[k]) & (request < ints_ref[k + 1]))
    owner = ints_ref[owners + q]
    rank = jnp.int32(0)
    for other in range(q):
        rank = rank + jnp.where(ints_ref[owners + other] == owner, 1, 0)
    return live, owner, jnp.minimum(rank, SEND_CAP - 1)


def put_start(out_ref, owner, rank, start):
    heads, head_size, _ = start.shape
    span = heads // 2 * head_size
    first = pl.multiple_of(rank * span, span)
    for k in range(heads // 2):
        pair = jnp.concatenate([start[2 * k], start[2 * k + 1]], axis=1)
        out_ref[owner, pl.ds(first + k * head_size, head_size), :] = pair.astype(BF)


def front_body(
    layer,
    head_rows,
    ints_ref,
    floats_ref,
    hidden_ref,
    weight_ref,
    inner_kernel_ref,
    proj_kernel_ref,
    norm_gain_ref,
    inner_cache_ref,
    proj_cache_ref,
    state_ref,
    part_ref,
    dx_ref,
    b_ref,
    dec_ref,
    x_pad,
    p_pad,
):
    requests, heads, head_size, state_size = state_ref.shape
    tokens = requests * S
    width = heads * head_size
    model_width = ROWS * hidden_ref.shape[2]
    block_tokens = hidden_ref.shape[1]
    in_cols = 2 * width + 2 * state_size + 128
    lane = lax.broadcasted_iota(jnp.int32, (1, 128), 1)

    def spread(pieces):
        return jnp.concatenate(
            [jnp.where(lane < 64, pieces[2 * k], pieces[2 * k + 1]) for k in range(heads // 2)],
            axis=1,
        )

    total = jnp.zeros((tokens, in_cols), F32)
    squares = jnp.zeros((tokens, 128), F32)
    for r in range(ROWS):
        rows_r = jnp.concatenate([hidden_ref[r], hidden_ref[ROWS + r]], axis=0)
        total = total + jnp.dot(rows_r, weight_ref[r, :, :in_cols], preferred_element_type=F32)
        wide = rows_r.astype(F32)
        wide = wide * wide
        squares = squares + wide[:, :128] + wide[:, 128:]
    inverse = lax.rsqrt(jnp.sum(squares, axis=1, keepdims=True) / model_width + EPSILON)
    total = total * inverse
    z = total[:, :width]
    x_pad[:, 8:24, :] = total[:, width : 2 * width].reshape(requests, S, width)
    p_pad[:, 8:24, :] = total[:, 2 * width : 2 * width + 2 * state_size].reshape(
        requests, S, 2 * state_size
    )
    x_pad[:, 5:8, :] = inner_cache_ref[...].astype(F32)
    p_pad[:, 5:8, :] = proj_cache_ref[...].astype(F32)
    conv_x = x_pad[:, 5 : 5 + S, :] * inner_kernel_ref[0:1, :]
    conv_p = p_pad[:, 5 : 5 + S, :] * proj_kernel_ref[0:1, :]
    for i in range(1, 4):
        conv_x = conv_x + x_pad[:, 5 + i : 5 + i + S, :] * inner_kernel_ref[i : i + 1, :]
        conv_p = conv_p + p_pad[:, 5 + i : 5 + i + S, :] * proj_kernel_ref[i : i + 1, :]
    x_conv = silu(conv_x).reshape(tokens, width)
    p_conv = silu(conv_p).reshape(tokens, 2 * state_size)
    b_conv = p_conv[:, :state_size]
    c_conv = p_conv[:, state_size:].astype(BF)
    b_ref[...] = b_conv
    step_raw = total[:, 2 * width + 2 * state_size :]
    t_now = lax.broadcasted_iota(jnp.int32, (tokens, tokens), 0)
    t_then = lax.broadcasted_iota(jnp.int32, (tokens, tokens), 1)
    causal = (t_now // S == t_then // S) & (t_then <= t_now)
    lower = causal.astype(F32)
    scores = lax.dot_general(
        c_conv, b_conv.astype(BF), (((1,), (1,)), ((), ())), preferred_element_type=F32
    )
    deltas = []
    sums_log = []
    mixes = []
    for h in range(heads):
        raw = jnp.broadcast_to(step_raw[:, h : h + 1], (tokens, 128))
        delta = softplus(raw + floats_ref[layer, h])
        rate = jnp.exp(jnp.full((1, 128), floats_ref[layer, heads + h], F32))
        log_decay = -delta * rate
        dec_ref[:, h * 128 : (h + 1) * 128] = jnp.exp(log_decay)
        cum = jnp.dot(
            lower, log_decay, precision=lax.Precision.HIGHEST, preferred_element_type=F32
        )
        gap = jnp.where(causal, cum - cum.T, 0.0)
        mixes.append((jnp.where(causal, jnp.exp(gap), 0.0) * scores).astype(BF))
        deltas.append(delta)
        sums_log.append(cum)
    dx = x_conv * spread(deltas)
    cum_all = spread(sums_log)
    grown = jnp.exp(cum_all)
    dx_ref[...] = dx
    y_diag = []
    for k in range(heads // 2):
        dx_k = dx[:, 128 * k : 128 * (k + 1)].astype(BF)
        first = jnp.dot(mixes[2 * k], dx_k, preferred_element_type=F32)
        second = jnp.dot(mixes[2 * k + 1], dx_k, preferred_element_type=F32)
        y_diag.append(jnp.where(lane < 64, first, second))
    y_off = []
    for q in range(requests):
        flat = state_ref[q].reshape(width, state_size).astype(BF)
        y_off.append(
            lax.dot_general(
                c_conv[q * S : (q + 1) * S, :], flat, (((1,), (1,)), ((), ())),
                preferred_element_type=F32,
            )
        )
    skip = spread([jnp.full((1, 128), floats_ref[layer, 2 * heads + h], F32) for h in range(heads)])
    y = (
        jnp.concatenate(y_diag, axis=1)
        + grown * jnp.concatenate(y_off, axis=0)
        + skip * x_conv
    )
    g = y * silu(z)
    yg = (g * norm_gain_ref[layer : layer + 1, :]).astype(BF)
    g2 = (g * g).astype(BF)
    ones = jnp.ones((SUM_ROWS, width), BF)
    part_row = head_rows + SEND_CAP * 2 * S
    sum_row = part_row + block_tokens
    part_ref[:, :part_row, :] = jnp.zeros((COLS, part_row, width), BF)
    for b in range(2):
        sums = lax.dot_general(
            ones,
            g2[b * block_tokens : (b + 1) * block_tokens, :],
            (((1,), (1,)), ((), ())),
            preferred_element_type=F32,
        ).astype(BF)
        for r in range(ROWS):
            part_ref[b * ROWS + r, sum_row:, :] = jnp.zeros((SUM_ROWS, width), BF)
            part_ref[b * ROWS + r, sum_row:, 0:block_tokens] = sums
    for r in range(ROWS):
        part = jnp.dot(yg, weight_ref[r, :, in_cols:], preferred_element_type=F32).astype(BF)
        for b in range(2):
            part_ref[b * ROWS + r, part_row:sum_row, :] = part[
                b * block_tokens : (b + 1) * block_tokens, :
            ]
    step = lax.broadcasted_iota(jnp.int32, (S, 1), 0)
    for q in range(requests):
        live, owner, rank = route(q, ints_ref, requests)
        taken = ints_ref[1 + q] - 1
        rows = slice(q * S, (q + 1) * S)
        cum_q = cum_all[rows, :]
        cum_end = jnp.sum(jnp.where(step == taken, cum_q, 0.0), axis=0, keepdims=True)
        inside = step <= taken
        weight = jnp.where(inside, jnp.exp(jnp.where(inside, cum_end - cum_q, 0.0)), 0.0)
        scale = jnp.exp(cum_end)
        high = scale.astype(BF).astype(F32)
        low = scale - high
        extra = jnp.where(
            step == 0,
            high[:, :128],
            jnp.where(
                step == 1, high[:, 128:], jnp.where(step == 2, low[:, :128], low[:, 128:])
            ),
        )
        first = pl.multiple_of(head_rows + rank * 2 * S, 2 * S)

        @pl.when(live)
        def _send():
            part_ref[owner, pl.ds(first, S), :] = (dx[rows, :] * weight).astype(BF)
            part_ref[owner, pl.ds(first + S, S), :] = jnp.concatenate(
                [b_conv[rows, :], extra], axis=1
            ).astype(BF)
            if head_rows:
                put_start(part_ref, owner, rank, state_ref[q])


def front(layer, head_rows, hidden_at, ints, floats, hidden, weight, inner_kernel, proj_kernel,
          norm_gain, inner_cache, proj_cache, state):
    layers, requests, heads, head_size, state_size = state.shape
    width = heads * head_size
    tokens = requests * S
    smem = pl.BlockSpec(memory_space=pltpu.SMEM)

    def whole(shape):
        return pl.BlockSpec(shape, lambda i: (0,) * len(shape))

    def layer_of(shape):
        return pl.BlockSpec((None,) + shape[1:], lambda i: (layer,) + (0,) * (len(shape) - 1))

    block_tokens = tokens // 2
    out_shapes = [
        ((COLS, head_rows + SEND_CAP * 2 * S + block_tokens + SUM_ROWS, width), BF),
        ((tokens, width), F32),
        ((tokens, state_size), F32),
        ((tokens, heads * 128), F32),
    ]
    return pl.pallas_call(
        lambda *refs: front_body(layer, head_rows, *refs),
        name="front%d" % layer,
        grid=(1,),
        in_specs=[
            smem, smem,
            pl.BlockSpec((COLS, block_tokens, hidden.shape[2]), lambda i: (0, hidden_at, 0)),
            whole(weight.shape),
            layer_of(inner_kernel.shape),
            layer_of(proj_kernel.shape),
            whole(norm_gain.shape),
            layer_of(inner_cache.shape),
            layer_of(proj_cache.shape),
            layer_of(state.shape),
        ],
        out_specs=[whole(shape) for shape, _ in out_shapes],
        out_shape=[jax.ShapeDtypeStruct(shape, kind) for shape, kind in out_shapes],
        scratch_shapes=[
            pltpu.VMEM((requests, 24, width), F32),
            pltpu.VMEM((requests, 24, 2 * state_size), F32),
        ],
        compiler_params=pltpu.CompilerParams(
            dimension_semantics=("arbitrary",), vmem_limit_bytes=40 * 1024 * 1024
        ),
    )(ints, floats, hidden, weight, inner_kernel, proj_kernel, norm_gain,
      inner_cache, proj_cache, state)


def states_body(dx_ref, b_ref, dec_ref, state_ref, *rest):
    steps_ref = rest[-1]
    heads, head_size, state_size = state_ref.shape
    dx_t = dx_ref[...].T
    for h in range(heads):
        state = state_ref[h]
        columns = dx_t[h * head_size : (h + 1) * head_size, :]
        for t in range(S):
            state = (
                state * dec_ref[t : t + 1, h * 128 : (h + 1) * 128]
                + columns[:, t : t + 1] * b_ref[t : t + 1, :]
            )
            steps_ref[t, h] = state.astype(BF)


def states(layer, dx, b, dec, state, previous):
    layers, requests, heads, head_size, state_size = state.shape
    width = heads * head_size
    in_specs = [
        pl.BlockSpec((S, width), lambda q: (q, 0)),
        pl.BlockSpec((S, state_size), lambda q: (q, 0)),
        pl.BlockSpec((S, heads * 128), lambda q: (q, 0)),
        pl.BlockSpec((None, None, heads, head_size, state_size), lambda q: (layer, q, 0, 0, 0)),
    ]
    operands = [dx, b, dec, state]
    aliases = {}
    if previous is not None:
        in_specs.append(pl.BlockSpec(memory_space=pl.ANY))
        aliases = {len(operands): 0}
        operands.append(previous)
    return pl.pallas_call(
        states_body,
        name="states%d" % layer,
        grid=(requests,),
        in_specs=in_specs,
        out_specs=pl.BlockSpec(
            (None, None, S, heads, head_size, state_size), lambda q: (layer, q, 0, 0, 0, 0)
        ),
        out_shape=jax.ShapeDtypeStruct(
            (layers, requests, S, heads, head_size, state_size), BF
        ),
        input_output_aliases=aliases,
        compiler_params=pltpu.CompilerParams(
            dimension_semantics=("arbitrary",), vmem_limit_bytes=24 * 1024 * 1024
        ),
    )(*operands)


def starts_body(ints_ref, state_ref, hidden_ref, send_ref):
    rows = send_ref.shape[1] - hidden_ref.shape[0]
    send_ref[:, :rows, :] = jnp.zeros((COLS, rows, send_ref.shape[2]), BF)
    hidden = hidden_ref[...]
    for c in range(COLS):
        send_ref[c, rows:, :] = hidden
    requests = state_ref.shape[0]
    for q in range(requests):
        live, owner, rank = route(q, ints_ref, requests)

        @pl.when(live)
        def _put():
            put_start(send_ref, owner, rank, state_ref[q])


def starts(layer, head_rows, ints, state, hidden):
    shape = (COLS, head_rows + hidden.shape[0], hidden.shape[1])
    return pl.pallas_call(
        starts_body,
        name="starts",
        grid=(1,),
        in_specs=[
            pl.BlockSpec(memory_space=pltpu.SMEM),
            pl.BlockSpec((None,) + state.shape[1:], lambda i: (layer, 0, 0, 0, 0)),
            pl.BlockSpec(hidden.shape, lambda i: (0, 0)),
        ],
        out_specs=pl.BlockSpec(shape, lambda i: (0, 0, 0)),
        out_shape=jax.ShapeDtypeStruct(shape, BF),
        compiler_params=pltpu.CompilerParams(
            dimension_semantics=("arbitrary",), vmem_limit_bytes=24 * 1024 * 1024
        ),
    )(ints, state, hidden)


def owned_body(starts_ref, factors_ref, *rest):
    out_ref = rest[-1]
    group = starts_ref.shape[0]
    slots, group_heads, head_size, state_size = out_ref.shape
    heads = group_heads // group
    span = heads // 2 * head_size
    for g in range(group):
        for slot in range(slots):
            row = slot * 2 * S
            dx = factors_ref[g, row : row + S, :]
            other = factors_ref[g, row + S : row + 2 * S, :]
            added = lax.dot_general(
                dx, other[:, :state_size], (((0,), (0,)), ((), ())), preferred_element_type=F32
            )
            tail = other[:, state_size:].astype(F32)
            for h in range(heads):
                k, half = h // 2, h % 2
                lane = half * 64
                scale = tail[k : k + 1, lane : lane + 1] + tail[k + 2 : k + 3, lane : lane + 1]
                at = slot * span + k * head_size
                begun = starts_ref[
                    g, at : at + head_size, half * state_size : (half + 1) * state_size
                ]
                out_ref[slot, g * heads + h] = (
                    begun.astype(F32) * scale + added[h * head_size : (h + 1) * head_size, :]
                ).astype(BF)


def owned_states(layer, state, head_rows, begun, factors, factors_at, previous):
    layers, _, heads, head_size, state_size = state.shape
    group = 4
    in_specs = [
        pl.BlockSpec((group, head_rows, begun.shape[2]), lambda i: (i, 0, 0)),
        pl.BlockSpec((group, SEND_CAP * 2 * S, begun.shape[2]), lambda i: (i, factors_at, 0)),
    ]
    operands = [begun, factors]
    aliases = {}
    if previous is not None:
        in_specs.append(pl.BlockSpec(memory_space=pl.ANY))
        aliases = {len(operands): 0}
        operands.append(previous)
    return pl.pallas_call(
        owned_body,
        name="owned%d" % layer,
        grid=(COLS // group,),
        in_specs=in_specs,
        out_specs=pl.BlockSpec(
            (SEND_CAP, None, group * heads, head_size, state_size),
            lambda i: (0, layer, i, 0, 0),
        ),
        out_shape=jax.ShapeDtypeStruct(
            (SEND_CAP, layers, COLS * heads, head_size, state_size), BF
        ),
        input_output_aliases=aliases,
        compiler_params=pltpu.CompilerParams(
            dimension_semantics=("arbitrary",), vmem_limit_bytes=16 * 1024 * 1024
        ),
    )(*operands)


def update_body(inner_width, part_ref, sums_ref, hidden_ref, out_ref):
    rows = hidden_ref.shape[0]
    total = part_ref[0].astype(F32)
    sums = sums_ref[0, :, 0:128].astype(F32)
    for c in range(1, COLS):
        total = total + part_ref[c].astype(F32)
        sums = sums + sums_ref[c, :, 0:128].astype(F32)
    scale = lax.rsqrt(sums.T[:rows, 0:1] / inner_width + EPSILON)
    fresh = (hidden_ref[...].astype(F32) + total * scale).astype(BF)
    if len(out_ref.shape) == 3:
        for c in range(COLS):
            out_ref[c] = fresh
    else:
        out_ref[...] = fresh


def update(inner_width, head_rows, received, hidden, spread):
    rows, lanes = hidden.shape
    shape = ((COLS,) if spread else ()) + hidden.shape
    part_at = (head_rows + SEND_CAP * 2 * S) // rows
    sums_at = (head_rows + SEND_CAP * 2 * S + rows) // SUM_ROWS
    return pl.pallas_call(
        lambda *refs: update_body(inner_width, *refs),
        name="update_spread" if spread else "update_last",
        grid=(1,),
        in_specs=[
            pl.BlockSpec((COLS, rows, lanes), lambda i: (0, part_at, 0)),
            pl.BlockSpec((COLS, SUM_ROWS, lanes), lambda i: (0, sums_at, 0)),
            pl.BlockSpec(hidden.shape, lambda i: (0, 0)),
        ],
        out_specs=pl.BlockSpec(shape, lambda i: (0,) * len(shape)),
        out_shape=jax.ShapeDtypeStruct(shape, BF),
    )(received, received, hidden)


def swap(x):
    return lax.all_to_all(x, "col", 0, 0, tiled=True)


def local(
    hidden_states,
    input_gain,
    inner_weight,
    proj_weight,
    step_weight,
    inner_kernel,
    proj_kernel,
    step_bias,
    decay_log,
    skip_gain,
    norm_gain,
    out_weight,
    inner_cache,
    proj_cache,
    state_cache,
    accepted,
    owners,
    tenant_ranges,
):
    layer_count = inner_weight.shape[0]
    row_width = inner_weight.shape[1]
    inner_local = inner_weight.shape[3]
    heads_local = step_weight.shape[2]
    requests_local = state_cache.shape[1]
    inner_width = inner_local * COLS
    base = (lax.axis_index("row") * requests_local).astype(jnp.int32).reshape(1)
    ints = jnp.concatenate([base, accepted, owners, tenant_ranges.reshape(-1)])
    floats = jnp.concatenate([step_bias, decay_log, skip_gain], axis=1)

    there = []
    for r in range(ROWS):
        for c in range(COLS):
            there.append((r * COLS + c, (c // 2) * COLS + (c % 2) * ROWS + r))
    back = [(b, a) for a, b in there]

    def packed(layer, inner, proj, step, gain, out):
        joined = jnp.concatenate(
            [
                inner[layer].reshape(row_width, 2 * inner_local),
                proj[layer],
                jnp.pad(step[layer], ((0, 0), (0, 128 - heads_local))),
            ],
            axis=1,
        )
        scaled = (joined.astype(F32) * gain[layer][:, None]).astype(BF)
        return jnp.concatenate([scaled, out[layer]], axis=1)

    raw = (inner_weight, proj_weight, step_weight, input_gain, out_weight)
    weights = [lax.all_gather(packed(0, *raw), "row", axis=0)]
    block = lax.ppermute(hidden_states, ("row", "col"), there)
    head_size, state_size = state_cache.shape[3:]
    start_rows = SEND_CAP * heads_local * head_size * state_size // block.shape[1]
    begun = swap(starts(0, start_rows, ints, state_cache, block))
    later = lax.optimization_barrier(raw + (block,))
    weights.append(lax.all_gather(packed(1, *later[:-1]), "row", axis=0))

    everything = begun
    hidden_at = start_rows // block.shape[0]
    steps = None
    owned = None
    for layer in range(layer_count):
        last = layer == layer_count - 1
        head_rows = start_rows if last else 0
        part, dx, b_conv, decay = front(
            layer, head_rows, hidden_at, ints, floats, everything, weights[layer], inner_kernel,
            proj_kernel, norm_gain, inner_cache, proj_cache, state_cache,
        )
        received = swap(part)
        steps = states(layer, dx, b_conv, decay, state_cache, steps)
        if last:
            received, steps, owned = lax.optimization_barrier((received, steps, owned))
            begun = received
        else:
            received, steps = lax.optimization_barrier((received, steps))
        fresh = update(inner_width, head_rows, received, block, not last)
        owned = owned_states(
            layer, state_cache, start_rows, begun, received, head_rows // (SEND_CAP * 2 * S), owned
        )
        if not last:
            block = fresh[0]
            everything = swap(fresh)
            hidden_at = 0
    hidden = lax.ppermute(fresh, ("row", "col"), back)
    owned_block = owned[None, None]
    return (hidden, steps, owned_block)


def solution(mesh):
    placed = (
        P("col", "row"),
        P(None, "row"),
        P(None, "row", None, "col"),
        P(None, "row", None),
        P(None, "row", "col"),
        P(None, None, "col"),
        P(),
        P(None, "col"),
        P(None, "col"),
        P(None, "col"),
        P(None, "col"),
        P(None, "col", "row"),
        P(None, "row", None, "col"),
        P(None, "row", None, None),
        P(None, "row", "col", None, None),
        P("row"),
        P("row"),
        P(),
    )
    return jax.shard_map(
        local,
        mesh=mesh,
        in_specs=placed,
        out_specs=(
            P("col", "row"),
            P(None, "row", None, "col", None, None),
            P("row", "col", None, None, None, None, None),
        ),
        check_vma=False,
    )
```

time: 792 us -> 200 us (0.25)
  blocking collectives: 217 us -> 0 us
  waiting for transfers between devices: 265 us -> 81.6 us
  matrix products: 105 us -> 0 us
  other arithmetic: 90.8 us -> 2.23 us
  local copies, waits for them, and re-layouts: 86.9 us -> 27 us
  Pallas kernels: 0 us -> 34.2 us
  starting transfers between devices: 7.69 us -> 39.5 us
    reduce_scatter x6 -> x0, waiting for transfers between devices: 259 us -> none  [the longest x2 134 us: local(): lax.psum_scatter(partial_out.astype(jnp.bfloat16), 'col', scatter_dimensi...]
    psum x2 -> x0, blocking collectives: 112 us -> none  [local(): gate_square = lax.psum(jnp.sum(gated_raw * gated_raw, axis=1), 'col')]
    dot_general x40 -> x0, matrix products: 101 us -> none  [the longest x32 80.9 us: advance(): jnp.einsum('rhpn,rn->rhp', updated, c_now, precision=lax.Precision.HIGHEST)]
    all_gather x4 -> x0, blocking collectives: 79.8 us -> none  [the longest x2 46.9 us: local(): all_tokens = lax.all_gather(hidden, 'col', axis=0, tiled=True)]
    all_to_all x1 -> x4, waiting for transfers between devices: 0.01 us -> 76.4 us  [swap(): return lax.all_to_all(x, 'col', 0, 0, tiled=True)]
    dynamic_update_slice x64 -> x0, other arithmetic: 62.7 us -> none  [ssm_scan(): last_state, (outputs, states) = lax.scan(advance, start_state, time_major)]
    pallas_call x0 -> x9, Pallas kernels: none -> 34.2 us  [the longest x2 15.6 us: states(): pl.pallas_call(states_body, name='states%d' % layer, grid=(requests,), in...]
    reshape x12 -> x1, local copies, waits for them, and re-layouts: 27.8 us -> 0.09 us  [local(): ints = jnp.concatenate([base, accepted, owners, tenant_ranges.reshape(-1)])]
  transfers between devices with their start and end apart: 9 -> 8, of which waited for: 7 -> 5; matrix products, arithmetic and copies ran while one was open for 8% -> 2% of each run, Pallas kernels for 0% -> 15%
where the time goes in v2:
time: 200 us; the launch traced here: 199 us
  waiting for transfers between devices  81.6 us (41%)
  starting transfers between devices  39.5 us (20%)
  Pallas kernels  34.2 us (17%)
  local copies, waits for them, and re-layouts  27 us (14%)
  between operations  14.4 us (7%)
  other arithmetic  2.23 us (1%)
    all_to_all x4, waiting for transfers between devices, swap(): return lax.all_to_all(x, 'col', 0, 0, tiled=True)  76.4 us
    all_to_all x4, starting transfers between devices, swap(): return lax.all_to_all(x, 'col', 0, 0, tiled=True)  28.5 us
    unnamed x80, local copies, waits for them, and re-layouts  20.2 us
    pallas_call x2, Pallas kernels, states(): pl.pallas_call(states_body, name='states%d' % layer, grid=(requests,), in...  15.6 us
    ppermute x1, starting transfers between devices, local(): hidden = lax.ppermute(fresh, ('row', 'col'), back)  7.81 us
    pallas_call x2, Pallas kernels, owned_states(): pl.pallas_call(owned_body, name='owned%d' % layer, grid=(COLS // group,),...  7.54 us
    pallas_call x2, Pallas kernels, front(): pl.pallas_call(lambda *refs: front_body(layer, head_rows, *refs), name='f...  6.23 us
    ppermute x1, waiting for transfers between devices, local(): block = lax.ppermute(hidden_states, ('row', 'col'), there)  5.17 us
  transfers between devices with their start and end apart: 8, of which 5 were waited for; matrix products, arithmetic and copies ran while one was open for 2% of the time, Pallas kernels for 15%

profile of v2, /device:TPU:32, one launch (start us, length us, event | category | flops | bytes accessed | tf_op | source)
XLA Modules:
  0.0 199.0 jit_solution(12057242843598819139)
XLA Ops:
  7.3 0.7 slice.36
  8.0 0.7 slice_bitcast_fusion.6
  8.7 0.1 copy.37
  8.8 0.9 slice_bitcast_fusion.3
  9.7 1.0 slice_bitcast_fusion.2
  10.7 1.1 slice.33
  12.0 0.9 pad_maximum_fusion
  13.0 3.2 %collective-permute-start = (bf16[64,256]{1,0:T(8,128)(2,1)S(1)}, bf16[64,256]{1,0:T(8,128)(2,1)S(1)}, u32[]{:S(2)}, u32[]{:S(2)}) collective-permute-start(bf16[64,256]{1,0:T(8,128)(2,1)S(1)} %copy-done.35), channel_id=1, source_target_pairs={{0,0},{1,8},{2,16},{3,24},{4,32},{5,40},{6,48},{7,56},{8,64},{9,72... | collective-permute-start | bytes 98312 | tf_op jit(solution)/shard_map/ppermute | solution.py:491
  16.2 5.2 %collective-permute-done.hidden_ref.refs_2_ = bf16[64,256]{1,0:T(8,128)(2,1)S(1)} collective-permute-done((bf16[64,256]{1,0:T(8,128)(2,1)S(1)}, bf16[64,256]{1,0:T(8,128)(2,1)S(1)}, u32[]{:S(2)}, u32[]{:S(2)}) %collective-permute-start) | collective-permute-done | bytes 32800 | tf_op jit(solution)/shard_map/ppermute | solution.py:491
  21.4 0.1 copy.38
  21.6 0.9 slice_bitcast_fusion
  22.5 0.1 multiply_convert_fusion
  22.7 0.9 pad_maximum_fusion.1
  23.9 0.9 starts.1
  24.8 1.5 copy-done.6
  26.3 10.5 %all-to-all-start = ((bf16[16,320,256]{2,1,0:T(8,128)(2,1)}), bf16[16,320,256]{2,1,0:T(8,128)(2,1)}, u32[]{:S(2)}, u32[]{:S(2)}) async-start(bf16[16,320,256]{2,1,0:T(8,128)(2,1)} %copy-done.6), calls=%async_computation | async-start | bytes 5242880 | tf_op jit(solution)/shard_map/all_to_all | solution.py:438
  37.0 34.9 %all-to-all-done.refs_2_.starts_ref = bf16[16,320,256]{2,1,0:T(8,128)(2,1)} async-done(((bf16[16,320,256]{2,1,0:T(8,128)(2,1)}), bf16[16,320,256]{2,1,0:T(8,128)(2,1)}, u32[]{:S(2)}, u32[]{:S(2)}) %all-to-all-start) | async-done | bytes 2621472 | tf_op jit(solution)/shard_map/all_to_all | solution.py:438
  71.9 2.4 %copy-done.8 = bf16[2048,1152]{1,0:T(8,128)(2,1)S(1)} copy-done((bf16[2048,1152]{1,0:T(8,128)(2,1)S(1)}, bf16[2048,1152]{1,0:T(8,128)(2,1)}, u32[]{:S(2)}) %copy-start.8) | copy-done | bytes 4718616
  74.3 3.3 %front0.1 = (bf16[16,144,256]{2,1,0:T(8,128)(2,1)S(1)}, f32[128,256]{1,0:T(8,128)S(1)}, f32[128,128]{1,0:T(8,128)S(1)}, f32[128,512]{1,0:T(8,128)S(1)}) custom-call(s32[25]{0:T(128)S(1)} %pad_add_fusion.ints_ref.refs_0_, f32[2,12]{1,0:T(2,128)S(1)} %pad_maximum_fusion.2.refs_1_, bf16[16,320,256]{2,1,0:T(8,128)(2,1)} %all-to-all-done.refs_2_.starts_ref, ...), custom_call_target="tpu_custom_call" | custom-call | tf_op jit(solution)/shard_map/front0/pallas_call | solution.py:232
  77.7 1.0 copy-done.10
  78.7 0.7 copy-done.13
  79.4 5.6 %all-to-all-start.1 = ((bf16[16,144,256]{2,1,0:T(8,128)(2,1)}), bf16[16,144,256]{2,1,0:T(8,128)(2,1)S(1)}, u32[]{:S(2)}, u32[]{:S(2)}) async-start(bf16[16,144,256]{2,1,0:T(8,128)(2,1)} %copy-done.10), calls=%async_computation.1 | async-start | bytes 2359296 | tf_op jit(solution)/shard_map/all_to_all | solution.py:438
  85.0 0.9 copy-done.14
  86.0 7.8 %states0.1.rest_0_ = bf16[2,8,16,4,64,128]{5,4,3,2,1,0:T(8,128)(2,1)} custom-call(f32[128,256]{1,0:T(8,128)S(1)} %get-tuple-element.22.dx_ref, f32[128,128]{1,0:T(8,128)S(1)} %get-tuple-element.23.b_ref, f32[128,512]{1,0:T(8,128)S(1)} %copy-done.14, f32[2,8,4,64,128]{4,3,2,1,0:T(8,128)S(1)} %copy-done.2), custom_call_target="tpu_custom_call" | custom-call | tf_op jit(solution)/shard_map/states0/pallas_call | solution.py:290
  93.8 6.6 %all-to-all-done.1.refs_0_.refs_1_.factors_ref = bf16[16,144,256]{2,1,0:T(8,128)(2,1)S(1)} async-done(((bf16[16,144,256]{2,1,0:T(8,128)(2,1)}), bf16[16,144,256]{2,1,0:T(8,128)(2,1)S(1)}, u32[]{:S(2)}, u32[]{:S(2)}) %all-to-all-start.1) | async-done | bytes 1179680 | tf_op jit(solution)/shard_map/all_to_all | solution.py:438
  100.4 1.0 copy-done.4
  101.4 2.1 %update_spread.1 = bf16[16,64,256]{2,1,0:T(8,128)(2,1)} custom-call(bf16[16,144,256]{2,1,0:T(8,128)(2,1)} %copy-done.4, bf16[16,144,256]{2,1,0:T(8,128)(2,1)} %copy-done.4, bf16[64,256]{1,0:T(8,128)(2,1)} %copy-done.15), custom_call_target="tpu_custom_call" | custom-call | tf_op jit(solution)/shard_map/update_spread/pallas_call | solution.py:423
  103.5 6.6 %all-to-all-start.2 = ((bf16[16,64,256]{2,1,0:T(8,128)(2,1)}), bf16[16,64,256]{2,1,0:T(8,128)(2,1)S(1)}, u32[]{:S(2)}, u32[]{:S(2)}) async-start(bf16[16,64,256]{2,1,0:T(8,128)(2,1)} %update_spread.1), calls=%async_computation.2 | async-start | bytes 1048576 | tf_op jit(solution)/shard_map/all_to_all | solution.py:438
  110.1 8.2 %all-to-all-done.2.refs_2_ = bf16[16,64,256]{2,1,0:T(8,128)(2,1)S(1)} async-done(((bf16[16,64,256]{2,1,0:T(8,128)(2,1)}), bf16[16,64,256]{2,1,0:T(8,128)(2,1)S(1)}, u32[]{:S(2)}, u32[]{:S(2)}) %all-to-all-start.2) | async-done | bytes 524320 | tf_op jit(solution)/shard_map/all_to_all | solution.py:438
  118.3 2.3 %copy-done.7 = bf16[2048,1152]{1,0:T(8,128)(2,1)S(1)} copy-done((bf16[2048,1152]{1,0:T(8,128)(2,1)S(1)}, bf16[2048,1152]{1,0:T(8,128)(2,1)}, u32[]{:S(2)}) %copy-start.7) | copy-done | bytes 4718616
  120.6 0.6 copy-done.19
  121.2 0.6 copy-done.21
  121.8 0.7 copy-done.23
  122.5 2.9 %front1.1 = (bf16[16,400,256]{2,1,0:T(8,128)(2,1)S(1)}, f32[128,256]{1,0:T(8,128)S(1)}, f32[128,128]{1,0:T(8,128)S(1)}, f32[128,512]{1,0:T(8,128)S(1)}) custom-call(s32[25]{0:T(128)S(1)} %copy-done.21, f32[2,12]{1,0:T(2,128)S(1)} %copy-done.19, bf16[16,64,256]{2,1,0:T(8,128)(2,1)S(1)} %all-to-all-done.2.refs_2_, bf16[8,256,1152]{2,1,0:T(8,128)(2,1)S(1)} %bitcast.26, ...), custom_call_target="tpu_custom_call" | custom-call | tf_op jit(solution)/shard_map/front1/pallas_call | solution.py:232
  125.4 1.7 copy-done.9
  127.1 0.7 copy-done.11
  127.8 5.8 %all-to-all-start.3 = ((bf16[16,400,256]{2,1,0:T(8,128)(2,1)}), bf16[16,400,256]{2,1,0:T(8,128)(2,1)S(1)}, u32[]{:S(2)}, u32[]{:S(2)}) async-start(bf16[16,400,256]{2,1,0:T(8,128)(2,1)} %copy-done.9), calls=%async_computation.3 | async-start | bytes 6553600 | tf_op jit(solution)/shard_map/all_to_all | solution.py:438
  133.6 1.3 copy-done.5
  134.8 4.6 %owned0.1.rest_0_ = bf16[2,2,64,64,128]{4,3,2,1,0:T(8,128)(2,1)} custom-call(bf16[16,320,256]{2,1,0:T(8,128)(2,1)} %all-to-all-done.refs_2_.starts_ref, bf16[16,144,256]{2,1,0:T(8,128)(2,1)S(1)} %copy-done.5), custom_call_target="tpu_custom_call" | custom-call | tf_op jit(solution)/shard_map/owned0/pallas_call | solution.py:383
  139.5 1.4 slice_bitcast_fusion.4.refs_2_
  140.8 7.8 %states1.1 = bf16[2,8,16,4,64,128]{5,4,3,2,1,0:T(8,128)(2,1)} custom-call(f32[128,256]{1,0:T(8,128)S(1)} %get-tuple-element.32.dx_ref, f32[128,128]{1,0:T(8,128)S(1)} %get-tuple-element.33.b_ref, f32[128,512]{1,0:T(8,128)S(1)} %copy-done.12, f32[2,8,4,64,128]{4,3,2,1,0:T(8,128)S(1)} %copy-done.3, ...), custom_call_target="tpu_custom_call", output_to_operand_aliasing={{}: (4, {})} | custom-call | tf_op jit(solution)/shard_map/states1/pallas_call | solution.py:290
  148.7 26.7 %all-to-all-done.3.refs_0_.refs_1_.starts_ref.factors_ref = bf16[16,400,256]{2,1,0:T(8,128)(2,1)S(1)} async-done(((bf16[16,400,256]{2,1,0:T(8,128)(2,1)}), bf16[16,400,256]{2,1,0:T(8,128)(2,1)S(1)}, u32[]{:S(2)}, u32[]{:S(2)}) %all-to-all-start.3) | async-done | bytes 3276832 | tf_op jit(solution)/shard_map/all_to_all | solution.py:438
  175.4 1.7 copy-done
  177.0 1.9 update_last.1
  178.9 7.8 %collective-permute-start.1 = (bf16[64,256]{1,0:T(8,128)(2,1)}, bf16[64,256]{1,0:T(8,128)(2,1)S(1)}, u32[]{:S(2)}, u32[]{:S(2)}) collective-permute-start(bf16[64,256]{1,0:T(8,128)(2,1)} %update_last.1), channel_id=1, source_target_pairs={{0,0},{8,1},{16,2},{24,3},{32,4},{40,5},{48,6},{56,7},{64,8},{72,9... | collective-permute-start | bytes 98312 | tf_op jit(solution)/shard_map/ppermute | solution.py:524
  186.7 1.9 copy-done.1
  188.6 2.9 %owned1.1 = bf16[2,2,64,64,128]{4,3,2,1,0:T(8,128)(2,1)} custom-call(bf16[16,400,256]{2,1,0:T(8,128)(2,1)S(1)} %copy-done.1, bf16[16,400,256]{2,1,0:T(8,128)(2,1)S(1)} %copy-done.1, bf16[2,2,64,64,128]{4,3,2,1,0:T(8,128)(2,1)} %owned0.1.rest_0_), custom_call_target="tpu_custom_call", output_to_operand_aliasing={{}: (2, {})} | custom-call | tf_op jit(solution)/shard_map/owned1/pallas_call | solution.py:383
  191.6 0.6 copy.44
  (77 shorter events, 0.8 us)
Async XLA Ops:
  7.2 14.2 %copy-start.28 = (f32[2,256]{1,0:T(2,128)S(1)}, f32[2,256]{1,0:T(2,128)}, u32[]{:S(2)}) copy-start(f32[2,256]{1,0:T(2,128)} %param.19) | copy-start | bytes 6148
  7.2 14.2 %copy-start.27 = (bf16[2,256,4]{1,2,0:T(4,128)(2,1)S(1)}, bf16[2,256,4]{1,2,0:T(4,128)(2,1)}, u32[]{:S(2)}) copy-start(bf16[2,256,4]{1,2,0:T(4,128)(2,1)} %param.22) | copy-start | bytes 12292
  7.2 14.3 %slice-start = ((bf16[2,256,2,256]{3,2,1,0:T(2,128)(2,1)}), bf16[1,256,2,256]{3,2,1,0:T(2,128)(2,1)S(1)}, s32[]{:S(2)}) async-start(bf16[2,256,2,256]{3,2,1,0:T(2,128)(2,1)} %param.20), calls=%async_computation.6 | async-start | bytes 524288 | tf_op jit(solution)/shard_map/slice | solution.py:480
  7.2 5.8 %copy-start.35 = (bf16[64,256]{1,0:T(8,128)(2,1)S(1)}, bf16[64,256]{1,0:T(8,128)(2,1)}, u32[]{:S(2)}) copy-start(bf16[64,256]{1,0:T(8,128)(2,1)} %param.18) | copy-start | bytes 98308
  7.2 64.7 %all-gather.5.cloned.1.call-start = ((), (), s32[]{:S(2)}) async-start(), calls=%async_computation.4 | async-start | bytes 5308416 | tf_op jit(solution)/shard_map/all_gather | solution.py:490
  9.7 11.8 %copy-start.24 = (bf16[2,256,256]{2,1,0:T(8,128)(2,1)S(1)}, bf16[2,256,256]{2,1,0:T(8,128)(2,1)}, u32[]{:S(2)}) copy-start(bf16[2,256,256]{2,1,0:T(8,128)(2,1)} %param.29) | copy-start | bytes 786436
  12.9 10.7 %copy-start.29 = (s32[4,2]{0,1:T(2,128)S(1)}, s32[4,2]{0,1:T(2,128)}, u32[]{:S(2)}) copy-start(s32[4,2]{0,1:T(2,128)} %param.35) | copy-start | bytes 100
  12.9 10.9 %copy-start.33 = (s32[8]{0:T(128)S(1)}, s32[8]{0:T(128)}, u32[]{:S(2)}) copy-start(s32[8]{0:T(128)} %param.34) | copy-start | bytes 100
  12.9 10.9 %copy-start.34 = (s32[8]{0:T(128)S(1)}, s32[8]{0:T(128)}, u32[]{:S(2)}) copy-start(s32[8]{0:T(128)} %param.33) | copy-start | bytes 100
  12.9 11.0 %copy-start.2 = (f32[2,8,4,64,128]{4,3,2,1,0:T(8,128)S(1)}, f32[2,8,4,64,128]{4,3,2,1,0:T(8,128)}, u32[]{:S(2)}) copy-start(f32[2,8,4,64,128]{4,3,2,1,0:T(8,128)} %state_ref.5) | copy-start | bytes 6291460
  12.9 97.1 %all-gather.7.cloned.1.call-start = ((), (), s32[]{:S(2)}) async-start(), calls=%async_computation.5 | async-start | bytes 5308416 | tf_op jit(solution)/shard_map/all_gather | solution.py:496
  13.0 8.3 %collective-permute-start = (bf16[64,256]{1,0:T(8,128)(2,1)S(1)}, bf16[64,256]{1,0:T(8,128)(2,1)S(1)}, u32[]{:S(2)}, u32[]{:S(2)}) collective-permute-start(bf16[64,256]{1,0:T(8,128)(2,1)S(1)} %copy-done.35), channel_id=1, source_target_pairs={{0,0},{1,8},{2,16},{3,24},{4,32},{5,40},{6,48},{7,56},{8,64},{9,72... | collective-permute-start | bytes 98312 | tf_op jit(solution)/shard_map/ppermute | solution.py:491
  21.3 3.4 %copy-start.15 = (bf16[64,256]{1,0:T(8,128)(2,1)}, bf16[64,256]{1,0:T(8,128)(2,1)S(1)}, u32[]{:S(2)}) copy-start(bf16[64,256]{1,0:T(8,128)(2,1)S(1)} %collective-permute-done.hidden_ref.refs_2_) | copy-start | bytes 98308
  23.9 48.0 %copy-start.20 = (s32[25]{0:T(128)}, s32[25]{0:T(128)S(1)}, u32[]{:S(2)}) copy-start(s32[25]{0:T(128)S(1)} %pad_add_fusion.ints_ref.refs_0_) | copy-start | bytes 304
  24.8 1.5 copy-start.6
  26.3 10.6 %copy-start.25 = (bf16[2,8,3,256]{3,1,2,0:T(8,128)(2,1)S(1)}, bf16[2,8,3,256]{3,1,2,0:T(8,128)(2,1)}, u32[]{:S(2)}) copy-start(bf16[2,8,3,256]{3,1,2,0:T(8,128)(2,1)} %param.30) | copy-start | bytes 73732
  26.3 10.6 %copy-start.26 = (bf16[2,8,3,256]{3,1,2,0:T(8,128)(2,1)S(1)}, bf16[2,8,3,256]{3,1,2,0:T(8,128)(2,1)}, u32[]{:S(2)}) copy-start(bf16[2,8,3,256]{3,1,2,0:T(8,128)(2,1)} %param.31) | copy-start | bytes 73732
  26.3 10.6 %copy-start.30 = (f32[2,4]{1,0:T(2,128)S(1)}, f32[2,4]{1,0:T(2,128)}, u32[]{:S(2)}) copy-start(f32[2,4]{1,0:T(2,128)} %param.27) | copy-start | bytes 100
  26.3 10.6 %copy-start.31 = (f32[2,4]{1,0:T(2,128)S(1)}, f32[2,4]{1,0:T(2,128)}, u32[]{:S(2)}) copy-start(f32[2,4]{1,0:T(2,128)} %param.26) | copy-start | bytes 100
  26.3 10.7 %copy-start.32 = (f32[2,4]{1,0:T(2,128)S(1)}, f32[2,4]{1,0:T(2,128)}, u32[]{:S(2)}) copy-start(f32[2,4]{1,0:T(2,128)} %param.25) | copy-start | bytes 100
  26.3 45.6 %copy-start.16 = (f32[2,4,256]{2,1,0:T(4,128)S(1)}, f32[2,4,256]{2,1,0:T(4,128)}, u32[]{:S(2)}) copy-start(f32[2,4,256]{2,1,0:T(4,128)} %refs_4_.3) | copy-start | bytes 24580
  26.3 45.6 %copy-start.17 = (f32[2,4,256]{2,1,0:T(4,128)S(1)}, f32[2,4,256]{2,1,0:T(4,128)}, u32[]{:S(2)}) copy-start(f32[2,4,256]{2,1,0:T(4,128)} %refs_5_.3) | copy-start | bytes 24580
  26.3 45.6 %copy-start.22 = (f32[2,256]{1,0:T(2,128)S(1)}, f32[2,256]{1,0:T(2,128)}, u32[]{:S(2)}) copy-start(f32[2,256]{1,0:T(2,128)} %refs_6_.3) | copy-start | bytes 6148
  26.3 45.6 %all-to-all-start = ((bf16[16,320,256]{2,1,0:T(8,128)(2,1)}), bf16[16,320,256]{2,1,0:T(8,128)(2,1)}, u32[]{:S(2)}, u32[]{:S(2)}) async-start(bf16[16,320,256]{2,1,0:T(8,128)(2,1)} %copy-done.6), calls=%async_computation | async-start | bytes 5242880 | tf_op jit(solution)/shard_map/all_to_all | solution.py:438
  37.0 40.6 %copy-start.18 = (f32[2,12]{1,0:T(2,128)}, f32[2,12]{1,0:T(2,128)S(1)}, u32[]{:S(2)}) copy-start(f32[2,12]{1,0:T(2,128)S(1)} %pad_maximum_fusion.2.refs_1_) | copy-start | bytes 292
  71.9 2.4 %copy-start.8 = (bf16[2048,1152]{1,0:T(8,128)(2,1)S(1)}, bf16[2048,1152]{1,0:T(8,128)(2,1)}, u32[]{:S(2)}) copy-start(bf16[2048,1152]{1,0:T(8,128)(2,1)} %all-gather.5.cloned.1.call-done) | copy-start | bytes 14155780
  77.7 1.0 copy-start.10
  78.7 0.7 copy-start.13
  79.4 21.0 %all-to-all-start.1 = ((bf16[16,144,256]{2,1,0:T(8,128)(2,1)}), bf16[16,144,256]{2,1,0:T(8,128)(2,1)S(1)}, u32[]{:S(2)}, u32[]{:S(2)}) async-start(bf16[16,144,256]{2,1,0:T(8,128)(2,1)} %copy-done.10), calls=%async_computation.1 | async-start | bytes 2359296 | tf_op jit(solution)/shard_map/all_to_all | solution.py:438
  85.0 0.9 copy-start.14
  100.4 1.0 copy-start.4
  103.5 14.8 %all-to-all-start.2 = ((bf16[16,64,256]{2,1,0:T(8,128)(2,1)}), bf16[16,64,256]{2,1,0:T(8,128)(2,1)S(1)}, u32[]{:S(2)}, u32[]{:S(2)}) async-start(bf16[16,64,256]{2,1,0:T(8,128)(2,1)} %update_spread.1), calls=%async_computation.2 | async-start | bytes 1048576 | tf_op jit(solution)/shard_map/all_to_all | solution.py:438
  118.3 2.3 %copy-start.7 = (bf16[2048,1152]{1,0:T(8,128)(2,1)S(1)}, bf16[2048,1152]{1,0:T(8,128)(2,1)}, u32[]{:S(2)}) copy-start(bf16[2048,1152]{1,0:T(8,128)(2,1)} %all-gather.7.cloned.1.call-done) | copy-start | bytes 14155780
  120.6 0.6 copy-start.19
  121.2 0.6 copy-start.21
  121.8 0.7 copy-start.23
  125.4 1.7 copy-start.9
  127.1 0.7 copy-start.11
  127.8 47.6 %all-to-all-start.3 = ((bf16[16,400,256]{2,1,0:T(8,128)(2,1)}), bf16[16,400,256]{2,1,0:T(8,128)(2,1)S(1)}, u32[]{:S(2)}, u32[]{:S(2)}) async-start(bf16[16,400,256]{2,1,0:T(8,128)(2,1)} %copy-done.9), calls=%async_computation.3 | async-start | bytes 6553600 | tf_op jit(solution)/shard_map/all_to_all | solution.py:438
  133.6 1.3 copy-start.5
  134.8 6.0 %copy-start.3 = (f32[2,8,4,64,128]{4,3,2,1,0:T(8,128)S(1)}, f32[2,8,4,64,128]{4,3,2,1,0:T(8,128)}, u32[]{:S(2)}) copy-start(f32[2,8,4,64,128]{4,3,2,1,0:T(8,128)} %state_ref.5) | copy-start | bytes 6291460
  134.8 6.0 %copy-start.12 = (f32[128,512]{1,0:T(8,128)S(1)}, f32[128,512]{1,0:T(8,128)}, u32[]{:S(2)}) copy-start(f32[128,512]{1,0:T(8,128)} %copy-done.11) | copy-start | bytes 786436
  175.4 1.7 copy-start
  178.9 12.7 %collective-permute-start.1 = (bf16[64,256]{1,0:T(8,128)(2,1)}, bf16[64,256]{1,0:T(8,128)(2,1)S(1)}, u32[]{:S(2)}, u32[]{:S(2)}) collective-permute-start(bf16[64,256]{1,0:T(8,128)(2,1)} %update_last.1), channel_id=1, source_target_pairs={{0,0},{8,1},{16,2},{24,3},{32,4},{40,5},{48,6},{56,7},{64,8},{72,9... | collective-permute-start | bytes 98312 | tf_op jit(solution)/shard_map/ppermute | solution.py:524
  186.7 1.9 copy-start.1
Sparse Core Ops, SparseCore 0:
  13.1 36.3 all-gather.4
  51.1 34.2 all-gather.6

commit v3 on v2

--- a/solution.py
+++ b/solution.py
@@ -13,6 +13,7 @@
 BF = jnp.bfloat16
 F32 = jnp.float32
 SUM_ROWS = 16
+VMEM_BYTES = 58 * 1024 * 1024
 
 
 def silu(v):
@@ -24,7 +25,7 @@
 
 
 def route(q, ints_ref, requests):
-    owners, ranges = 1 + requests, 1 + 2 * requests
+    owners, ranges = 2 + requests, 2 + 2 * requests
     request = ints_ref[0] + q
     live = (request >= ints_ref[ranges]) & (request < ints_ref[ranges + 1])
     for k in range(ranges + 2, ints_ref.shape[0], 2):
@@ -36,18 +37,8 @@
     return live, owner, jnp.minimum(rank, SEND_CAP - 1)
 
 
-def put_start(out_ref, owner, rank, start):
-    heads, head_size, _ = start.shape
-    span = heads // 2 * head_size
-    first = pl.multiple_of(rank * span, span)
-    for k in range(heads // 2):
-        pair = jnp.concatenate([start[2 * k], start[2 * k + 1]], axis=1)
-        out_ref[owner, pl.ds(first + k * head_size, head_size), :] = pair.astype(BF)
-
-
 def front_body(
     layer,
-    head_rows,
     ints_ref,
     floats_ref,
     hidden_ref,
@@ -64,6 +55,7 @@
     dec_ref,
     x_pad,
     p_pad,
+    misc_ref,
 ):
     requests, heads, head_size, state_size = state_ref.shape
     tokens = requests * S
@@ -159,29 +151,25 @@
     yg = (g * norm_gain_ref[layer : layer + 1, :]).astype(BF)
     g2 = (g * g).astype(BF)
     ones = jnp.ones((SUM_ROWS, width), BF)
-    part_row = head_rows + SEND_CAP * 2 * S
-    sum_row = part_row + block_tokens
-    part_ref[:, :part_row, :] = jnp.zeros((COLS, part_row, width), BF)
+    misc_row = block_tokens + SEND_CAP * S
+    line = lax.broadcasted_iota(jnp.int32, (SUM_ROWS, 1), 0)
+    part_ref[:, block_tokens:misc_row, :] = jnp.zeros((COLS, SEND_CAP * S, width), BF)
+    nothing = jnp.zeros((SUM_ROWS, width - block_tokens), F32)
     for b in range(2):
         sums = lax.dot_general(
             ones,
             g2[b * block_tokens : (b + 1) * block_tokens, :],
             (((1,), (1,)), ((), ())),
             preferred_element_type=F32,
-        ).astype(BF)
+        )
+        sums = jnp.where(line == 0, jnp.concatenate([sums, nothing], axis=1), 0.0)
         for r in range(ROWS):
-            part_ref[b * ROWS + r, sum_row:, :] = jnp.zeros((SUM_ROWS, width), BF)
-            part_ref[b * ROWS + r, sum_row:, 0:block_tokens] = sums
-    for r in range(ROWS):
-        part = jnp.dot(yg, weight_ref[r, :, in_cols:], preferred_element_type=F32).astype(BF)
-        for b in range(2):
-            part_ref[b * ROWS + r, part_row:sum_row, :] = part[
-                b * block_tokens : (b + 1) * block_tokens, :
-            ]
+            misc_ref[b * ROWS + r] = sums
     step = lax.broadcasted_iota(jnp.int32, (S, 1), 0)
+    column = ints_ref[1]
     for q in range(requests):
         live, owner, rank = route(q, ints_ref, requests)
-        taken = ints_ref[1 + q] - 1
+        taken = ints_ref[2 + q] - 1
         rows = slice(q * S, (q + 1) * S)
         cum_q = cum_all[rows, :]
         cum_end = jnp.sum(jnp.where(step == taken, cum_q, 0.0), axis=0, keepdims=True)
@@ -190,26 +178,31 @@
         scale = jnp.exp(cum_end)
         high = scale.astype(BF).astype(F32)
         low = scale - high
+        mine = jnp.sum(jnp.where(step == column, b_conv[rows, :], 0.0), axis=0, keepdims=True)
+        mine = jnp.concatenate([mine, jnp.zeros((1, width - state_size), F32)], axis=1)
+        at = 1 + 3 * rank
         extra = jnp.where(
-            step == 0,
-            high[:, :128],
-            jnp.where(
-                step == 1, high[:, 128:], jnp.where(step == 2, low[:, :128], low[:, 128:])
-            ),
-        )
-        first = pl.multiple_of(head_rows + rank * 2 * S, 2 * S)
+            line == at,
+            mine,
+            jnp.where(line == at + 1, high, jnp.where(line == at + 2, low, 0.0)),
+        )
+        first = pl.multiple_of(block_tokens + rank * S, S)
 
         @pl.when(live)
         def _send():
             part_ref[owner, pl.ds(first, S), :] = (dx[rows, :] * weight).astype(BF)
-            part_ref[owner, pl.ds(first + S, S), :] = jnp.concatenate(
-                [b_conv[rows, :], extra], axis=1
-            ).astype(BF)
-            if head_rows:
-                put_start(part_ref, owner, rank, state_ref[q])
-
-
-def front(layer, head_rows, hidden_at, ints, floats, hidden, weight, inner_kernel, proj_kernel,
+            misc_ref[owner] = misc_ref[owner] + extra
+
+    part_ref[:, misc_row:, :] = misc_ref[...].astype(BF)
+    for r in range(ROWS):
+        part = jnp.dot(yg, weight_ref[r, :, in_cols:], preferred_element_type=F32).astype(BF)
+        for b in range(2):
+            part_ref[b * ROWS + r, 0:block_tokens, :] = part[
+                b * block_tokens : (b + 1) * block_tokens, :
+            ]
+
+
+def front(layer, ints, floats, hidden, weight, inner_kernel, proj_kernel,
           norm_gain, inner_cache, proj_cache, state):
     layers, requests, heads, head_size, state_size = state.shape
     width = heads * head_size
@@ -224,18 +217,18 @@
 
     block_tokens = tokens // 2
     out_shapes = [
-        ((COLS, head_rows + SEND_CAP * 2 * S + block_tokens + SUM_ROWS, width), BF),
+        ((COLS, block_tokens + SEND_CAP * S + SUM_ROWS, width), BF),
         ((tokens, width), F32),
         ((tokens, state_size), F32),
         ((tokens, heads * 128), F32),
     ]
     return pl.pallas_call(
-        lambda *refs: front_body(layer, head_rows, *refs),
+        lambda *refs: front_body(layer, *refs),
         name="front%d" % layer,
         grid=(1,),
         in_specs=[
             smem, smem,
-            pl.BlockSpec((COLS, block_tokens, hidden.shape[2]), lambda i: (0, hidden_at, 0)),
+            whole(hidden.shape),
             whole(weight.shape),
             layer_of(inner_kernel.shape),
             layer_of(proj_kernel.shape),
@@ -249,9 +242,10 @@
         scratch_shapes=[
             pltpu.VMEM((requests, 24, width), F32),
             pltpu.VMEM((requests, 24, 2 * state_size), F32),
+            pltpu.VMEM((COLS, SUM_ROWS, width), F32),
         ],
         compiler_params=pltpu.CompilerParams(
-            dimension_semantics=("arbitrary",), vmem_limit_bytes=40 * 1024 * 1024
+            dimension_semantics=("arbitrary",), vmem_limit_bytes=VMEM_BYTES
         ),
     )(ints, floats, hidden, weight, inner_kernel, proj_kernel, norm_gain,
       inner_cache, proj_cache, state)
@@ -300,81 +294,78 @@
         ),
         input_output_aliases=aliases,
         compiler_params=pltpu.CompilerParams(
-            dimension_semantics=("arbitrary",), vmem_limit_bytes=24 * 1024 * 1024
+            dimension_semantics=("arbitrary",), vmem_limit_bytes=VMEM_BYTES
         ),
     )(*operands)
 
 
-def starts_body(ints_ref, state_ref, hidden_ref, send_ref):
-    rows = send_ref.shape[1] - hidden_ref.shape[0]
-    send_ref[:, :rows, :] = jnp.zeros((COLS, rows, send_ref.shape[2]), BF)
-    hidden = hidden_ref[...]
-    for c in range(COLS):
-        send_ref[c, rows:, :] = hidden
+def starts_body(ints_ref, state_ref, send_ref):
+    send_ref[...] = jnp.zeros(send_ref.shape, BF)
     requests = state_ref.shape[0]
     for q in range(requests):
         live, owner, rank = route(q, ints_ref, requests)
 
         @pl.when(live)
         def _put():
-            put_start(send_ref, owner, rank, state_ref[q])
-
-
-def starts(layer, head_rows, ints, state, hidden):
-    shape = (COLS, head_rows + hidden.shape[0], hidden.shape[1])
+            send_ref[owner, rank] = state_ref[q].astype(BF)
+
+
+def starts(layer, ints, state):
+    shape = (COLS, SEND_CAP) + state.shape[2:]
     return pl.pallas_call(
         starts_body,
-        name="starts",
+        name="starts%d" % layer,
         grid=(1,),
         in_specs=[
             pl.BlockSpec(memory_space=pltpu.SMEM),
             pl.BlockSpec((None,) + state.shape[1:], lambda i: (layer, 0, 0, 0, 0)),
-            pl.BlockSpec(hidden.shape, lambda i: (0, 0)),
         ],
-        out_specs=pl.BlockSpec(shape, lambda i: (0, 0, 0)),
+        out_specs=pl.BlockSpec(shape, lambda i: (0, 0, 0, 0, 0)),
         out_shape=jax.ShapeDtypeStruct(shape, BF),
         compiler_params=pltpu.CompilerParams(
-            dimension_semantics=("arbitrary",), vmem_limit_bytes=24 * 1024 * 1024
-        ),
-    )(ints, state, hidden)
-
-
-def owned_body(starts_ref, factors_ref, *rest):
+            dimension_semantics=("arbitrary",), vmem_limit_bytes=VMEM_BYTES
+        ),
+    )(ints, state)
+
+
+def owned_body(starts_ref, dx_ref, misc_ref, *rest):
     out_ref = rest[-1]
+    i = pl.program_id(0)
     group = starts_ref.shape[0]
     slots, group_heads, head_size, state_size = out_ref.shape
     heads = group_heads // group
-    span = heads // 2 * head_size
-    for g in range(group):
-        for slot in range(slots):
-            row = slot * 2 * S
-            dx = factors_ref[g, row : row + S, :]
-            other = factors_ref[g, row + S : row + 2 * S, :]
+    for slot in range(slots):
+        row = 1 + 3 * slot
+        b_all = misc_ref[:, row, 0:state_size]
+        for g in range(group):
+            dx = dx_ref[g, slot * S : (slot + 1) * S, :]
             added = lax.dot_general(
-                dx, other[:, :state_size], (((0,), (0,)), ((), ())), preferred_element_type=F32
+                dx, b_all, (((0,), (0,)), ((), ())), preferred_element_type=F32
             )
-            tail = other[:, state_size:].astype(F32)
+            scales = misc_ref[i * group + g, row + 1 : row + 3, :].astype(F32)
+            scales = scales[0:1, :] + scales[1:2, :]
             for h in range(heads):
-                k, half = h // 2, h % 2
-                lane = half * 64
-                scale = tail[k : k + 1, lane : lane + 1] + tail[k + 2 : k + 3, lane : lane + 1]
-                at = slot * span + k * head_size
-                begun = starts_ref[
-                    g, at : at + head_size, half * state_size : (half + 1) * state_size
-                ]
+                scale = scales[:, h * head_size : h * head_size + 1]
                 out_ref[slot, g * heads + h] = (
-                    begun.astype(F32) * scale + added[h * head_size : (h + 1) * head_size, :]
+                    starts_ref[g, slot, h].astype(F32) * scale
+                    + added[h * head_size : (h + 1) * head_size, :]
                 ).astype(BF)
 
 
-def owned_states(layer, state, head_rows, begun, factors, factors_at, previous):
+def owned_states(layer, state, begun, received, previous):
     layers, _, heads, head_size, state_size = state.shape
     group = 4
+    width = received.shape[2]
+    dx_rows = SEND_CAP * S
+    block_tokens = received.shape[1] - dx_rows - SUM_ROWS
+    dx_at = block_tokens // dx_rows
+    misc_at = (block_tokens + dx_rows) // SUM_ROWS
     in_specs = [
-        pl.BlockSpec((group, head_rows, begun.shape[2]), lambda i: (i, 0, 0)),
-        pl.BlockSpec((group, SEND_CAP * 2 * S, begun.shape[2]), lambda i: (i, factors_at, 0)),
+        pl.BlockSpec((group,) + begun.shape[1:], lambda i: (i, 0, 0, 0, 0)),
+        pl.BlockSpec((group, dx_rows, width), lambda i: (i, dx_at, 0)),
+        pl.BlockSpec((COLS, SUM_ROWS, width), lambda i: (0, misc_at, 0)),
     ]
-    operands = [begun, factors]
+    operands = [begun, received, received]
     aliases = {}
     if previous is not None:
         in_specs.append(pl.BlockSpec(memory_space=pl.ANY))
@@ -394,12 +385,12 @@
         ),
         input_output_aliases=aliases,
         compiler_params=pltpu.CompilerParams(
-            dimension_semantics=("arbitrary",), vmem_limit_bytes=16 * 1024 * 1024
+            dimension_semantics=("arbitrary",), vmem_limit_bytes=VMEM_BYTES
         ),
     )(*operands)
 
 
-def update_body(inner_width, part_ref, sums_ref, hidden_ref, out_ref):
+def update_body(inner_width, part_ref, sums_ref, hidden_ref, *outs):
     rows = hidden_ref.shape[0]
     total = part_ref[0].astype(F32)
     sums = sums_ref[0, :, 0:128].astype(F32)
@@ -408,29 +399,34 @@
         sums = sums + sums_ref[c, :, 0:128].astype(F32)
     scale = lax.rsqrt(sums.T[:rows, 0:1] / inner_width + EPSILON)
     fresh = (hidden_ref[...].astype(F32) + total * scale).astype(BF)
-    if len(out_ref.shape) == 3:
+    outs[0][...] = fresh
+    for spread_ref in outs[1:]:
         for c in range(COLS):
-            out_ref[c] = fresh
-    else:
-        out_ref[...] = fresh
-
-
-def update(inner_width, head_rows, received, hidden, spread):
+            spread_ref[c] = fresh
+
+
+def update(inner_width, received, hidden, spread):
     rows, lanes = hidden.shape
-    shape = ((COLS,) if spread else ()) + hidden.shape
-    part_at = (head_rows + SEND_CAP * 2 * S) // rows
-    sums_at = (head_rows + SEND_CAP * 2 * S + rows) // SUM_ROWS
+    shapes = [hidden.shape] + ([(COLS,) + hidden.shape] if spread else [])
+    sums_at = (rows + SEND_CAP * S) // SUM_ROWS
+
+    def whole(shape):
+        return pl.BlockSpec(shape, lambda i: (0,) * len(shape))
+
     return pl.pallas_call(
         lambda *refs: update_body(inner_width, *refs),
         name="update_spread" if spread else "update_last",
         grid=(1,),
         in_specs=[
-            pl.BlockSpec((COLS, rows, lanes), lambda i: (0, part_at, 0)),
+            pl.BlockSpec((COLS, rows, lanes), lambda i: (0, 0, 0)),
             pl.BlockSpec((COLS, SUM_ROWS, lanes), lambda i: (0, sums_at, 0)),
-            pl.BlockSpec(hidden.shape, lambda i: (0, 0)),
+            whole(hidden.shape),
         ],
-        out_specs=pl.BlockSpec(shape, lambda i: (0,) * len(shape)),
-        out_shape=jax.ShapeDtypeStruct(shape, BF),
+        out_specs=[whole(shape) for shape in shapes],
+        out_shape=[jax.ShapeDtypeStruct(shape, BF) for shape in shapes],
+        compiler_params=pltpu.CompilerParams(
+            dimension_semantics=("arbitrary",), vmem_limit_bytes=VMEM_BYTES
+        ),
     )(received, received, hidden)
 
 
@@ -465,7 +461,8 @@
     requests_local = state_cache.shape[1]
     inner_width = inner_local * COLS
     base = (lax.axis_index("row") * requests_local).astype(jnp.int32).reshape(1)
-    ints = jnp.concatenate([base, accepted, owners, tenant_ranges.reshape(-1)])
+    column = lax.axis_index("col").astype(jnp.int32).reshape(1)
+    ints = jnp.concatenate([base, column, accepted, owners, tenant_ranges.reshape(-1)])
     floats = jnp.concatenate([step_bias, decay_log, skip_gain], axis=1)
 
     there = []
@@ -486,42 +483,36 @@
         scaled = (joined.astype(F32) * gain[layer][:, None]).astype(BF)
         return jnp.concatenate([scaled, out[layer]], axis=1)
 
+    block = lax.ppermute(hidden_states, ("row", "col"), there)
     raw = (inner_weight, proj_weight, step_weight, input_gain, out_weight)
-    weights = [lax.all_gather(packed(0, *raw), "row", axis=0)]
-    block = lax.ppermute(hidden_states, ("row", "col"), there)
-    head_size, state_size = state_cache.shape[3:]
-    start_rows = SEND_CAP * heads_local * head_size * state_size // block.shape[1]
-    begun = swap(starts(0, start_rows, ints, state_cache, block))
-    later = lax.optimization_barrier(raw + (block,))
-    weights.append(lax.all_gather(packed(1, *later[:-1]), "row", axis=0))
-
-    everything = begun
-    hidden_at = start_rows // block.shape[0]
+    first, block = lax.optimization_barrier((packed(0, *raw), block))
+    weights = [lax.all_gather(first, "row", axis=0)]
+    everything = swap(jnp.broadcast_to(block[None], (COLS,) + block.shape))
+    sends = [starts(layer, ints, state_cache) for layer in range(layer_count)]
+    everything, sends, raw = lax.optimization_barrier((everything, sends, raw))
+    weights.append(lax.all_gather(packed(1, *raw), "row", axis=0))
+    begun = swap(sends[0])
+    send = sends[1]
+
     steps = None
     owned = None
     for layer in range(layer_count):
         last = layer == layer_count - 1
-        head_rows = start_rows if last else 0
         part, dx, b_conv, decay = front(
-            layer, head_rows, hidden_at, ints, floats, everything, weights[layer], inner_kernel,
-            proj_kernel, norm_gain, inner_cache, proj_cache, state_cache,
-        )
+            layer, ints, floats, everything, weights[layer], inner_kernel, proj_kernel,
+            norm_gain, inner_cache, proj_cache, state_cache,
+        )
+        part, begun, owned = lax.optimization_barrier((part, begun, owned))
         received = swap(part)
         steps = states(layer, dx, b_conv, decay, state_cache, steps)
-        if last:
-            received, steps, owned = lax.optimization_barrier((received, steps, owned))
-            begun = received
-        else:
-            received, steps = lax.optimization_barrier((received, steps))
-        fresh = update(inner_width, head_rows, received, block, not last)
-        owned = owned_states(
-            layer, state_cache, start_rows, begun, received, head_rows // (SEND_CAP * 2 * S), owned
-        )
+        received, steps = lax.optimization_barrier((received, steps))
+        fresh = update(inner_width, received, block, not last)
+        owned = owned_states(layer, state_cache, begun, received, owned)
         if not last:
             block = fresh[0]
-            everything = swap(fresh)
-            hidden_at = 0
-    hidden = lax.ppermute(fresh, ("row", "col"), back)
+            everything, send = lax.optimization_barrier((swap(fresh[1]), send))
+            begun = swap(send)
+    hidden = lax.ppermute(fresh[0], ("row", "col"), back)
     owned_block = owned[None, None]
     return (hidden, steps, owned_block)
 

time: 200 us -> 182 us (0.910)
  waiting for transfers between devices: 81.6 us -> 40.8 us
  Pallas kernels: 34.2 us -> 51.3 us
  local copies, waits for them, and re-layouts: 27 us -> 11.5 us
  blocking collectives: 0 us -> 15.2 us
  starting transfers between devices: 39.5 us -> 43.9 us
    all_to_all x4 -> x5, waiting for transfers between devices: 76.4 us -> 32.5 us  [swap(): return lax.all_to_all(x, 'col', 0, 0, tiled=True)]
    all_to_all x0 -> x1, blocking collectives: none -> 15.2 us  [swap(): return lax.all_to_all(x, 'col', 0, 0, tiled=True)]
    unnamed x80 -> x44, local copies, waits for them, and re-layouts: 20.2 us -> 5.61 us
    pallas_call x3 -> x4, Pallas kernels: 7.09 us -> 18.7 us  [the longest x2 12.6 us: front(): pl.pallas_call(lambda *refs: front_body(layer, *refs), name='front%d' % l...]
    all_gather x2, waiting for transfers between devices: 0.01 us -> 8.21 us  [the longest x1 8.21 us: local(): weights = [lax.all_gather(first, 'row', axis=0)]]
    all_to_all x4 -> x5, starting transfers between devices: 28.5 us -> 34.2 us  [swap(): return lax.all_to_all(x, 'col', 0, 0, tiled=True)]
    ppermute x1, waiting for transfers between devices: 5.17 us -> 0.01 us  [local(): block = lax.ppermute(hidden_states, ('row', 'col'), there)]
    pallas_call x2, Pallas kernels: 15.6 us -> 19.6 us  [states(): pl.pallas_call(states_body, name='states%d' % layer, grid=(requests,), in...]
  transfers between devices with their start and end apart: 8 -> 9, of which waited for: 5 -> 6; matrix products, arithmetic and copies ran while one was open for 2% -> 6% of each run, Pallas kernels for 15% -> 28%
where the time goes in v3:
time: 182 us; the launch traced here: 180 us
  Pallas kernels  51.3 us (28%)
  starting transfers between devices  43.9 us (24%)
  waiting for transfers between devices  40.8 us (22%)
  blocking collectives  15.2 us (8%)
  between operations  14.3 us (8%)
  local copies, waits for them, and re-layouts  11.5 us (6%)
  other arithmetic  2.71 us (1%)
    all_to_all x5, starting transfers between devices, swap(): return lax.all_to_all(x, 'col', 0, 0, tiled=True)  34.2 us
    all_to_all x5, waiting for transfers between devices, swap(): return lax.all_to_all(x, 'col', 0, 0, tiled=True)  32.5 us
    pallas_call x2, Pallas kernels, states(): pl.pallas_call(states_body, name='states%d' % layer, grid=(requests,), in...  19.6 us
    all_to_all x1, blocking collectives, swap(): return lax.all_to_all(x, 'col', 0, 0, tiled=True)  15.2 us
    pallas_call x2, Pallas kernels, front(): pl.pallas_call(lambda *refs: front_body(layer, *refs), name='front%d' % l...  12.6 us
    pallas_call x2, Pallas kernels, owned_states(): pl.pallas_call(owned_body, name='owned%d' % layer, grid=(COLS // group,),...  9.06 us
    all_gather x1, waiting for transfers between devices, local(): weights = [lax.all_gather(first, 'row', axis=0)]  8.21 us
    ppermute x1, starting transfers between devices, local(): hidden = lax.ppermute(fresh[0], ('row', 'col'), back)  6.54 us
  transfers between devices with their start and end apart: 9, of which 6 were waited for; matrix products, arithmetic and copies ran while one was open for 6% of the time, Pallas kernels for 28%

profile of v3, /device:TPU:32, one launch (start us, length us, event | category | flops | bytes accessed | tf_op | source)
XLA Modules:
  0.0 179.6 jit_solution(8470026046453710591)
XLA Ops:
  7.2 0.0 all-gather.5.cloned.1.call-start
  7.2 3.0 %collective-permute-start = (bf16[64,256]{1,0:T(8,128)(2,1)}, bf16[64,256]{1,0:T(8,128)(2,1)S(1)}, u32[]{:S(2)}, u32[]{:S(2)}) collective-permute-start(bf16[64,256]{1,0:T(8,128)(2,1)} %param.18), channel_id=1, source_target_pairs={{0,0},{1,8},{2,16},{3,24},{4,32},{5,40},{6,48},{7,56},{8,64},{9,72... | collective-permute-start | bytes 98312 | tf_op jit(solution)/shard_map/ppermute | solution.py:486
  10.2 0.7 slice.33
  10.9 0.7 slice_bitcast_fusion.5
  11.6 0.1 copy.37
  11.8 0.9 slice_bitcast_fusion.3
  12.7 0.9 slice_bitcast_fusion.2
  13.6 1.1 slice.30
  14.8 0.1 multiply_convert_fusion.1
  15.0 0.9 pad_maximum_fusion
  15.9 0.8 broadcast_in_dim.4
  16.7 10.2 %all-to-all-start = ((bf16[16,64,256]{2,1,0:T(8,128)(2,1)}), bf16[16,64,256]{2,1,0:T(8,128)(2,1)S(1)}, u32[]{:S(2)}, u32[]{:S(2)}) async-start(bf16[16,64,256]{2,1,0:T(8,128)(2,1)} %broadcast_in_dim.4), calls=%async_computation | async-start | bytes 1048576 | tf_op jit(solution)/shard_map/all_to_all | solution.py:434
  26.9 0.0 all-gather.7.cloned.1.call-start
  26.9 0.1 copy.30
  27.0 0.1 reshape.20
  27.1 0.7 concatenate.18.ints_ref.refs_0_
  27.8 3.1 %starts1.1 = bf16[16,2,4,64,128]{4,3,2,1,0:T(8,128)(2,1)} custom-call(s32[26]{0:T(128)} %concatenate.18.ints_ref.refs_0_, f32[2,8,4,64,128]{4,3,2,1,0:T(8,128)} %state_ref.7), custom_call_target="tpu_custom_call" | custom-call | tf_op jit(solution)/shard_map/starts1/pallas_call | solution.py:315
  30.9 3.1 %starts0.1 = bf16[16,2,4,64,128]{4,3,2,1,0:T(8,128)(2,1)} custom-call(s32[26]{0:T(128)} %concatenate.18.ints_ref.refs_0_, f32[2,8,4,64,128]{4,3,2,1,0:T(8,128)} %state_ref.7), custom_call_target="tpu_custom_call" | custom-call | tf_op jit(solution)/shard_map/starts0/pallas_call | solution.py:315
  33.9 1.8 %all-to-all-done.refs_2_ = bf16[16,64,256]{2,1,0:T(8,128)(2,1)S(1)} async-done(((bf16[16,64,256]{2,1,0:T(8,128)(2,1)}), bf16[16,64,256]{2,1,0:T(8,128)(2,1)S(1)}, u32[]{:S(2)}, u32[]{:S(2)}) %all-to-all-start) | async-done | bytes 524320 | tf_op jit(solution)/shard_map/all_to_all | solution.py:434
  35.8 0.1 copy.38
  36.0 0.1 multiply_convert_fusion
  36.2 0.9 pad_maximum_fusion.1
  37.2 6.4 %all-to-all-start.1 = ((bf16[16,2,4,64,128]{4,3,2,1,0:T(8,128)(2,1)}), bf16[16,2,4,64,128]{4,3,2,1,0:T(8,128)(2,1)S(1)}, u32[]{:S(2)}, u32[]{:S(2)}) async-start(bf16[16,2,4,64,128]{4,3,2,1,0:T(8,128)(2,1)} %starts0.1), calls=%async_computation.1 | async-start | bytes 4194304 | tf_op jit(solution)/shard_map/all_to_all | solution.py:434
  43.5 0.6 copy.32.refs_7_
  44.1 0.6 copy.33.refs_8_
  44.8 0.7 pad_maximum_fusion.2.refs_1_
  45.4 8.2 %all-gather.5.cloned.1.call-done = bf16[2048,1152]{1,0:T(8,128)(2,1)} async-done(((bf16[256,1152]{1,0:T(8,128)(2,1)}), bf16[2048,1152]{1,0:T(8,128)(2,1)}) %all-gather.5.cloned.1.call-update) | async-done | bytes 4718608 | tf_op jit(solution)/shard_map/all_gather | solution.py:489
  53.6 6.3 %front0.1 = (bf16[16,112,256]{2,1,0:T(8,128)(2,1)}, f32[128,256]{1,0:T(8,128)}, f32[128,128]{1,0:T(8,128)}, f32[128,512]{1,0:T(8,128)}) custom-call(s32[26]{0:T(128)} %concatenate.18.ints_ref.refs_0_, f32[2,12]{1,0:T(2,128)} %pad_maximum_fusion.2.refs_1_, bf16[16,64,256]{2,1,0:T(8,128)(2,1)} %copy-done.4, bf16[8,256,1152]{2,1,0:T(8,128)(2,1)} %bitcast.26, ...), custom_call_target="tpu_custom_call" | custom-call | tf_op jit(solution)/shard_map/front0/pallas_call | solution.py:225
  59.9 11.5 %all-to-all-done.1.starts_ref = bf16[16,2,4,64,128]{4,3,2,1,0:T(8,128)(2,1)S(1)} async-done(((bf16[16,2,4,64,128]{4,3,2,1,0:T(8,128)(2,1)}), bf16[16,2,4,64,128]{4,3,2,1,0:T(8,128)(2,1)S(1)}, u32[]{:S(2)}, u32[]{:S(2)}) %all-to-all-start.1) | async-done | bytes 2097184 | tf_op jit(solution)/shard_map/all_to_all | solution.py:434
  71.4 1.3 copy-done.3
  72.8 5.4 %all-to-all-start.2 = ((bf16[16,112,256]{2,1,0:T(8,128)(2,1)}), bf16[16,112,256]{2,1,0:T(8,128)(2,1)S(1)}, u32[]{:S(2)}, u32[]{:S(2)}) async-start(bf16[16,112,256]{2,1,0:T(8,128)(2,1)} %get-tuple-element.39), calls=%async_computation.2 | async-start | bytes 1835008 | tf_op jit(solution)/shard_map/all_to_all | solution.py:434
  78.2 9.8 %states0.1.rest_0_ = bf16[2,8,16,4,64,128]{5,4,3,2,1,0:T(8,128)(2,1)} custom-call(f32[128,256]{1,0:T(8,128)} %get-tuple-element.40.dx_ref, f32[128,128]{1,0:T(8,128)} %get-tuple-element.41.b_ref, f32[128,512]{1,0:T(8,128)} %get-tuple-element.42.dec_ref, f32[2,8,4,64,128]{4,3,2,1,0:T(8,128)} %state_ref.7), custom_call_target="tpu_custom_call" | custom-call | tf_op jit(solution)/shard_map/states0/pallas_call | solution.py:284
  88.0 2.9 %all-to-all-done.2.refs_0_.refs_1_.dx_ref.misc_ref = bf16[16,112,256]{2,1,0:T(8,128)(2,1)S(1)} async-done(((bf16[16,112,256]{2,1,0:T(8,128)(2,1)}), bf16[16,112,256]{2,1,0:T(8,128)(2,1)S(1)}, u32[]{:S(2)}, u32[]{:S(2)}) %all-to-all-start.2) | async-done | bytes 917536 | tf_op jit(solution)/shard_map/all_to_all | solution.py:434
  90.8 0.9 copy-done.1
  91.8 2.1 %update_spread.1 = (bf16[64,256]{1,0:T(8,128)(2,1)}, bf16[16,64,256]{2,1,0:T(8,128)(2,1)}) custom-call(bf16[16,112,256]{2,1,0:T(8,128)(2,1)} %copy-done.1, bf16[16,112,256]{2,1,0:T(8,128)(2,1)} %copy-done.1, bf16[64,256]{1,0:T(8,128)(2,1)} %copy-done.7), custom_call_target="tpu_custom_call" | custom-call | tf_op jit(solution)/shard_map/update_spread/pallas_call | solution.py:416
  93.9 15.2 %all_to_all.30.refs_2_ = bf16[16,64,256]{2,1,0:T(8,128)(2,1)} all-to-all(bf16[16,64,256]{2,1,0:T(8,128)(2,1)} %get-tuple-element.44), channel_id=1, replica_groups=mesh['row'=8,'col'=16] {'col'}, dimensions={0} | all-to-all | bytes 1048576 | tf_op jit(solution)/shard_map/all_to_all | solution.py:434
  109.0 5.8 %all-to-all-start.4 = ((bf16[16,2,4,64,128]{4,3,2,1,0:T(8,128)(2,1)}), bf16[16,2,4,64,128]{4,3,2,1,0:T(8,128)(2,1)S(1)}, u32[]{:S(2)}, u32[]{:S(2)}) async-start(bf16[16,2,4,64,128]{4,3,2,1,0:T(8,128)(2,1)} %starts1.1), calls=%async_computation.4 | async-start | bytes 4194304 | tf_op jit(solution)/shard_map/all_to_all | solution.py:434
  114.8 4.5 %owned0.1.rest_0_ = bf16[2,2,64,64,128]{4,3,2,1,0:T(8,128)(2,1)} custom-call(bf16[16,2,4,64,128]{4,3,2,1,0:T(8,128)(2,1)} %copy-done.3, bf16[16,112,256]{2,1,0:T(8,128)(2,1)} %copy-done.1, bf16[16,112,256]{2,1,0:T(8,128)(2,1)} %copy-done.1), custom_call_target="tpu_custom_call" | custom-call | tf_op jit(solution)/shard_map/owned0/pallas_call | solution.py:374
  119.3 6.3 %front1.1 = (bf16[16,112,256]{2,1,0:T(8,128)(2,1)}, f32[128,256]{1,0:T(8,128)}, f32[128,128]{1,0:T(8,128)}, f32[128,512]{1,0:T(8,128)}) custom-call(s32[26]{0:T(128)} %concatenate.18.ints_ref.refs_0_, f32[2,12]{1,0:T(2,128)} %pad_maximum_fusion.2.refs_1_, bf16[16,64,256]{2,1,0:T(8,128)(2,1)} %all_to_all.30.refs_2_, bf16[8,256,1152]{2,1,0:T(8,128)(2,1)} %bitcast.27, ...), custom_call_target="tpu_custom_call" | custom-call | tf_op jit(solution)/shard_map/front1/pallas_call | solution.py:225
  125.6 13.8 %all-to-all-done.4.starts_ref = bf16[16,2,4,64,128]{4,3,2,1,0:T(8,128)(2,1)S(1)} async-done(((bf16[16,2,4,64,128]{4,3,2,1,0:T(8,128)(2,1)}), bf16[16,2,4,64,128]{4,3,2,1,0:T(8,128)(2,1)S(1)}, u32[]{:S(2)}, u32[]{:S(2)}) %all-to-all-start.4) | async-done | bytes 2097184 | tf_op jit(solution)/shard_map/all_to_all | solution.py:434
  139.5 6.5 %all-to-all-start.5 = ((bf16[16,112,256]{2,1,0:T(8,128)(2,1)}), bf16[16,112,256]{2,1,0:T(8,128)(2,1)S(1)}, u32[]{:S(2)}, u32[]{:S(2)}) async-start(bf16[16,112,256]{2,1,0:T(8,128)(2,1)} %get-tuple-element.55), calls=%async_computation.5 | async-start | bytes 1835008 | tf_op jit(solution)/shard_map/all_to_all | solution.py:434
  146.0 9.7 %states1.1 = bf16[2,8,16,4,64,128]{5,4,3,2,1,0:T(8,128)(2,1)} custom-call(f32[128,256]{1,0:T(8,128)} %get-tuple-element.56.dx_ref, f32[128,128]{1,0:T(8,128)} %get-tuple-element.57.b_ref, f32[128,512]{1,0:T(8,128)} %get-tuple-element.58.dec_ref, f32[2,8,4,64,128]{4,3,2,1,0:T(8,128)} %state_ref.7, ...), custom_call_target="tpu_custom_call", output_to_operand_aliasing={{}: (4, {})} | custom-call | tf_op jit(solution)/shard_map/states1/pallas_call | solution.py:284
  155.7 2.5 %all-to-all-done.5.refs_0_.refs_1_.dx_ref.misc_ref = bf16[16,112,256]{2,1,0:T(8,128)(2,1)S(1)} async-done(((bf16[16,112,256]{2,1,0:T(8,128)(2,1)}), bf16[16,112,256]{2,1,0:T(8,128)(2,1)S(1)}, u32[]{:S(2)}, u32[]{:S(2)}) %all-to-all-start.5) | async-done | bytes 917536 | tf_op jit(solution)/shard_map/all_to_all | solution.py:434
  158.3 0.9 copy-done
  159.2 1.9 %update_last.1 = bf16[64,256]{1,0:T(8,128)(2,1)} custom-call(bf16[16,112,256]{2,1,0:T(8,128)(2,1)} %copy-done, bf16[16,112,256]{2,1,0:T(8,128)(2,1)} %copy-done, bf16[64,256]{1,0:T(8,128)(2,1)} %get-tuple-element.61.refs_2_), custom_call_target="tpu_custom_call" | custom-call | tf_op jit(solution)/shard_map/update_last/pallas_call | solution.py:416
  161.0 6.5 %collective-permute-start.1 = (bf16[64,256]{1,0:T(8,128)(2,1)}, bf16[64,256]{1,0:T(8,128)(2,1)S(1)}, u32[]{:S(2)}, u32[]{:S(2)}) collective-permute-start(bf16[64,256]{1,0:T(8,128)(2,1)} %update_last.1), channel_id=1, source_target_pairs={{0,0},{8,1},{16,2},{24,3},{32,4},{40,5},{48,6},{56,7},{64,8},{72,9... | collective-permute-start | bytes 98312 | tf_op jit(solution)/shard_map/ppermute | solution.py:515
  167.6 4.5 %owned1.1 = bf16[2,2,64,64,128]{4,3,2,1,0:T(8,128)(2,1)} custom-call(bf16[16,2,4,64,128]{4,3,2,1,0:T(8,128)(2,1)} %copy-done.2, bf16[16,112,256]{2,1,0:T(8,128)(2,1)} %copy-done, bf16[16,112,256]{2,1,0:T(8,128)(2,1)} %copy-done, bf16[2,2,64,64,128]{4,3,2,1,0:T(8,128)(2,1)} %owned0.1.rest_0_), custom_call_target="tpu_custom_call", output_to_operand_aliasing={{}: (3, {})} | custom-call | tf_op jit(solution)/shard_map/owned1/pallas_call | solution.py:374
  172.1 0.6 copy.44
  (45 shorter events, 0.2 us)
Async XLA Ops:
  7.2 46.5 %all-gather.5.cloned.1.call-start = ((), (), s32[]{:S(2)}) async-start(), calls=%async_computation.6 | async-start | bytes 5308416 | tf_op jit(solution)/shard_map/all_gather | solution.py:489
  7.2 8.6 %collective-permute-start = (bf16[64,256]{1,0:T(8,128)(2,1)}, bf16[64,256]{1,0:T(8,128)(2,1)S(1)}, u32[]{:S(2)}, u32[]{:S(2)}) collective-permute-start(bf16[64,256]{1,0:T(8,128)(2,1)} %param.18), channel_id=1, source_target_pairs={{0,0},{1,8},{2,16},{3,24},{4,32},{5,40},{6,48},{7,56},{8,64},{9,72... | collective-permute-start | bytes 98312 | tf_op jit(solution)/shard_map/ppermute | solution.py:486
  14.8 12.1 %copy-start.12 = (s32[4,2]{0,1:T(2,128)S(1)}, s32[4,2]{0,1:T(2,128)}, u32[]{:S(2)}) copy-start(s32[4,2]{0,1:T(2,128)} %param.35) | copy-start | bytes 100
  14.8 12.3 %copy-start.16 = (s32[8]{0:T(128)S(1)}, s32[8]{0:T(128)}, u32[]{:S(2)}) copy-start(s32[8]{0:T(128)} %param.33) | copy-start | bytes 100
  14.8 12.3 %copy-start.17 = (s32[8]{0:T(128)S(1)}, s32[8]{0:T(128)}, u32[]{:S(2)}) copy-start(s32[8]{0:T(128)} %param.34) | copy-start | bytes 100
  15.8 15.0 %copy-start.7 = (bf16[64,256]{1,0:T(8,128)(2,1)}, bf16[64,256]{1,0:T(8,128)(2,1)S(1)}, u32[]{:S(2)}) copy-start(bf16[64,256]{1,0:T(8,128)(2,1)S(1)} %collective-permute-done.refs_2_) | copy-start | bytes 98308
  16.7 19.1 %all-to-all-start = ((bf16[16,64,256]{2,1,0:T(8,128)(2,1)}), bf16[16,64,256]{2,1,0:T(8,128)(2,1)S(1)}, u32[]{:S(2)}, u32[]{:S(2)}) async-start(bf16[16,64,256]{2,1,0:T(8,128)(2,1)} %broadcast_in_dim.4), calls=%async_computation | async-start | bytes 1048576 | tf_op jit(solution)/shard_map/all_to_all | solution.py:434
  26.9 92.4 %all-gather.7.cloned.1.call-start = ((), (), s32[]{:S(2)}) async-start(), calls=%async_computation.7 | async-start | bytes 5308416 | tf_op jit(solution)/shard_map/all_gather | solution.py:493
  30.8 4.9 %copy-start.11 = (f32[2,256]{1,0:T(2,128)S(1)}, f32[2,256]{1,0:T(2,128)}, u32[]{:S(2)}) copy-start(f32[2,256]{1,0:T(2,128)} %param.19) | copy-start | bytes 6148
  30.8 4.9 %copy-start.10 = (bf16[2,256,4]{1,2,0:T(4,128)(2,1)S(1)}, bf16[2,256,4]{1,2,0:T(4,128)(2,1)}, u32[]{:S(2)}) copy-start(bf16[2,256,4]{1,2,0:T(4,128)(2,1)} %param.22) | copy-start | bytes 12292
  30.8 5.1 %slice-start = ((bf16[2,256,2,256]{3,2,1,0:T(2,128)(2,1)}), bf16[1,256,2,256]{3,2,1,0:T(2,128)(2,1)S(1)}, s32[]{:S(2)}) async-start(bf16[2,256,2,256]{3,2,1,0:T(2,128)(2,1)} %param.20), calls=%async_computation.8 | async-start | bytes 524288 | tf_op jit(solution)/shard_map/slice | solution.py:477
  30.8 5.1 %copy-start.5 = (bf16[2,256,256]{2,1,0:T(8,128)(2,1)S(1)}, bf16[2,256,256]{2,1,0:T(8,128)(2,1)}, u32[]{:S(2)}) copy-start(bf16[2,256,256]{2,1,0:T(8,128)(2,1)} %param.29) | copy-start | bytes 786436
  30.8 5.1 %copy-start.6 = (bf16[2,256,256]{2,1,0:T(8,128)(2,1)S(1)}, bf16[2,256,256]{2,1,0:T(8,128)(2,1)}, u32[]{:S(2)}) copy-start(bf16[2,256,256]{2,1,0:T(8,128)(2,1)} %param.21) | copy-start | bytes 786436
  35.8 1.3 copy-start.4
  37.1 6.4 %copy-start.8 = (bf16[2,8,3,256]{3,1,2,0:T(8,128)(2,1)S(1)}, bf16[2,8,3,256]{3,1,2,0:T(8,128)(2,1)}, u32[]{:S(2)}) copy-start(bf16[2,8,3,256]{3,1,2,0:T(8,128)(2,1)} %param.30) | copy-start | bytes 73732
  37.1 7.0 %copy-start.9 = (bf16[2,8,3,256]{3,1,2,0:T(8,128)(2,1)S(1)}, bf16[2,8,3,256]{3,1,2,0:T(8,128)(2,1)}, u32[]{:S(2)}) copy-start(bf16[2,8,3,256]{3,1,2,0:T(8,128)(2,1)} %param.31) | copy-start | bytes 73732
  37.1 7.6 %copy-start.13 = (f32[2,4]{1,0:T(2,128)S(1)}, f32[2,4]{1,0:T(2,128)}, u32[]{:S(2)}) copy-start(f32[2,4]{1,0:T(2,128)} %param.27) | copy-start | bytes 100
  37.1 7.6 %copy-start.14 = (f32[2,4]{1,0:T(2,128)S(1)}, f32[2,4]{1,0:T(2,128)}, u32[]{:S(2)}) copy-start(f32[2,4]{1,0:T(2,128)} %param.26) | copy-start | bytes 100
  37.1 7.6 %copy-start.15 = (f32[2,4]{1,0:T(2,128)S(1)}, f32[2,4]{1,0:T(2,128)}, u32[]{:S(2)}) copy-start(f32[2,4]{1,0:T(2,128)} %param.25) | copy-start | bytes 100
  37.2 34.2 %all-to-all-start.1 = ((bf16[16,2,4,64,128]{4,3,2,1,0:T(8,128)(2,1)}), bf16[16,2,4,64,128]{4,3,2,1,0:T(8,128)(2,1)S(1)}, u32[]{:S(2)}, u32[]{:S(2)}) async-start(bf16[16,2,4,64,128]{4,3,2,1,0:T(8,128)(2,1)} %starts0.1), calls=%async_computation.1 | async-start | bytes 4194304 | tf_op jit(solution)/shard_map/all_to_all | solution.py:434
  71.4 1.3 copy-start.3
  72.8 18.1 %all-to-all-start.2 = ((bf16[16,112,256]{2,1,0:T(8,128)(2,1)}), bf16[16,112,256]{2,1,0:T(8,128)(2,1)S(1)}, u32[]{:S(2)}, u32[]{:S(2)}) async-start(bf16[16,112,256]{2,1,0:T(8,128)(2,1)} %get-tuple-element.39), calls=%async_computation.2 | async-start | bytes 1835008 | tf_op jit(solution)/shard_map/all_to_all | solution.py:434
  90.8 0.9 copy-start.1
  109.0 30.4 %all-to-all-start.4 = ((bf16[16,2,4,64,128]{4,3,2,1,0:T(8,128)(2,1)}), bf16[16,2,4,64,128]{4,3,2,1,0:T(8,128)(2,1)S(1)}, u32[]{:S(2)}, u32[]{:S(2)}) async-start(bf16[16,2,4,64,128]{4,3,2,1,0:T(8,128)(2,1)} %starts1.1), calls=%async_computation.4 | async-start | bytes 4194304 | tf_op jit(solution)/shard_map/all_to_all | solution.py:434
  139.5 16.3 %copy-start.2 = (bf16[16,2,4,64,128]{4,3,2,1,0:T(8,128)(2,1)}, bf16[16,2,4,64,128]{4,3,2,1,0:T(8,128)(2,1)S(1)}, u32[]{:S(2)}) copy-start(bf16[16,2,4,64,128]{4,3,2,1,0:T(8,128)(2,1)S(1)} %all-to-all-done.4.starts_ref) | copy-start | bytes 6291460
  139.5 18.8 %all-to-all-start.5 = ((bf16[16,112,256]{2,1,0:T(8,128)(2,1)}), bf16[16,112,256]{2,1,0:T(8,128)(2,1)S(1)}, u32[]{:S(2)}, u32[]{:S(2)}) async-start(bf16[16,112,256]{2,1,0:T(8,128)(2,1)} %get-tuple-element.55), calls=%async_computation.5 | async-start | bytes 1835008 | tf_op jit(solution)/shard_map/all_to_all | solution.py:434
  158.3 0.9 copy-start
  161.0 11.1 %collective-permute-start.1 = (bf16[64,256]{1,0:T(8,128)(2,1)}, bf16[64,256]{1,0:T(8,128)(2,1)S(1)}, u32[]{:S(2)}, u32[]{:S(2)}) collective-permute-start(bf16[64,256]{1,0:T(8,128)(2,1)} %update_last.1), channel_id=1, source_target_pairs={{0,0},{8,1},{16,2},{24,3},{32,4},{40,5},{48,6},{56,7},{64,8},{72,9... | collective-permute-start | bytes 98312 | tf_op jit(solution)/shard_map/ppermute | solution.py:515
Sparse Core Ops, SparseCore 0:
  16.0 37.6 all-gather.4
  55.3 34.2 all-gather.6

commit v4 on v3

--- a/solution.py
+++ b/solution.py
@@ -14,6 +14,7 @@
 F32 = jnp.float32
 SUM_ROWS = 16
 VMEM_BYTES = 58 * 1024 * 1024
+SMALL_VMEM_BYTES = 12 * 1024 * 1024
 
 
 def silu(v):
@@ -22,6 +23,46 @@
 
 def softplus(v):
     return jnp.maximum(v, 0.0) + jnp.log1p(jnp.exp(-jnp.abs(v)))
+
+
+def pack_body(layer, inner_ref, proj_ref, step_ref, gain_ref, out_ref, packed_ref):
+    rows, width = out_ref.shape
+    states = proj_ref.shape[1]
+    gain = jnp.broadcast_to(gain_ref[layer : layer + 1, :], (8, rows)).T[:, 0:1]
+    step = step_ref[...].astype(F32)
+    step = jnp.concatenate([step, jnp.zeros((128 - step.shape[0], rows), F32)], axis=0).T
+    at = 0
+    for piece in (inner_ref[0], inner_ref[1], proj_ref[...], step):
+        end = at + piece.shape[1]
+        packed_ref[:, at:end] = (piece.astype(F32) * gain).astype(BF)
+        at = end
+    packed_ref[:, at:] = out_ref[...]
+
+
+def pack(layer, inner, proj, step, gain, out):
+    rows, width = inner.shape[2:]
+    cols = 2 * width + proj.shape[2] + 128 + out.shape[2]
+
+    def layer_of(shape):
+        return pl.BlockSpec((None,) + shape[1:], lambda i: (layer,) + (0,) * (len(shape) - 1))
+
+    return pl.pallas_call(
+        lambda *refs: pack_body(layer, *refs),
+        name="pack%d" % layer,
+        grid=(1,),
+        in_specs=[
+            layer_of(inner.shape),
+            layer_of(proj.shape),
+            layer_of(step.shape),
+            pl.BlockSpec(gain.shape, lambda i: (0, 0)),
+            layer_of(out.shape),
+        ],
+        out_specs=pl.BlockSpec((rows, cols), lambda i: (0, 0)),
+        out_shape=jax.ShapeDtypeStruct((rows, cols), BF),
+        compiler_params=pltpu.CompilerParams(
+            dimension_semantics=("arbitrary",), vmem_limit_bytes=VMEM_BYTES
+        ),
+    )(inner, proj, step, gain, out)
 
 
 def route(q, ints_ref, requests):
@@ -294,7 +335,7 @@
         ),
         input_output_aliases=aliases,
         compiler_params=pltpu.CompilerParams(
-            dimension_semantics=("arbitrary",), vmem_limit_bytes=VMEM_BYTES
+            dimension_semantics=("arbitrary",), vmem_limit_bytes=SMALL_VMEM_BYTES
         ),
     )(*operands)
 
@@ -329,26 +370,37 @@
 
 
 def owned_body(starts_ref, dx_ref, misc_ref, *rest):
-    out_ref = rest[-1]
+    out_ref, b_s, scale_s = rest[-3:]
     i = pl.program_id(0)
     group = starts_ref.shape[0]
     slots, group_heads, head_size, state_size = out_ref.shape
     heads = group_heads // group
+
+    @pl.when(i == 0)
+    def _first():
+        for slot in range(slots):
+            row = 1 + 3 * slot
+            for c in range(COLS):
+                lines = misc_ref[c].astype(F32)
+                b_s[slot, c : c + 1, :] = lines[row : row + 1, 0:state_size]
+                scale_s[slot, c : c + 1, :] = (
+                    lines[row + 1 : row + 2, :] + lines[row + 2 : row + 3, :]
+                )
+
     for slot in range(slots):
-        row = 1 + 3 * slot
-        b_all = misc_ref[:, row, 0:state_size]
+        dx = jnp.concatenate(
+            [dx_ref[g, slot * S : (slot + 1) * S, :] for g in range(group)], axis=1
+        )
+        added = lax.dot_general(
+            dx, b_s[slot].astype(BF), (((0,), (0,)), ((), ())), preferred_element_type=F32
+        )
         for g in range(group):
-            dx = dx_ref[g, slot * S : (slot + 1) * S, :]
-            added = lax.dot_general(
-                dx, b_all, (((0,), (0,)), ((), ())), preferred_element_type=F32
-            )
-            scales = misc_ref[i * group + g, row + 1 : row + 3, :].astype(F32)
-            scales = scales[0:1, :] + scales[1:2, :]
+            scales = scale_s[slot, pl.ds(i * group + g, 1), :]
             for h in range(heads):
                 scale = scales[:, h * head_size : h * head_size + 1]
+                at = (g * heads + h) * head_size
                 out_ref[slot, g * heads + h] = (
-                    starts_ref[g, slot, h].astype(F32) * scale
-                    + added[h * head_size : (h + 1) * head_size, :]
+                    starts_ref[g, slot, h].astype(F32) * scale + added[at : at + head_size, :]
                 ).astype(BF)
 
 
@@ -383,9 +435,13 @@
         out_shape=jax.ShapeDtypeStruct(
             (SEND_CAP, layers, COLS * heads, head_size, state_size), BF
         ),
+        scratch_shapes=[
+            pltpu.VMEM((SEND_CAP, COLS, state_size), F32),
+            pltpu.VMEM((SEND_CAP, COLS, width), F32),
+        ],
         input_output_aliases=aliases,
         compiler_params=pltpu.CompilerParams(
-            dimension_semantics=("arbitrary",), vmem_limit_bytes=VMEM_BYTES
+            dimension_semantics=("arbitrary",), vmem_limit_bytes=SMALL_VMEM_BYTES
         ),
     )(*operands)
 
@@ -425,7 +481,7 @@
         out_specs=[whole(shape) for shape in shapes],
         out_shape=[jax.ShapeDtypeStruct(shape, BF) for shape in shapes],
         compiler_params=pltpu.CompilerParams(
-            dimension_semantics=("arbitrary",), vmem_limit_bytes=VMEM_BYTES
+            dimension_semantics=("arbitrary",), vmem_limit_bytes=SMALL_VMEM_BYTES
         ),
     )(received, received, hidden)
 
@@ -455,7 +511,6 @@
     tenant_ranges,
 ):
     layer_count = inner_weight.shape[0]
-    row_width = inner_weight.shape[1]
     inner_local = inner_weight.shape[3]
     heads_local = step_weight.shape[2]
     requests_local = state_cache.shape[1]
@@ -471,26 +526,20 @@
             there.append((r * COLS + c, (c // 2) * COLS + (c % 2) * ROWS + r))
     back = [(b, a) for a, b in there]
 
-    def packed(layer, inner, proj, step, gain, out):
-        joined = jnp.concatenate(
-            [
-                inner[layer].reshape(row_width, 2 * inner_local),
-                proj[layer],
-                jnp.pad(step[layer], ((0, 0), (0, 128 - heads_local))),
-            ],
-            axis=1,
-        )
-        scaled = (joined.astype(F32) * gain[layer][:, None]).astype(BF)
-        return jnp.concatenate([scaled, out[layer]], axis=1)
-
     block = lax.ppermute(hidden_states, ("row", "col"), there)
-    raw = (inner_weight, proj_weight, step_weight, input_gain, out_weight)
-    first, block = lax.optimization_barrier((packed(0, *raw), block))
+    raw = (
+        jnp.transpose(inner_weight, (0, 2, 1, 3)),
+        proj_weight,
+        jnp.transpose(step_weight, (0, 2, 1)),
+        input_gain,
+        out_weight,
+    )
+    first, block = lax.optimization_barrier((pack(0, *raw), block))
     weights = [lax.all_gather(first, "row", axis=0)]
     everything = swap(jnp.broadcast_to(block[None], (COLS,) + block.shape))
     sends = [starts(layer, ints, state_cache) for layer in range(layer_count)]
     everything, sends, raw = lax.optimization_barrier((everything, sends, raw))
-    weights.append(lax.all_gather(packed(1, *raw), "row", axis=0))
+    weights.append(lax.all_gather(pack(1, *raw), "row", axis=0))
     begun = swap(sends[0])
     send = sends[1]
 

time: 182 us -> 176 us (0.967)
  starting transfers between devices: 43.9 us -> 47.6 us
  Pallas kernels: 51.3 us -> 48.4 us
  waiting for transfers between devices: 40.8 us -> 38.5 us
  other arithmetic: 2.71 us -> 0.6 us
    pallas_call x0 -> x2, Pallas kernels: none -> 4.52 us  [pack(): pl.pallas_call(lambda *refs: pack_body(layer, *refs), name='pack%d' % lay...]
    pallas_call x2, Pallas kernels: 19.6 us -> 15.6 us  [states(): pl.pallas_call(states_body, name='states%d' % layer, grid=(requests,), in...]
    unnamed x44 -> x39, local copies, waits for them, and re-layouts: 5.61 us -> 9.29 us
    pallas_call x2, Pallas kernels: 3.95 us -> 0.41 us  [update(): pl.pallas_call(lambda *refs: update_body(inner_width, *refs), name='updat...]
    all_to_all x5, waiting for transfers between devices: 32.5 us -> 29.5 us  [swap(): return lax.all_to_all(x, 'col', 0, 0, tiled=True)]
    squeeze x5 -> x0, local copies, waits for them, and re-layouts: 2.54 us -> none  [the longest x2 0.94 us: packed(): return jnp.concatenate([scaled, out[layer]], axis=1)]
    all_to_all x5, starting transfers between devices: 34.2 us -> 36.7 us  [swap(): return lax.all_to_all(x, 'col', 0, 0, tiled=True)]
    slice x5 -> x0, local copies, waits for them, and re-layouts: 1.83 us -> none  [the longest x3 1.14 us: packed(): inner[layer].reshape(row_width, 2 * inner_local)]
  transfers between devices with their start and end apart: 9 -> 9, of which waited for: 6 -> 7; matrix products, arithmetic and copies ran while one was open for 6% -> 3% of each run, Pallas kernels for 28% -> 28%
where the time goes in v4:
time: 176 us; the launch traced here: 174 us
  Pallas kernels  48.4 us (28%)
  starting transfers between devices  47.6 us (27%)
  waiting for transfers between devices  38.5 us (22%)
  blocking collectives  14.4 us (8%)
  between operations  14.2 us (8%)
  local copies, waits for them, and re-layouts  10.8 us (6%)
    all_to_all x5, starting transfers between devices, swap(): return lax.all_to_all(x, 'col', 0, 0, tiled=True)  36.7 us
    all_to_all x5, waiting for transfers between devices, swap(): return lax.all_to_all(x, 'col', 0, 0, tiled=True)  29.5 us
    pallas_call x2, Pallas kernels, states(): pl.pallas_call(states_body, name='states%d' % layer, grid=(requests,), in...  15.6 us
    all_to_all x1, blocking collectives, swap(): return lax.all_to_all(x, 'col', 0, 0, tiled=True)  14.4 us
    pallas_call x2, Pallas kernels, front(): pl.pallas_call(lambda *refs: front_body(layer, *refs), name='front%d' % l...  12.8 us
    unnamed x39, local copies, waits for them, and re-layouts  9.29 us
    pallas_call x2, Pallas kernels, owned_states(): pl.pallas_call(owned_body, name='owned%d' % layer, grid=(COLS // group,),...  9.01 us
    ppermute x1, starting transfers between devices, local(): hidden = lax.ppermute(fresh[0], ('row', 'col'), back)  7.71 us
  transfers between devices with their start and end apart: 9, of which 7 were waited for; matrix products, arithmetic and copies ran while one was open for 3% of the time, Pallas kernels for 28%

profile of v4, /device:TPU:32, one launch (start us, length us, event | category | flops | bytes accessed | tf_op | source)
XLA Modules:
  0.0 174.4 jit_solution(8075408622673871917)
XLA Ops:
  7.2 0.0 all-gather.5.cloned.1.call-start
  7.2 3.0 %collective-permute-start = (bf16[64,256]{1,0:T(8,128)(2,1)}, bf16[64,256]{1,0:T(8,128)(2,1)S(1)}, u32[]{:S(2)}, u32[]{:S(2)}) collective-permute-start(bf16[64,256]{1,0:T(8,128)(2,1)} %param.18), channel_id=1, source_target_pairs={{0,0},{1,8},{2,16},{3,24},{4,32},{5,40},{6,48},{7,56},{8,64},{9,72... | collective-permute-start | bytes 98312 | tf_op jit(solution)/shard_map/ppermute | solution.py:529
  10.3 1.9 %copy.36 = bf16[2,256,2,256]{3,1,2,0:T(8,128)(2,1)} copy(bf16[2,256,2,256]{3,2,1,0:T(2,128)(2,1)} %param.20) | data formatting | bytes 1048576 | tf_op args[2]
  12.2 2.1 %pack0.1 = bf16[256,1152]{1,0:T(8,128)(2,1)} custom-call(bf16[2,2,256,256]{3,2,1,0:T(8,128)(2,1)} %bitcast.12, bf16[2,256,256]{2,1,0:T(8,128)(2,1)} %refs_1_.2, bf16[2,4,256]{2,1,0:T(4,128)(2,1)} %bitcast.14, f32[2,256]{1,0:T(2,128)} %refs_3_.2, bf16[2,256,256]{2,1,0:T(8,128)(2,1)} %refs_4_.5), custom_call_target="tpu_custom_call" | custom-call | tf_op jit(solution)/shard_map/pack0/pallas_call | solution.py:49
  14.3 1.3 collective-permute-done.refs_2_
  15.7 0.0 all-gather.5.cloned.1.call-update
  15.7 0.8 broadcast_in_dim.4
  16.5 10.4 %all-to-all-start = ((bf16[16,64,256]{2,1,0:T(8,128)(2,1)}), bf16[16,64,256]{2,1,0:T(8,128)(2,1)S(1)}, u32[]{:S(2)}, u32[]{:S(2)}) async-start(bf16[16,64,256]{2,1,0:T(8,128)(2,1)} %broadcast_in_dim.4), calls=%async_computation | async-start | bytes 1048576 | tf_op jit(solution)/shard_map/all_to_all | solution.py:490
  26.9 0.0 all-gather.7.cloned.1.call-start
  27.0 0.1 copy.29
  27.1 0.1 reshape.18
  27.2 0.6 concatenate.6.ints_ref.refs_0_
  27.8 3.0 %starts1.1 = bf16[16,2,4,64,128]{4,3,2,1,0:T(8,128)(2,1)} custom-call(s32[26]{0:T(128)} %concatenate.6.ints_ref.refs_0_, f32[2,8,4,64,128]{4,3,2,1,0:T(8,128)} %state_ref.7), custom_call_target="tpu_custom_call" | custom-call | tf_op jit(solution)/shard_map/starts1/pallas_call | solution.py:356
  30.8 3.0 %starts0.1 = bf16[16,2,4,64,128]{4,3,2,1,0:T(8,128)(2,1)} custom-call(s32[26]{0:T(128)} %concatenate.6.ints_ref.refs_0_, f32[2,8,4,64,128]{4,3,2,1,0:T(8,128)} %state_ref.7), custom_call_target="tpu_custom_call" | custom-call | tf_op jit(solution)/shard_map/starts0/pallas_call | solution.py:356
  33.8 0.0 copy-start.14
  33.8 1.6 all-to-all-done.refs_2_
  35.4 2.4 %pack1.1 = bf16[256,1152]{1,0:T(8,128)(2,1)} custom-call(bf16[2,2,256,256]{3,2,1,0:T(8,128)(2,1)} %bitcast.13, bf16[2,256,256]{2,1,0:T(8,128)(2,1)} %refs_1_.2, bf16[2,4,256]{2,1,0:T(4,128)(2,1)} %bitcast.15, f32[2,256]{1,0:T(2,128)} %refs_3_.2, bf16[2,256,256]{2,1,0:T(8,128)(2,1)} %refs_4_.5), custom_call_target="tpu_custom_call" | custom-call | tf_op jit(solution)/shard_map/pack1/pallas_call | solution.py:49
  37.7 0.0 all-gather.7.cloned.1.call-update
  37.8 6.5 %all-to-all-start.1 = ((bf16[16,2,4,64,128]{4,3,2,1,0:T(8,128)(2,1)}), bf16[16,2,4,64,128]{4,3,2,1,0:T(8,128)(2,1)}, u32[]{:S(2)}, u32[]{:S(2)}) async-start(bf16[16,2,4,64,128]{4,3,2,1,0:T(8,128)(2,1)} %starts0.1), calls=%async_computation.1 | async-start | bytes 4194304 | tf_op jit(solution)/shard_map/all_to_all | solution.py:490
  44.2 0.6 copy.31.refs_7_
  44.9 0.6 copy.32.refs_8_
  45.5 0.6 pad_maximum_fusion.refs_1_
  46.1 7.6 %all-gather.5.cloned.1.call-done = bf16[2048,1152]{1,0:T(8,128)(2,1)} async-done(((bf16[256,1152]{1,0:T(8,128)(2,1)}), bf16[2048,1152]{1,0:T(8,128)(2,1)}) %all-gather.5.cloned.1.call-update) | async-done | bytes 4718608 | tf_op jit(solution)/shard_map/all_gather | solution.py:538
  53.7 6.4 %front0.1 = (bf16[16,112,256]{2,1,0:T(8,128)(2,1)}, f32[128,256]{1,0:T(8,128)}, f32[128,128]{1,0:T(8,128)}, f32[128,512]{1,0:T(8,128)}) custom-call(s32[26]{0:T(128)} %concatenate.6.ints_ref.refs_0_, f32[2,12]{1,0:T(2,128)} %pad_maximum_fusion.refs_1_, bf16[16,64,256]{2,1,0:T(8,128)(2,1)} %copy-done.8, bf16[8,256,1152]{2,1,0:T(8,128)(2,1)} %bitcast.10, ...), custom_call_target="tpu_custom_call" | custom-call | tf_op jit(solution)/shard_map/front0/pallas_call | solution.py:266
  60.1 9.7 %all-to-all-done.1.starts_ref = bf16[16,2,4,64,128]{4,3,2,1,0:T(8,128)(2,1)} async-done(((bf16[16,2,4,64,128]{4,3,2,1,0:T(8,128)(2,1)}), bf16[16,2,4,64,128]{4,3,2,1,0:T(8,128)(2,1)}, u32[]{:S(2)}, u32[]{:S(2)}) %all-to-all-start.1) | async-done | bytes 2097184 | tf_op jit(solution)/shard_map/all_to_all | solution.py:490
  69.8 6.7 %all-to-all-start.2 = ((bf16[16,112,256]{2,1,0:T(8,128)(2,1)}), bf16[16,112,256]{2,1,0:T(8,128)(2,1)S(1)}, u32[]{:S(2)}, u32[]{:S(2)}) async-start(bf16[16,112,256]{2,1,0:T(8,128)(2,1)} %get-tuple-element.39), calls=%async_computation.2 | async-start | bytes 1835008 | tf_op jit(solution)/shard_map/all_to_all | solution.py:490
  76.5 0.0 copy-start.3
  76.5 0.9 copy-done.3
  77.4 0.9 copy-done.5
  78.3 0.8 copy-done.7
  79.2 7.8 %states0.1.rest_0_ = bf16[2,8,16,4,64,128]{5,4,3,2,1,0:T(8,128)(2,1)} custom-call(f32[128,256]{1,0:T(8,128)S(1)} %copy-done.5, f32[128,128]{1,0:T(8,128)S(1)} %copy-done.7, f32[128,512]{1,0:T(8,128)S(1)} %copy-done.3, f32[2,8,4,64,128]{4,3,2,1,0:T(8,128)S(1)} %copy-done), custom_call_target="tpu_custom_call" | custom-call | tf_op jit(solution)/shard_map/states0/pallas_call | solution.py:325
  87.0 1.9 %all-to-all-done.2.refs_0_.refs_1_.dx_ref.misc_ref = bf16[16,112,256]{2,1,0:T(8,128)(2,1)S(1)} async-done(((bf16[16,112,256]{2,1,0:T(8,128)(2,1)}), bf16[16,112,256]{2,1,0:T(8,128)(2,1)S(1)}, u32[]{:S(2)}, u32[]{:S(2)}) %all-to-all-start.2) | async-done | bytes 917536 | tf_op jit(solution)/shard_map/all_to_all | solution.py:490
  88.9 0.2 update_spread.1
  89.1 14.4 %all_to_all.30.refs_2_ = bf16[16,64,256]{2,1,0:T(8,128)(2,1)} all-to-all(bf16[16,64,256]{2,1,0:T(8,128)(2,1)S(1)} %get-tuple-element.44), channel_id=1, replica_groups=mesh['row'=8,'col'=16] {'col'}, dimensions={0} | all-to-all | bytes 1048576 | tf_op jit(solution)/shard_map/all_to_all | solution.py:490
  103.5 6.4 %all-to-all-start.4 = ((bf16[16,2,4,64,128]{4,3,2,1,0:T(8,128)(2,1)}), bf16[16,2,4,64,128]{4,3,2,1,0:T(8,128)(2,1)}, u32[]{:S(2)}, u32[]{:S(2)}) async-start(bf16[16,2,4,64,128]{4,3,2,1,0:T(8,128)(2,1)} %starts1.1), calls=%async_computation.4 | async-start | bytes 4194304 | tf_op jit(solution)/shard_map/all_to_all | solution.py:490
  110.0 4.5 %owned0.1.rest_0_ = bf16[2,2,64,64,128]{4,3,2,1,0:T(8,128)(2,1)} custom-call(bf16[16,2,4,64,128]{4,3,2,1,0:T(8,128)(2,1)} %all-to-all-done.1.starts_ref, bf16[16,112,256]{2,1,0:T(8,128)(2,1)S(1)} %all-to-all-done.2.refs_0_.refs_1_.dx_ref.misc_ref, bf16[16,112,256]{2,1,0:T(8,128)(2,1)S(1)} %all-to-all-done.2.refs_0_.refs_1_.dx_ref.misc_ref), custom_call_target="tpu_custom_call" | custom-call | tf_op jit(solution)/shard_map/owned0/pallas_call | solution.py:426
  114.5 6.4 %front1.1 = (bf16[16,112,256]{2,1,0:T(8,128)(2,1)}, f32[128,256]{1,0:T(8,128)}, f32[128,128]{1,0:T(8,128)}, f32[128,512]{1,0:T(8,128)}) custom-call(s32[26]{0:T(128)} %concatenate.6.ints_ref.refs_0_, f32[2,12]{1,0:T(2,128)} %pad_maximum_fusion.refs_1_, bf16[16,64,256]{2,1,0:T(8,128)(2,1)} %all_to_all.30.refs_2_, bf16[8,256,1152]{2,1,0:T(8,128)(2,1)} %bitcast.11, ...), custom_call_target="tpu_custom_call" | custom-call | tf_op jit(solution)/shard_map/front1/pallas_call | solution.py:266
  120.9 14.5 %all-to-all-done.4.starts_ref = bf16[16,2,4,64,128]{4,3,2,1,0:T(8,128)(2,1)} async-done(((bf16[16,2,4,64,128]{4,3,2,1,0:T(8,128)(2,1)}), bf16[16,2,4,64,128]{4,3,2,1,0:T(8,128)(2,1)}, u32[]{:S(2)}, u32[]{:S(2)}) %all-to-all-start.4) | async-done | bytes 2097184 | tf_op jit(solution)/shard_map/all_to_all | solution.py:490
  135.4 6.7 %all-to-all-start.5 = ((bf16[16,112,256]{2,1,0:T(8,128)(2,1)}), bf16[16,112,256]{2,1,0:T(8,128)(2,1)S(1)}, u32[]{:S(2)}, u32[]{:S(2)}) async-start(bf16[16,112,256]{2,1,0:T(8,128)(2,1)} %get-tuple-element.55), calls=%async_computation.5 | async-start | bytes 1835008 | tf_op jit(solution)/shard_map/all_to_all | solution.py:490
  142.1 0.9 copy-done.2
  143.1 0.9 copy-done.4
  144.0 0.8 copy-done.6
  144.8 7.8 %states1.1 = bf16[2,8,16,4,64,128]{5,4,3,2,1,0:T(8,128)(2,1)} custom-call(f32[128,256]{1,0:T(8,128)S(1)} %copy-done.4, f32[128,128]{1,0:T(8,128)S(1)} %copy-done.6, f32[128,512]{1,0:T(8,128)S(1)} %copy-done.2, f32[2,8,4,64,128]{4,3,2,1,0:T(8,128)S(1)} %copy-done.1, bf16[2,8,16,4,64,128]{5,4,3,2,1,0:T(8,128)(2,1)} %states0.1.rest_0_), custom_call_target="tpu_custom_call", output_to_operand_aliasing={{}: (4, {})} | custom-call | tf_op jit(solution)/shard_map/states1/pallas_call | solution.py:325
  152.6 1.9 %all-to-all-done.5.refs_0_.refs_1_.dx_ref.misc_ref = bf16[16,112,256]{2,1,0:T(8,128)(2,1)S(1)} async-done(((bf16[16,112,256]{2,1,0:T(8,128)(2,1)}), bf16[16,112,256]{2,1,0:T(8,128)(2,1)S(1)}, u32[]{:S(2)}, u32[]{:S(2)}) %all-to-all-start.5) | async-done | bytes 917536 | tf_op jit(solution)/shard_map/all_to_all | solution.py:490
  154.5 0.2 update_last.1
  154.7 7.7 %collective-permute-start.1 = (bf16[64,256]{1,0:T(8,128)(2,1)S(1)}, bf16[64,256]{1,0:T(8,128)(2,1)S(1)}, u32[]{:S(2)}, u32[]{:S(2)}) collective-permute-start(bf16[64,256]{1,0:T(8,128)(2,1)S(1)} %update_last.1), channel_id=1, source_target_pairs={{0,0},{8,1},{16,2},{24,3},{32,4},{40,5},{48,6},{56,7},{64,8},{72,9... | collective-permute-start | bytes 98312 | tf_op jit(solution)/shard_map/ppermute | solution.py:564
  162.4 4.5 %owned1.1 = bf16[2,2,64,64,128]{4,3,2,1,0:T(8,128)(2,1)} custom-call(bf16[16,2,4,64,128]{4,3,2,1,0:T(8,128)(2,1)} %all-to-all-done.4.starts_ref, bf16[16,112,256]{2,1,0:T(8,128)(2,1)S(1)} %all-to-all-done.5.refs_0_.refs_1_.dx_ref.misc_ref, bf16[16,112,256]{2,1,0:T(8,128)(2,1)S(1)} %all-to-all-done.5.refs_0_.refs_1_.dx_ref.misc_ref, ...), custom_call_target="tpu_custom_call", output_to_operand_aliasing={{}: (3, {})} | custom-call | tf_op jit(solution)/shard_map/owned1/pallas_call | solution.py:426
  167.0 0.6 copy.40
  (28 shorter events, 0.1 us)
Async XLA Ops:
  7.2 19.8 %copy-start.11 = (s32[4,2]{0,1:T(2,128)S(1)}, s32[4,2]{0,1:T(2,128)}, u32[]{:S(2)}) copy-start(s32[4,2]{0,1:T(2,128)} %param.35) | copy-start | bytes 100
  7.2 20.0 %copy-start.16 = (s32[8]{0:T(128)S(1)}, s32[8]{0:T(128)}, u32[]{:S(2)}) copy-start(s32[8]{0:T(128)} %param.34) | copy-start | bytes 100
  7.2 20.0 %copy-start.15 = (s32[8]{0:T(128)S(1)}, s32[8]{0:T(128)}, u32[]{:S(2)}) copy-start(s32[8]{0:T(128)} %param.33) | copy-start | bytes 100
  7.2 46.5 %all-gather.5.cloned.1.call-start = ((), (), s32[]{:S(2)}) async-start(), calls=%async_computation.6 | async-start | bytes 5308416 | tf_op jit(solution)/shard_map/all_gather | solution.py:538
  7.2 8.4 %collective-permute-start = (bf16[64,256]{1,0:T(8,128)(2,1)}, bf16[64,256]{1,0:T(8,128)(2,1)S(1)}, u32[]{:S(2)}, u32[]{:S(2)}) collective-permute-start(bf16[64,256]{1,0:T(8,128)(2,1)} %param.18), channel_id=1, source_target_pairs={{0,0},{1,8},{2,16},{3,24},{4,32},{5,40},{6,48},{7,56},{8,64},{9,72... | collective-permute-start | bytes 98312 | tf_op jit(solution)/shard_map/ppermute | solution.py:529
  16.5 18.8 %all-to-all-start = ((bf16[16,64,256]{2,1,0:T(8,128)(2,1)}), bf16[16,64,256]{2,1,0:T(8,128)(2,1)S(1)}, u32[]{:S(2)}, u32[]{:S(2)}) async-start(bf16[16,64,256]{2,1,0:T(8,128)(2,1)} %broadcast_in_dim.4), calls=%async_computation | async-start | bytes 1048576 | tf_op jit(solution)/shard_map/all_to_all | solution.py:490
  26.9 87.6 %all-gather.7.cloned.1.call-start = ((), (), s32[]{:S(2)}) async-start(), calls=%async_computation.7 | async-start | bytes 5308416 | tf_op jit(solution)/shard_map/all_gather | solution.py:542
  33.8 10.5 %copy-start.9 = (bf16[2,8,3,256]{3,1,2,0:T(8,128)(2,1)S(1)}, bf16[2,8,3,256]{3,1,2,0:T(8,128)(2,1)}, u32[]{:S(2)}) copy-start(bf16[2,8,3,256]{3,1,2,0:T(8,128)(2,1)} %param.30) | copy-start | bytes 73732
  33.8 11.1 %copy-start.10 = (bf16[2,8,3,256]{3,1,2,0:T(8,128)(2,1)S(1)}, bf16[2,8,3,256]{3,1,2,0:T(8,128)(2,1)}, u32[]{:S(2)}) copy-start(bf16[2,8,3,256]{3,1,2,0:T(8,128)(2,1)} %param.31) | copy-start | bytes 73732
  33.8 11.7 %copy-start.12 = (f32[2,4]{1,0:T(2,128)S(1)}, f32[2,4]{1,0:T(2,128)}, u32[]{:S(2)}) copy-start(f32[2,4]{1,0:T(2,128)} %param.27) | copy-start | bytes 100
  33.8 11.7 %copy-start.13 = (f32[2,4]{1,0:T(2,128)S(1)}, f32[2,4]{1,0:T(2,128)}, u32[]{:S(2)}) copy-start(f32[2,4]{1,0:T(2,128)} %param.26) | copy-start | bytes 100
  33.8 11.7 %copy-start.14 = (f32[2,4]{1,0:T(2,128)S(1)}, f32[2,4]{1,0:T(2,128)}, u32[]{:S(2)}) copy-start(f32[2,4]{1,0:T(2,128)} %param.25) | copy-start | bytes 100
  35.4 18.3 %copy-start.8 = (bf16[16,64,256]{2,1,0:T(8,128)(2,1)}, bf16[16,64,256]{2,1,0:T(8,128)(2,1)S(1)}, u32[]{:S(2)}) copy-start(bf16[16,64,256]{2,1,0:T(8,128)(2,1)S(1)} %all-to-all-done.refs_2_) | copy-start | bytes 1572868
  37.8 32.0 %all-to-all-start.1 = ((bf16[16,2,4,64,128]{4,3,2,1,0:T(8,128)(2,1)}), bf16[16,2,4,64,128]{4,3,2,1,0:T(8,128)(2,1)}, u32[]{:S(2)}, u32[]{:S(2)}) async-start(bf16[16,2,4,64,128]{4,3,2,1,0:T(8,128)(2,1)} %starts0.1), calls=%async_computation.1 | async-start | bytes 4194304 | tf_op jit(solution)/shard_map/all_to_all | solution.py:490
  53.7 22.8 %copy-start = (f32[2,8,4,64,128]{4,3,2,1,0:T(8,128)S(1)}, f32[2,8,4,64,128]{4,3,2,1,0:T(8,128)}, u32[]{:S(2)}) copy-start(f32[2,8,4,64,128]{4,3,2,1,0:T(8,128)} %state_ref.7) | copy-start | bytes 6291460
  69.8 19.1 %all-to-all-start.2 = ((bf16[16,112,256]{2,1,0:T(8,128)(2,1)}), bf16[16,112,256]{2,1,0:T(8,128)(2,1)S(1)}, u32[]{:S(2)}, u32[]{:S(2)}) async-start(bf16[16,112,256]{2,1,0:T(8,128)(2,1)} %get-tuple-element.39), calls=%async_computation.2 | async-start | bytes 1835008 | tf_op jit(solution)/shard_map/all_to_all | solution.py:490
  76.5 1.0 copy-start.3
  77.4 0.9 copy-start.5
  78.3 0.8 copy-start.7
  103.5 31.9 %all-to-all-start.4 = ((bf16[16,2,4,64,128]{4,3,2,1,0:T(8,128)(2,1)}), bf16[16,2,4,64,128]{4,3,2,1,0:T(8,128)(2,1)}, u32[]{:S(2)}, u32[]{:S(2)}) async-start(bf16[16,2,4,64,128]{4,3,2,1,0:T(8,128)(2,1)} %starts1.1), calls=%async_computation.4 | async-start | bytes 4194304 | tf_op jit(solution)/shard_map/all_to_all | solution.py:490
  114.5 27.6 %copy-start.1 = (f32[2,8,4,64,128]{4,3,2,1,0:T(8,128)S(1)}, f32[2,8,4,64,128]{4,3,2,1,0:T(8,128)}, u32[]{:S(2)}) copy-start(f32[2,8,4,64,128]{4,3,2,1,0:T(8,128)} %state_ref.7) | copy-start | bytes 6291460
  135.4 19.2 %all-to-all-start.5 = ((bf16[16,112,256]{2,1,0:T(8,128)(2,1)}), bf16[16,112,256]{2,1,0:T(8,128)(2,1)S(1)}, u32[]{:S(2)}, u32[]{:S(2)}) async-start(bf16[16,112,256]{2,1,0:T(8,128)(2,1)} %get-tuple-element.55), calls=%async_computation.5 | async-start | bytes 1835008 | tf_op jit(solution)/shard_map/all_to_all | solution.py:490
  142.1 1.0 copy-start.2
  143.1 0.9 copy-start.4
  144.0 0.8 copy-start.6
  154.7 12.2 %collective-permute-start.1 = (bf16[64,256]{1,0:T(8,128)(2,1)S(1)}, bf16[64,256]{1,0:T(8,128)(2,1)S(1)}, u32[]{:S(2)}, u32[]{:S(2)}) collective-permute-start(bf16[64,256]{1,0:T(8,128)(2,1)S(1)} %update_last.1), channel_id=1, source_target_pairs={{0,0},{8,1},{16,2},{24,3},{32,4},{40,5},{48,6},{56,7},{64,8},{72,9... | collective-permute-start | bytes 98312 | tf_op jit(solution)/shard_map/ppermute | solution.py:564
Sparse Core Ops, SparseCore 0:
  15.8 37.8 all-gather.4
  55.4 34.2 all-gather.6

commit v5 on v4

--- a/solution.py
+++ b/solution.py
@@ -378,29 +378,31 @@
 
     @pl.when(i == 0)
     def _first():
+        b_s[...] = jnp.zeros(b_s.shape, F32)
         for slot in range(slots):
             row = 1 + 3 * slot
             for c in range(COLS):
                 lines = misc_ref[c].astype(F32)
-                b_s[slot, c : c + 1, :] = lines[row : row + 1, 0:state_size]
+                b_s[
+                    slot * S + c : slot * S + c + 1, slot * state_size : (slot + 1) * state_size
+                ] = lines[row : row + 1, 0:state_size]
                 scale_s[slot, c : c + 1, :] = (
                     lines[row + 1 : row + 2, :] + lines[row + 2 : row + 3, :]
                 )
 
+    dx = jnp.concatenate([dx_ref[g] for g in range(group)], axis=1)
+    added = lax.dot_general(
+        dx, b_s[...].astype(BF), (((0,), (0,)), ((), ())), preferred_element_type=F32
+    )
     for slot in range(slots):
-        dx = jnp.concatenate(
-            [dx_ref[g, slot * S : (slot + 1) * S, :] for g in range(group)], axis=1
-        )
-        added = lax.dot_general(
-            dx, b_s[slot].astype(BF), (((0,), (0,)), ((), ())), preferred_element_type=F32
-        )
         for g in range(group):
             scales = scale_s[slot, pl.ds(i * group + g, 1), :]
             for h in range(heads):
                 scale = scales[:, h * head_size : h * head_size + 1]
                 at = (g * heads + h) * head_size
                 out_ref[slot, g * heads + h] = (
-                    starts_ref[g, slot, h].astype(F32) * scale + added[at : at + head_size, :]
+                    starts_ref[g, slot, h].astype(F32) * scale
+                    + added[at : at + head_size, slot * state_size : (slot + 1) * state_size]
                 ).astype(BF)
 
 
@@ -436,7 +438,7 @@
             (SEND_CAP, layers, COLS * heads, head_size, state_size), BF
         ),
         scratch_shapes=[
-            pltpu.VMEM((SEND_CAP, COLS, state_size), F32),
+            pltpu.VMEM((SEND_CAP * S, SEND_CAP * state_size), F32),
             pltpu.VMEM((SEND_CAP, COLS, width), F32),
         ],
         input_output_aliases=aliases,
@@ -538,8 +540,10 @@
     weights = [lax.all_gather(first, "row", axis=0)]
     everything = swap(jnp.broadcast_to(block[None], (COLS,) + block.shape))
     sends = [starts(layer, ints, state_cache) for layer in range(layer_count)]
-    everything, sends, raw = lax.optimization_barrier((everything, sends, raw))
-    weights.append(lax.all_gather(pack(1, *raw), "row", axis=0))
+    sends, raw = lax.optimization_barrier((sends, raw))
+    second = pack(1, *raw)
+    everything, sends, second = lax.optimization_barrier((everything, sends, second))
+    weights.append(lax.all_gather(second, "row", axis=0))
     begun = swap(sends[0])
     send = sends[1]
 

time: 176 us -> 176 us (level)
  starting transfers between devices: 47.6 us -> 45.3 us
    ppermute x1, starting transfers between devices: 7.71 us -> 5.93 us  [local(): hidden = lax.ppermute(fresh[0], ('row', 'col'), back)]
  transfers between devices with their start and end apart: 9 -> 9, of which waited for: 7 -> 6; matrix products, arithmetic and copies ran while one was open for 3% -> 3% of each run, Pallas kernels for 28% -> 28%
where the time goes in v5:
time: 176 us; the launch traced here: 174 us
  Pallas kernels  48.2 us (27%)
  starting transfers between devices  45.3 us (26%)
  waiting for transfers between devices  40 us (23%)
  blocking collectives  14.5 us (8%)
  between operations  14.2 us (8%)
  local copies, waits for them, and re-layouts  10.9 us (6%)
    all_to_all x5, starting transfers between devices, swap(): return lax.all_to_all(x, 'col', 0, 0, tiled=True)  36.2 us
    all_to_all x5, waiting for transfers between devices, swap(): return lax.all_to_all(x, 'col', 0, 0, tiled=True)  30.2 us
    pallas_call x2, Pallas kernels, states(): pl.pallas_call(states_body, name='states%d' % layer, grid=(requests,), in...  15.6 us
    all_to_all x1, blocking collectives, swap(): return lax.all_to_all(x, 'col', 0, 0, tiled=True)  14.5 us
    pallas_call x2, Pallas kernels, front(): pl.pallas_call(lambda *refs: front_body(layer, *refs), name='front%d' % l...  12.8 us
    unnamed x39, local copies, waits for them, and re-layouts  9.29 us
    pallas_call x2, Pallas kernels, owned_states(): pl.pallas_call(owned_body, name='owned%d' % layer, grid=(COLS // group,),...  8.92 us
    all_gather x1, waiting for transfers between devices, local(): weights = [lax.all_gather(first, 'row', axis=0)]  8.42 us
  transfers between devices with their start and end apart: 9, of which 6 were waited for; matrix products, arithmetic and copies ran while one was open for 3% of the time, Pallas kernels for 28%

profile of v5, /device:TPU:32, one launch (start us, length us, event | category | flops | bytes accessed | tf_op | source)
XLA Modules:
  0.0 173.6 jit_solution(9675849074570744962)
XLA Ops:
  7.2 0.0 all-gather.5.cloned.1.call-start
  7.2 3.0 %collective-permute-start = (bf16[64,256]{1,0:T(8,128)(2,1)}, bf16[64,256]{1,0:T(8,128)(2,1)S(1)}, u32[]{:S(2)}, u32[]{:S(2)}) collective-permute-start(bf16[64,256]{1,0:T(8,128)(2,1)} %param.18), channel_id=1, source_target_pairs={{0,0},{1,8},{2,16},{3,24},{4,32},{5,40},{6,48},{7,56},{8,64},{9,72... | collective-permute-start | bytes 98312 | tf_op jit(solution)/shard_map/ppermute | solution.py:531
  10.3 1.9 %copy.36 = bf16[2,256,2,256]{3,1,2,0:T(8,128)(2,1)} copy(bf16[2,256,2,256]{3,2,1,0:T(2,128)(2,1)} %param.20) | data formatting | bytes 1048576 | tf_op args[2]
  12.2 2.1 %pack0.1 = bf16[256,1152]{1,0:T(8,128)(2,1)} custom-call(bf16[2,2,256,256]{3,2,1,0:T(8,128)(2,1)} %bitcast.12, bf16[2,256,256]{2,1,0:T(8,128)(2,1)} %refs_1_.2, bf16[2,4,256]{2,1,0:T(4,128)(2,1)} %bitcast.14, f32[2,256]{1,0:T(2,128)} %refs_3_.2, bf16[2,256,256]{2,1,0:T(8,128)(2,1)} %refs_4_.4), custom_call_target="tpu_custom_call" | custom-call | tf_op jit(solution)/shard_map/pack0/pallas_call | solution.py:49
  14.3 1.3 collective-permute-done.refs_2_
  15.7 0.0 all-gather.5.cloned.1.call-update
  15.7 0.9 broadcast_in_dim.4
  16.6 10.4 %all-to-all-start = ((bf16[16,64,256]{2,1,0:T(8,128)(2,1)}), bf16[16,64,256]{2,1,0:T(8,128)(2,1)S(1)}, u32[]{:S(2)}, u32[]{:S(2)}) async-start(bf16[16,64,256]{2,1,0:T(8,128)(2,1)} %broadcast_in_dim.4), calls=%async_computation | async-start | bytes 1048576 | tf_op jit(solution)/shard_map/all_to_all | solution.py:492
  26.9 0.0 all-gather.7.cloned.1.call-start
  27.0 0.1 copy.29
  27.1 0.1 reshape.18
  27.2 0.6 concatenate.6.ints_ref.refs_0_
  27.8 3.1 %starts1.1 = bf16[16,2,4,64,128]{4,3,2,1,0:T(8,128)(2,1)} custom-call(s32[26]{0:T(128)} %concatenate.6.ints_ref.refs_0_, f32[2,8,4,64,128]{4,3,2,1,0:T(8,128)} %state_ref.7), custom_call_target="tpu_custom_call" | custom-call | tf_op jit(solution)/shard_map/starts1/pallas_call | solution.py:356
  30.8 3.0 %starts0.1 = bf16[16,2,4,64,128]{4,3,2,1,0:T(8,128)(2,1)} custom-call(s32[26]{0:T(128)} %concatenate.6.ints_ref.refs_0_, f32[2,8,4,64,128]{4,3,2,1,0:T(8,128)} %state_ref.7), custom_call_target="tpu_custom_call" | custom-call | tf_op jit(solution)/shard_map/starts0/pallas_call | solution.py:356
  33.8 0.0 copy-start.14
  33.9 2.2 %pack1.1 = bf16[256,1152]{1,0:T(8,128)(2,1)} custom-call(bf16[2,2,256,256]{3,2,1,0:T(8,128)(2,1)} %bitcast.13, bf16[2,256,256]{2,1,0:T(8,128)(2,1)} %refs_1_.2, bf16[2,4,256]{2,1,0:T(4,128)(2,1)} %bitcast.15, f32[2,256]{1,0:T(2,128)} %refs_3_.2, bf16[2,256,256]{2,1,0:T(8,128)(2,1)} %refs_4_.4), custom_call_target="tpu_custom_call" | custom-call | tf_op jit(solution)/shard_map/pack1/pallas_call | solution.py:49
  36.1 0.0 all-to-all-done.refs_2_
  36.1 0.0 all-gather.7.cloned.1.call-update
  36.1 7.2 %all-to-all-start.1 = ((bf16[16,2,4,64,128]{4,3,2,1,0:T(8,128)(2,1)}), bf16[16,2,4,64,128]{4,3,2,1,0:T(8,128)(2,1)}, u32[]{:S(2)}, u32[]{:S(2)}) async-start(bf16[16,2,4,64,128]{4,3,2,1,0:T(8,128)(2,1)} %starts0.1), calls=%async_computation.1 | async-start | bytes 4194304 | tf_op jit(solution)/shard_map/all_to_all | solution.py:492
  43.4 0.6 copy.31.refs_7_
  44.0 0.6 copy.32.refs_8_
  44.6 0.6 pad_maximum_fusion.refs_1_
  45.2 8.4 %all-gather.5.cloned.1.call-done = bf16[2048,1152]{1,0:T(8,128)(2,1)} async-done(((bf16[256,1152]{1,0:T(8,128)(2,1)}), bf16[2048,1152]{1,0:T(8,128)(2,1)}) %all-gather.5.cloned.1.call-update) | async-done | bytes 4718608 | tf_op jit(solution)/shard_map/all_gather | solution.py:540
  53.6 6.4 %front0.1 = (bf16[16,112,256]{2,1,0:T(8,128)(2,1)}, f32[128,256]{1,0:T(8,128)}, f32[128,128]{1,0:T(8,128)}, f32[128,512]{1,0:T(8,128)}) custom-call(s32[26]{0:T(128)} %concatenate.6.ints_ref.refs_0_, f32[2,12]{1,0:T(2,128)} %pad_maximum_fusion.refs_1_, bf16[16,64,256]{2,1,0:T(8,128)(2,1)} %copy-done.8, bf16[8,256,1152]{2,1,0:T(8,128)(2,1)} %bitcast.10, ...), custom_call_target="tpu_custom_call" | custom-call | tf_op jit(solution)/shard_map/front0/pallas_call | solution.py:266
  60.1 9.9 %all-to-all-done.1.starts_ref = bf16[16,2,4,64,128]{4,3,2,1,0:T(8,128)(2,1)} async-done(((bf16[16,2,4,64,128]{4,3,2,1,0:T(8,128)(2,1)}), bf16[16,2,4,64,128]{4,3,2,1,0:T(8,128)(2,1)}, u32[]{:S(2)}, u32[]{:S(2)}) %all-to-all-start.1) | async-done | bytes 2097184 | tf_op jit(solution)/shard_map/all_to_all | solution.py:492
  70.0 5.9 %all-to-all-start.2 = ((bf16[16,112,256]{2,1,0:T(8,128)(2,1)}), bf16[16,112,256]{2,1,0:T(8,128)(2,1)S(1)}, u32[]{:S(2)}, u32[]{:S(2)}) async-start(bf16[16,112,256]{2,1,0:T(8,128)(2,1)} %get-tuple-element.49), calls=%async_computation.2 | async-start | bytes 1835008 | tf_op jit(solution)/shard_map/all_to_all | solution.py:492
  75.8 0.0 copy-start.3
  75.8 0.9 copy-done.3
  76.8 0.9 copy-done.5
  77.7 0.8 copy-done.7
  78.5 7.8 %states0.1.rest_0_ = bf16[2,8,16,4,64,128]{5,4,3,2,1,0:T(8,128)(2,1)} custom-call(f32[128,256]{1,0:T(8,128)S(1)} %copy-done.5, f32[128,128]{1,0:T(8,128)S(1)} %copy-done.7, f32[128,512]{1,0:T(8,128)S(1)} %copy-done.3, f32[2,8,4,64,128]{4,3,2,1,0:T(8,128)S(1)} %copy-done), custom_call_target="tpu_custom_call" | custom-call | tf_op jit(solution)/shard_map/states0/pallas_call | solution.py:325
  86.3 2.3 %all-to-all-done.2.refs_0_.refs_1_.dx_ref.misc_ref = bf16[16,112,256]{2,1,0:T(8,128)(2,1)S(1)} async-done(((bf16[16,112,256]{2,1,0:T(8,128)(2,1)}), bf16[16,112,256]{2,1,0:T(8,128)(2,1)S(1)}, u32[]{:S(2)}, u32[]{:S(2)}) %all-to-all-start.2) | async-done | bytes 917536 | tf_op jit(solution)/shard_map/all_to_all | solution.py:492
  88.6 0.2 update_spread.1
  88.9 14.5 %all_to_all.30.refs_2_ = bf16[16,64,256]{2,1,0:T(8,128)(2,1)} all-to-all(bf16[16,64,256]{2,1,0:T(8,128)(2,1)S(1)} %get-tuple-element.54), channel_id=1, replica_groups=mesh['row'=8,'col'=16] {'col'}, dimensions={0} | all-to-all | bytes 1048576 | tf_op jit(solution)/shard_map/all_to_all | solution.py:492
  103.3 6.7 %all-to-all-start.4 = ((bf16[16,2,4,64,128]{4,3,2,1,0:T(8,128)(2,1)}), bf16[16,2,4,64,128]{4,3,2,1,0:T(8,128)(2,1)}, u32[]{:S(2)}, u32[]{:S(2)}) async-start(bf16[16,2,4,64,128]{4,3,2,1,0:T(8,128)(2,1)} %starts1.1), calls=%async_computation.4 | async-start | bytes 4194304 | tf_op jit(solution)/shard_map/all_to_all | solution.py:492
  110.0 4.5 %owned0.1.rest_0_ = bf16[2,2,64,64,128]{4,3,2,1,0:T(8,128)(2,1)} custom-call(bf16[16,2,4,64,128]{4,3,2,1,0:T(8,128)(2,1)} %all-to-all-done.1.starts_ref, bf16[16,112,256]{2,1,0:T(8,128)(2,1)S(1)} %all-to-all-done.2.refs_0_.refs_1_.dx_ref.misc_ref, bf16[16,112,256]{2,1,0:T(8,128)(2,1)S(1)} %all-to-all-done.2.refs_0_.refs_1_.dx_ref.misc_ref), custom_call_target="tpu_custom_call" | custom-call | tf_op jit(solution)/shard_map/owned0/pallas_call | solution.py:428
  114.5 6.4 %front1.1 = (bf16[16,112,256]{2,1,0:T(8,128)(2,1)}, f32[128,256]{1,0:T(8,128)}, f32[128,128]{1,0:T(8,128)}, f32[128,512]{1,0:T(8,128)}) custom-call(s32[26]{0:T(128)} %concatenate.6.ints_ref.refs_0_, f32[2,12]{1,0:T(2,128)} %pad_maximum_fusion.refs_1_, bf16[16,64,256]{2,1,0:T(8,128)(2,1)} %all_to_all.30.refs_2_, bf16[8,256,1152]{2,1,0:T(8,128)(2,1)} %bitcast.11, ...), custom_call_target="tpu_custom_call" | custom-call | tf_op jit(solution)/shard_map/front1/pallas_call | solution.py:266
  120.9 15.7 %all-to-all-done.4.starts_ref = bf16[16,2,4,64,128]{4,3,2,1,0:T(8,128)(2,1)} async-done(((bf16[16,2,4,64,128]{4,3,2,1,0:T(8,128)(2,1)}), bf16[16,2,4,64,128]{4,3,2,1,0:T(8,128)(2,1)}, u32[]{:S(2)}, u32[]{:S(2)}) %all-to-all-start.4) | async-done | bytes 2097184 | tf_op jit(solution)/shard_map/all_to_all | solution.py:492
  136.6 6.1 %all-to-all-start.5 = ((bf16[16,112,256]{2,1,0:T(8,128)(2,1)}), bf16[16,112,256]{2,1,0:T(8,128)(2,1)S(1)}, u32[]{:S(2)}, u32[]{:S(2)}) async-start(bf16[16,112,256]{2,1,0:T(8,128)(2,1)} %get-tuple-element.61), calls=%async_computation.5 | async-start | bytes 1835008 | tf_op jit(solution)/shard_map/all_to_all | solution.py:492
  142.7 0.9 copy-done.2
  143.6 0.9 copy-done.4
  144.5 0.8 copy-done.6
  145.4 7.8 %states1.1 = bf16[2,8,16,4,64,128]{5,4,3,2,1,0:T(8,128)(2,1)} custom-call(f32[128,256]{1,0:T(8,128)S(1)} %copy-done.4, f32[128,128]{1,0:T(8,128)S(1)} %copy-done.6, f32[128,512]{1,0:T(8,128)S(1)} %copy-done.2, f32[2,8,4,64,128]{4,3,2,1,0:T(8,128)S(1)} %copy-done.1, bf16[2,8,16,4,64,128]{5,4,3,2,1,0:T(8,128)(2,1)} %states0.1.rest_0_), custom_call_target="tpu_custom_call", output_to_operand_aliasing={{}: (4, {})} | custom-call | tf_op jit(solution)/shard_map/states1/pallas_call | solution.py:325
  153.2 2.4 %all-to-all-done.5.refs_0_.refs_1_.dx_ref.misc_ref = bf16[16,112,256]{2,1,0:T(8,128)(2,1)S(1)} async-done(((bf16[16,112,256]{2,1,0:T(8,128)(2,1)}), bf16[16,112,256]{2,1,0:T(8,128)(2,1)S(1)}, u32[]{:S(2)}, u32[]{:S(2)}) %all-to-all-start.5) | async-done | bytes 917536 | tf_op jit(solution)/shard_map/all_to_all | solution.py:492
  155.5 0.2 update_last.1
  155.7 5.9 %collective-permute-start.1 = (bf16[64,256]{1,0:T(8,128)(2,1)S(1)}, bf16[64,256]{1,0:T(8,128)(2,1)S(1)}, u32[]{:S(2)}, u32[]{:S(2)}) collective-permute-start(bf16[64,256]{1,0:T(8,128)(2,1)S(1)} %update_last.1), channel_id=1, source_target_pairs={{0,0},{8,1},{16,2},{24,3},{32,4},{40,5},{48,6},{56,7},{64,8},{72,9... | collective-permute-start | bytes 98312 | tf_op jit(solution)/shard_map/ppermute | solution.py:568
  161.6 4.5 %owned1.1 = bf16[2,2,64,64,128]{4,3,2,1,0:T(8,128)(2,1)} custom-call(bf16[16,2,4,64,128]{4,3,2,1,0:T(8,128)(2,1)} %all-to-all-done.4.starts_ref, bf16[16,112,256]{2,1,0:T(8,128)(2,1)S(1)} %all-to-all-done.5.refs_0_.refs_1_.dx_ref.misc_ref, bf16[16,112,256]{2,1,0:T(8,128)(2,1)S(1)} %all-to-all-done.5.refs_0_.refs_1_.dx_ref.misc_ref, ...), custom_call_target="tpu_custom_call", output_to_operand_aliasing={{}: (3, {})} | custom-call | tf_op jit(solution)/shard_map/owned1/pallas_call | solution.py:428
  166.1 0.6 copy.40
  (28 shorter events, 0.1 us)
Async XLA Ops:
  7.2 19.8 %copy-start.11 = (s32[4,2]{0,1:T(2,128)S(1)}, s32[4,2]{0,1:T(2,128)}, u32[]{:S(2)}) copy-start(s32[4,2]{0,1:T(2,128)} %param.35) | copy-start | bytes 100
  7.2 20.0 %copy-start.16 = (s32[8]{0:T(128)S(1)}, s32[8]{0:T(128)}, u32[]{:S(2)}) copy-start(s32[8]{0:T(128)} %param.34) | copy-start | bytes 100
  7.2 20.0 %copy-start.15 = (s32[8]{0:T(128)S(1)}, s32[8]{0:T(128)}, u32[]{:S(2)}) copy-start(s32[8]{0:T(128)} %param.33) | copy-start | bytes 100
  7.2 46.4 %all-gather.5.cloned.1.call-start = ((), (), s32[]{:S(2)}) async-start(), calls=%async_computation.6 | async-start | bytes 5308416 | tf_op jit(solution)/shard_map/all_gather | solution.py:540
  7.2 8.4 %collective-permute-start = (bf16[64,256]{1,0:T(8,128)(2,1)}, bf16[64,256]{1,0:T(8,128)(2,1)S(1)}, u32[]{:S(2)}, u32[]{:S(2)}) collective-permute-start(bf16[64,256]{1,0:T(8,128)(2,1)} %param.18), channel_id=1, source_target_pairs={{0,0},{1,8},{2,16},{3,24},{4,32},{5,40},{6,48},{7,56},{8,64},{9,72... | collective-permute-start | bytes 98312 | tf_op jit(solution)/shard_map/ppermute | solution.py:531
  16.6 19.5 %all-to-all-start = ((bf16[16,64,256]{2,1,0:T(8,128)(2,1)}), bf16[16,64,256]{2,1,0:T(8,128)(2,1)S(1)}, u32[]{:S(2)}, u32[]{:S(2)}) async-start(bf16[16,64,256]{2,1,0:T(8,128)(2,1)} %broadcast_in_dim.4), calls=%async_computation | async-start | bytes 1048576 | tf_op jit(solution)/shard_map/all_to_all | solution.py:492
  26.9 87.6 %all-gather.7.cloned.1.call-start = ((), (), s32[]{:S(2)}) async-start(), calls=%async_computation.7 | async-start | bytes 5308416 | tf_op jit(solution)/shard_map/all_gather | solution.py:546
  33.8 9.5 %copy-start.9 = (bf16[2,8,3,256]{3,1,2,0:T(8,128)(2,1)S(1)}, bf16[2,8,3,256]{3,1,2,0:T(8,128)(2,1)}, u32[]{:S(2)}) copy-start(bf16[2,8,3,256]{3,1,2,0:T(8,128)(2,1)} %param.30) | copy-start | bytes 73732
  33.8 10.2 %copy-start.10 = (bf16[2,8,3,256]{3,1,2,0:T(8,128)(2,1)S(1)}, bf16[2,8,3,256]{3,1,2,0:T(8,128)(2,1)}, u32[]{:S(2)}) copy-start(bf16[2,8,3,256]{3,1,2,0:T(8,128)(2,1)} %param.31) | copy-start | bytes 73732
  33.8 10.8 %copy-start.12 = (f32[2,4]{1,0:T(2,128)S(1)}, f32[2,4]{1,0:T(2,128)}, u32[]{:S(2)}) copy-start(f32[2,4]{1,0:T(2,128)} %param.27) | copy-start | bytes 100
  33.8 10.8 %copy-start.13 = (f32[2,4]{1,0:T(2,128)S(1)}, f32[2,4]{1,0:T(2,128)}, u32[]{:S(2)}) copy-start(f32[2,4]{1,0:T(2,128)} %param.26) | copy-start | bytes 100
  33.8 10.8 %copy-start.14 = (f32[2,4]{1,0:T(2,128)S(1)}, f32[2,4]{1,0:T(2,128)}, u32[]{:S(2)}) copy-start(f32[2,4]{1,0:T(2,128)} %param.25) | copy-start | bytes 100
  36.1 17.6 %copy-start.8 = (bf16[16,64,256]{2,1,0:T(8,128)(2,1)}, bf16[16,64,256]{2,1,0:T(8,128)(2,1)S(1)}, u32[]{:S(2)}) copy-start(bf16[16,64,256]{2,1,0:T(8,128)(2,1)S(1)} %all-to-all-done.refs_2_) | copy-start | bytes 1572868
  36.1 33.9 %all-to-all-start.1 = ((bf16[16,2,4,64,128]{4,3,2,1,0:T(8,128)(2,1)}), bf16[16,2,4,64,128]{4,3,2,1,0:T(8,128)(2,1)}, u32[]{:S(2)}, u32[]{:S(2)}) async-start(bf16[16,2,4,64,128]{4,3,2,1,0:T(8,128)(2,1)} %starts0.1), calls=%async_computation.1 | async-start | bytes 4194304 | tf_op jit(solution)/shard_map/all_to_all | solution.py:492
  53.6 22.2 %copy-start = (f32[2,8,4,64,128]{4,3,2,1,0:T(8,128)S(1)}, f32[2,8,4,64,128]{4,3,2,1,0:T(8,128)}, u32[]{:S(2)}) copy-start(f32[2,8,4,64,128]{4,3,2,1,0:T(8,128)} %state_ref.7) | copy-start | bytes 6291460
  70.0 18.7 %all-to-all-start.2 = ((bf16[16,112,256]{2,1,0:T(8,128)(2,1)}), bf16[16,112,256]{2,1,0:T(8,128)(2,1)S(1)}, u32[]{:S(2)}, u32[]{:S(2)}) async-start(bf16[16,112,256]{2,1,0:T(8,128)(2,1)} %get-tuple-element.49), calls=%async_computation.2 | async-start | bytes 1835008 | tf_op jit(solution)/shard_map/all_to_all | solution.py:492
  75.8 1.0 copy-start.3
  76.8 0.9 copy-start.5
  77.7 0.8 copy-start.7
  103.3 33.2 %all-to-all-start.4 = ((bf16[16,2,4,64,128]{4,3,2,1,0:T(8,128)(2,1)}), bf16[16,2,4,64,128]{4,3,2,1,0:T(8,128)(2,1)}, u32[]{:S(2)}, u32[]{:S(2)}) async-start(bf16[16,2,4,64,128]{4,3,2,1,0:T(8,128)(2,1)} %starts1.1), calls=%async_computation.4 | async-start | bytes 4194304 | tf_op jit(solution)/shard_map/all_to_all | solution.py:492
  114.5 28.2 %copy-start.1 = (f32[2,8,4,64,128]{4,3,2,1,0:T(8,128)S(1)}, f32[2,8,4,64,128]{4,3,2,1,0:T(8,128)}, u32[]{:S(2)}) copy-start(f32[2,8,4,64,128]{4,3,2,1,0:T(8,128)} %state_ref.7) | copy-start | bytes 6291460
  136.6 18.9 %all-to-all-start.5 = ((bf16[16,112,256]{2,1,0:T(8,128)(2,1)}), bf16[16,112,256]{2,1,0:T(8,128)(2,1)S(1)}, u32[]{:S(2)}, u32[]{:S(2)}) async-start(bf16[16,112,256]{2,1,0:T(8,128)(2,1)} %get-tuple-element.61), calls=%async_computation.5 | async-start | bytes 1835008 | tf_op jit(solution)/shard_map/all_to_all | solution.py:492
  142.7 1.0 copy-start.2
  143.6 0.9 copy-start.4
  144.5 0.8 copy-start.6
  155.7 10.4 %collective-permute-start.1 = (bf16[64,256]{1,0:T(8,128)(2,1)S(1)}, bf16[64,256]{1,0:T(8,128)(2,1)S(1)}, u32[]{:S(2)}, u32[]{:S(2)}) collective-permute-start(bf16[64,256]{1,0:T(8,128)(2,1)S(1)} %update_last.1), channel_id=1, source_target_pairs={{0,0},{8,1},{16,2},{24,3},{32,4},{40,5},{48,6},{56,7},{64,8},{72,9... | collective-permute-start | bytes 98312 | tf_op jit(solution)/shard_map/ppermute | solution.py:568
Sparse Core Ops, SparseCore 0:
  15.8 37.7 all-gather.4
  55.3 34.2 all-gather.6

commit v6 on v5

--- a/solution.py
+++ b/solution.py
@@ -369,82 +369,80 @@
     )(ints, state)
 
 
-def owned_body(starts_ref, dx_ref, misc_ref, *rest):
-    out_ref, b_s, scale_s = rest[-3:]
-    i = pl.program_id(0)
-    group = starts_ref.shape[0]
-    slots, group_heads, head_size, state_size = out_ref.shape
-    heads = group_heads // group
-
-    @pl.when(i == 0)
-    def _first():
-        b_s[...] = jnp.zeros(b_s.shape, F32)
+def owned_body(layer, starts_ref, received_ref, *rest):
+    out_ref, stage, b_s, sems = rest[-4:]
+    cols, slots, heads, head_size, state_size = starts_ref.shape
+    group = 4
+    dx_rows = slots * S
+    misc_at = received_ref.shape[1] - SUM_ROWS
+    dx_at = misc_at - dx_rows
+    b_s[...] = jnp.zeros(b_s.shape, F32)
+    scales = []
+    for c in range(cols):
+        lines = received_ref[c, misc_at:, :].astype(F32)
         for slot in range(slots):
             row = 1 + 3 * slot
-            for c in range(COLS):
-                lines = misc_ref[c].astype(F32)
-                b_s[
-                    slot * S + c : slot * S + c + 1, slot * state_size : (slot + 1) * state_size
-                ] = lines[row : row + 1, 0:state_size]
-                scale_s[slot, c : c + 1, :] = (
-                    lines[row + 1 : row + 2, :] + lines[row + 2 : row + 3, :]
+            b_s[
+                slot * S + c : slot * S + c + 1, slot * state_size : (slot + 1) * state_size
+            ] = lines[row : row + 1, 0:state_size]
+            scales.append(lines[row + 1 : row + 2, :] + lines[row + 2 : row + 3, :])
+    b_all = b_s[...].astype(BF)
+    copies = []
+    for i in range(cols // group):
+        dx = jnp.concatenate(
+            [received_ref[i * group + g, dx_at:misc_at, :] for g in range(group)], axis=1
+        )
+        added = lax.dot_general(dx, b_all, (((0,), (0,)), ((), ())), preferred_element_type=F32)
+        for slot in range(slots):
+            for g in range(group):
+                c = i * group + g
+                for h in range(heads):
+                    scale = scales[c * slots + slot][:, h * head_size : h * head_size + 1]
+                    at = (g * heads + h) * head_size
+                    stage[slot, c * heads + h] = (
+                        starts_ref[c, slot, h].astype(F32) * scale
+                        + added[at : at + head_size, slot * state_size : (slot + 1) * state_size]
+                    ).astype(BF)
+            span = pl.ds(i * group * heads, group * heads)
+            copies.append(
+                pltpu.make_async_copy(
+                    stage.at[slot, span],
+                    out_ref.at[slot, layer, span],
+                    sems.at[i * slots + slot],
                 )
-
-    dx = jnp.concatenate([dx_ref[g] for g in range(group)], axis=1)
-    added = lax.dot_general(
-        dx, b_s[...].astype(BF), (((0,), (0,)), ((), ())), preferred_element_type=F32
-    )
-    for slot in range(slots):
-        for g in range(group):
-            scales = scale_s[slot, pl.ds(i * group + g, 1), :]
-            for h in range(heads):
-                scale = scales[:, h * head_size : h * head_size + 1]
-                at = (g * heads + h) * head_size
-                out_ref[slot, g * heads + h] = (
-                    starts_ref[g, slot, h].astype(F32) * scale
-                    + added[at : at + head_size, slot * state_size : (slot + 1) * state_size]
-                ).astype(BF)
+            )
+            copies[-1].start()
+    for copy in copies:
+        copy.wait()
 
 
 def owned_states(layer, state, begun, received, previous):
     layers, _, heads, head_size, state_size = state.shape
-    group = 4
-    width = received.shape[2]
-    dx_rows = SEND_CAP * S
-    block_tokens = received.shape[1] - dx_rows - SUM_ROWS
-    dx_at = block_tokens // dx_rows
-    misc_at = (block_tokens + dx_rows) // SUM_ROWS
-    in_specs = [
-        pl.BlockSpec((group,) + begun.shape[1:], lambda i: (i, 0, 0, 0, 0)),
-        pl.BlockSpec((group, dx_rows, width), lambda i: (i, dx_at, 0)),
-        pl.BlockSpec((COLS, SUM_ROWS, width), lambda i: (0, misc_at, 0)),
-    ]
-    operands = [begun, received, received]
+    resident = pl.BlockSpec(memory_space=pltpu.VMEM)
+    anywhere = pl.BlockSpec(memory_space=pl.ANY)
+    in_specs = [resident, resident]
+    operands = [begun, received]
     aliases = {}
     if previous is not None:
-        in_specs.append(pl.BlockSpec(memory_space=pl.ANY))
+        in_specs.append(anywhere)
         aliases = {len(operands): 0}
         operands.append(previous)
+    all_heads = COLS * heads
     return pl.pallas_call(
-        owned_body,
+        lambda *refs: owned_body(layer, *refs),
         name="owned%d" % layer,
-        grid=(COLS // group,),
         in_specs=in_specs,
-        out_specs=pl.BlockSpec(
-            (SEND_CAP, None, group * heads, head_size, state_size),
-            lambda i: (0, layer, i, 0, 0),
-        ),
+        out_specs=anywhere,
         out_shape=jax.ShapeDtypeStruct(
-            (SEND_CAP, layers, COLS * heads, head_size, state_size), BF
+            (SEND_CAP, layers, all_heads, head_size, state_size), BF
         ),
         scratch_shapes=[
+            pltpu.VMEM((SEND_CAP, all_heads, head_size, state_size), BF),
             pltpu.VMEM((SEND_CAP * S, SEND_CAP * state_size), F32),
-            pltpu.VMEM((SEND_CAP, COLS, width), F32),
+            pltpu.SemaphoreType.DMA((SEND_CAP * COLS // 4,)),
         ],
         input_output_aliases=aliases,
-        compiler_params=pltpu.CompilerParams(
-            dimension_semantics=("arbitrary",), vmem_limit_bytes=SMALL_VMEM_BYTES
-        ),
+        compiler_params=pltpu.CompilerParams(vmem_limit_bytes=SMALL_VMEM_BYTES),
     )(*operands)
 
 

time: 176 us -> 176 us (level)
  transfers between devices with their start and end apart: 9 -> 9, of which waited for: 6 -> 6; matrix products, arithmetic and copies ran while one was open for 3% -> 3% of each run, Pallas kernels for 28% -> 27%
where the time goes in v6:
time: 176 us; the launch traced here: 173 us
  Pallas kernels  46.7 us (27%)
  starting transfers between devices  45.4 us (26%)
  waiting for transfers between devices  40.5 us (23%)
  blocking collectives  14.5 us (8%)
  between operations  14.2 us (8%)
  local copies, waits for them, and re-layouts  10.9 us (6%)
    all_to_all x5, starting transfers between devices, swap(): return lax.all_to_all(x, 'col', 0, 0, tiled=True)  36.2 us
    all_to_all x5, waiting for transfers between devices, swap(): return lax.all_to_all(x, 'col', 0, 0, tiled=True)  30.7 us
    pallas_call x2, Pallas kernels, states(): pl.pallas_call(states_body, name='states%d' % layer, grid=(requests,), in...  15.6 us
    all_to_all x1, blocking collectives, swap(): return lax.all_to_all(x, 'col', 0, 0, tiled=True)  14.5 us
    pallas_call x2, Pallas kernels, front(): pl.pallas_call(lambda *refs: front_body(layer, *refs), name='front%d' % l...  12.8 us
    unnamed x39, local copies, waits for them, and re-layouts  9.29 us
    all_gather x1, waiting for transfers between devices, local(): weights = [lax.all_gather(first, 'row', axis=0)]  8.46 us
    pallas_call x2, Pallas kernels, owned_states(): pl.pallas_call(lambda *refs: owned_body(layer, *refs), name='owned%d' % l...  7.44 us
  transfers between devices with their start and end apart: 9, of which 6 were waited for; matrix products, arithmetic and copies ran while one was open for 3% of the time, Pallas kernels for 27%

profile of v6, /device:TPU:32, one launch (start us, length us, event | category | flops | bytes accessed | tf_op | source)
XLA Modules:
  0.0 172.8 jit_solution(9543821502793602055)
XLA Ops:
  7.2 0.0 all-gather.5.cloned.1.call-start
  7.2 3.0 %collective-permute-start = (bf16[64,256]{1,0:T(8,128)(2,1)}, bf16[64,256]{1,0:T(8,128)(2,1)S(1)}, u32[]{:S(2)}, u32[]{:S(2)}) collective-permute-start(bf16[64,256]{1,0:T(8,128)(2,1)} %param.18), channel_id=1, source_target_pairs={{0,0},{1,8},{2,16},{3,24},{4,32},{5,40},{6,48},{7,56},{8,64},{9,72... | collective-permute-start | bytes 98312 | tf_op jit(solution)/shard_map/ppermute | solution.py:529
  10.3 1.9 %copy.36 = bf16[2,256,2,256]{3,1,2,0:T(8,128)(2,1)} copy(bf16[2,256,2,256]{3,2,1,0:T(2,128)(2,1)} %param.20) | data formatting | bytes 1048576 | tf_op args[2]
  12.2 2.1 %pack0.1 = bf16[256,1152]{1,0:T(8,128)(2,1)} custom-call(bf16[2,2,256,256]{3,2,1,0:T(8,128)(2,1)} %bitcast.12, bf16[2,256,256]{2,1,0:T(8,128)(2,1)} %refs_1_.2, bf16[2,4,256]{2,1,0:T(4,128)(2,1)} %bitcast.14, f32[2,256]{1,0:T(2,128)} %refs_3_.2, bf16[2,256,256]{2,1,0:T(8,128)(2,1)} %refs_4_.4), custom_call_target="tpu_custom_call" | custom-call | tf_op jit(solution)/shard_map/pack0/pallas_call | solution.py:49
  14.3 1.3 collective-permute-done.refs_2_
  15.7 0.0 all-gather.5.cloned.1.call-update
  15.7 0.9 broadcast_in_dim.4
  16.6 10.4 %all-to-all-start = ((bf16[16,64,256]{2,1,0:T(8,128)(2,1)}), bf16[16,64,256]{2,1,0:T(8,128)(2,1)S(1)}, u32[]{:S(2)}, u32[]{:S(2)}) async-start(bf16[16,64,256]{2,1,0:T(8,128)(2,1)} %broadcast_in_dim.4), calls=%async_computation | async-start | bytes 1048576 | tf_op jit(solution)/shard_map/all_to_all | solution.py:490
  26.9 0.0 all-gather.7.cloned.1.call-start
  27.0 0.1 copy.29
  27.1 0.1 reshape.18
  27.2 0.6 concatenate.6.ints_ref.refs_0_
  27.8 3.0 %starts1.1 = bf16[16,2,4,64,128]{4,3,2,1,0:T(8,128)(2,1)} custom-call(s32[26]{0:T(128)} %concatenate.6.ints_ref.refs_0_, f32[2,8,4,64,128]{4,3,2,1,0:T(8,128)} %state_ref.7), custom_call_target="tpu_custom_call" | custom-call | tf_op jit(solution)/shard_map/starts1/pallas_call | solution.py:356
  30.8 3.0 %starts0.1 = bf16[16,2,4,64,128]{4,3,2,1,0:T(8,128)(2,1)} custom-call(s32[26]{0:T(128)} %concatenate.6.ints_ref.refs_0_, f32[2,8,4,64,128]{4,3,2,1,0:T(8,128)} %state_ref.7), custom_call_target="tpu_custom_call" | custom-call | tf_op jit(solution)/shard_map/starts0/pallas_call | solution.py:356
  33.8 0.0 copy-start.14
  33.8 2.2 %pack1.1 = bf16[256,1152]{1,0:T(8,128)(2,1)} custom-call(bf16[2,2,256,256]{3,2,1,0:T(8,128)(2,1)} %bitcast.13, bf16[2,256,256]{2,1,0:T(8,128)(2,1)} %refs_1_.2, bf16[2,4,256]{2,1,0:T(4,128)(2,1)} %bitcast.15, f32[2,256]{1,0:T(2,128)} %refs_3_.2, bf16[2,256,256]{2,1,0:T(8,128)(2,1)} %refs_4_.4), custom_call_target="tpu_custom_call" | custom-call | tf_op jit(solution)/shard_map/pack1/pallas_call | solution.py:49
  36.0 0.0 all-gather.7.cloned.1.call-update
  36.1 7.2 %all-to-all-start.1 = ((bf16[16,2,4,64,128]{4,3,2,1,0:T(8,128)(2,1)}), bf16[16,2,4,64,128]{4,3,2,1,0:T(8,128)(2,1)}, u32[]{:S(2)}, u32[]{:S(2)}) async-start(bf16[16,2,4,64,128]{4,3,2,1,0:T(8,128)(2,1)} %starts0.1), calls=%async_computation.1 | async-start | bytes 4194304 | tf_op jit(solution)/shard_map/all_to_all | solution.py:490
  43.3 0.6 copy.31.refs_7_
  43.9 0.6 copy.32.refs_8_
  44.6 0.6 pad_maximum_fusion.refs_1_
  45.2 8.5 %all-gather.5.cloned.1.call-done = bf16[2048,1152]{1,0:T(8,128)(2,1)} async-done(((bf16[256,1152]{1,0:T(8,128)(2,1)}), bf16[2048,1152]{1,0:T(8,128)(2,1)}) %all-gather.5.cloned.1.call-update) | async-done | bytes 4718608 | tf_op jit(solution)/shard_map/all_gather | solution.py:538
  53.6 6.4 %front0.1 = (bf16[16,112,256]{2,1,0:T(8,128)(2,1)}, f32[128,256]{1,0:T(8,128)}, f32[128,128]{1,0:T(8,128)}, f32[128,512]{1,0:T(8,128)}) custom-call(s32[26]{0:T(128)} %concatenate.6.ints_ref.refs_0_, f32[2,12]{1,0:T(2,128)} %pad_maximum_fusion.refs_1_, bf16[16,64,256]{2,1,0:T(8,128)(2,1)} %copy-done.8, bf16[8,256,1152]{2,1,0:T(8,128)(2,1)} %bitcast.10, ...), custom_call_target="tpu_custom_call" | custom-call | tf_op jit(solution)/shard_map/front0/pallas_call | solution.py:266
  60.0 10.1 %all-to-all-done.1.refs_0_ = bf16[16,2,4,64,128]{4,3,2,1,0:T(8,128)(2,1)} async-done(((bf16[16,2,4,64,128]{4,3,2,1,0:T(8,128)(2,1)}), bf16[16,2,4,64,128]{4,3,2,1,0:T(8,128)(2,1)}, u32[]{:S(2)}, u32[]{:S(2)}) %all-to-all-start.1) | async-done | bytes 2097184 | tf_op jit(solution)/shard_map/all_to_all | solution.py:490
  70.1 5.8 %all-to-all-start.2 = ((bf16[16,112,256]{2,1,0:T(8,128)(2,1)}), bf16[16,112,256]{2,1,0:T(8,128)(2,1)S(1)}, u32[]{:S(2)}, u32[]{:S(2)}) async-start(bf16[16,112,256]{2,1,0:T(8,128)(2,1)} %get-tuple-element.49), calls=%async_computation.2 | async-start | bytes 1835008 | tf_op jit(solution)/shard_map/all_to_all | solution.py:490
  75.9 0.0 copy-start.3
  75.9 0.9 copy-done.3
  76.8 0.9 copy-done.5
  77.7 0.8 copy-done.7
  78.6 7.8 %states0.1.rest_0_ = bf16[2,8,16,4,64,128]{5,4,3,2,1,0:T(8,128)(2,1)} custom-call(f32[128,256]{1,0:T(8,128)S(1)} %copy-done.5, f32[128,128]{1,0:T(8,128)S(1)} %copy-done.7, f32[128,512]{1,0:T(8,128)S(1)} %copy-done.3, f32[2,8,4,64,128]{4,3,2,1,0:T(8,128)S(1)} %copy-done), custom_call_target="tpu_custom_call" | custom-call | tf_op jit(solution)/shard_map/states0/pallas_call | solution.py:325
  86.4 2.4 %all-to-all-done.2.refs_0_.refs_1_ = bf16[16,112,256]{2,1,0:T(8,128)(2,1)S(1)} async-done(((bf16[16,112,256]{2,1,0:T(8,128)(2,1)}), bf16[16,112,256]{2,1,0:T(8,128)(2,1)S(1)}, u32[]{:S(2)}, u32[]{:S(2)}) %all-to-all-start.2) | async-done | bytes 917536 | tf_op jit(solution)/shard_map/all_to_all | solution.py:490
  88.8 0.2 update_spread.1
  89.0 14.5 %all_to_all.30.refs_2_ = bf16[16,64,256]{2,1,0:T(8,128)(2,1)} all-to-all(bf16[16,64,256]{2,1,0:T(8,128)(2,1)S(1)} %get-tuple-element.54), channel_id=1, replica_groups=mesh['row'=8,'col'=16] {'col'}, dimensions={0} | all-to-all | bytes 1048576 | tf_op jit(solution)/shard_map/all_to_all | solution.py:490
  103.5 6.5 %all-to-all-start.4 = ((bf16[16,2,4,64,128]{4,3,2,1,0:T(8,128)(2,1)}), bf16[16,2,4,64,128]{4,3,2,1,0:T(8,128)(2,1)}, u32[]{:S(2)}, u32[]{:S(2)}) async-start(bf16[16,2,4,64,128]{4,3,2,1,0:T(8,128)(2,1)} %starts1.1), calls=%async_computation.4 | async-start | bytes 4194304 | tf_op jit(solution)/shard_map/all_to_all | solution.py:490
  110.1 3.7 %owned0.1.refs_2_ = bf16[2,2,64,64,128]{4,3,2,1,0:T(8,128)(2,1)} custom-call(bf16[16,2,4,64,128]{4,3,2,1,0:T(8,128)(2,1)} %all-to-all-done.1.refs_0_, bf16[16,112,256]{2,1,0:T(8,128)(2,1)S(1)} %all-to-all-done.2.refs_0_.refs_1_), custom_call_target="tpu_custom_call" | custom-call | tf_op jit(solution)/shard_map/owned0/pallas_call | solution.py:431
  113.8 0.0 all-gather.7.cloned.1.call-done
  113.9 6.4 %front1.1 = (bf16[16,112,256]{2,1,0:T(8,128)(2,1)}, f32[128,256]{1,0:T(8,128)}, f32[128,128]{1,0:T(8,128)}, f32[128,512]{1,0:T(8,128)}) custom-call(s32[26]{0:T(128)} %concatenate.6.ints_ref.refs_0_, f32[2,12]{1,0:T(2,128)} %pad_maximum_fusion.refs_1_, bf16[16,64,256]{2,1,0:T(8,128)(2,1)} %all_to_all.30.refs_2_, bf16[8,256,1152]{2,1,0:T(8,128)(2,1)} %bitcast.11, ...), custom_call_target="tpu_custom_call" | custom-call | tf_op jit(solution)/shard_map/front1/pallas_call | solution.py:266
  120.3 16.0 %all-to-all-done.4.refs_0_ = bf16[16,2,4,64,128]{4,3,2,1,0:T(8,128)(2,1)} async-done(((bf16[16,2,4,64,128]{4,3,2,1,0:T(8,128)(2,1)}), bf16[16,2,4,64,128]{4,3,2,1,0:T(8,128)(2,1)}, u32[]{:S(2)}, u32[]{:S(2)}) %all-to-all-start.4) | async-done | bytes 2097184 | tf_op jit(solution)/shard_map/all_to_all | solution.py:490
  136.3 6.2 %all-to-all-start.5 = ((bf16[16,112,256]{2,1,0:T(8,128)(2,1)}), bf16[16,112,256]{2,1,0:T(8,128)(2,1)S(1)}, u32[]{:S(2)}, u32[]{:S(2)}) async-start(bf16[16,112,256]{2,1,0:T(8,128)(2,1)} %get-tuple-element.61), calls=%async_computation.5 | async-start | bytes 1835008 | tf_op jit(solution)/shard_map/all_to_all | solution.py:490
  142.6 0.9 copy-done.2
  143.5 0.9 copy-done.4
  144.4 0.8 copy-done.6
  145.2 7.8 %states1.1 = bf16[2,8,16,4,64,128]{5,4,3,2,1,0:T(8,128)(2,1)} custom-call(f32[128,256]{1,0:T(8,128)S(1)} %copy-done.4, f32[128,128]{1,0:T(8,128)S(1)} %copy-done.6, f32[128,512]{1,0:T(8,128)S(1)} %copy-done.2, f32[2,8,4,64,128]{4,3,2,1,0:T(8,128)S(1)} %copy-done.1, bf16[2,8,16,4,64,128]{5,4,3,2,1,0:T(8,128)(2,1)} %states0.1.rest_0_), custom_call_target="tpu_custom_call", output_to_operand_aliasing={{}: (4, {})} | custom-call | tf_op jit(solution)/shard_map/states1/pallas_call | solution.py:325
  153.1 2.2 %all-to-all-done.5.refs_0_.refs_1_ = bf16[16,112,256]{2,1,0:T(8,128)(2,1)S(1)} async-done(((bf16[16,112,256]{2,1,0:T(8,128)(2,1)}), bf16[16,112,256]{2,1,0:T(8,128)(2,1)S(1)}, u32[]{:S(2)}, u32[]{:S(2)}) %all-to-all-start.5) | async-done | bytes 917536 | tf_op jit(solution)/shard_map/all_to_all | solution.py:490
  155.3 0.2 update_last.1
  155.5 6.2 %collective-permute-start.1 = (bf16[64,256]{1,0:T(8,128)(2,1)S(1)}, bf16[64,256]{1,0:T(8,128)(2,1)S(1)}, u32[]{:S(2)}, u32[]{:S(2)}) collective-permute-start(bf16[64,256]{1,0:T(8,128)(2,1)S(1)} %update_last.1), channel_id=1, source_target_pairs={{0,0},{8,1},{16,2},{24,3},{32,4},{40,5},{48,6},{56,7},{64,8},{72,9... | collective-permute-start | bytes 98312 | tf_op jit(solution)/shard_map/ppermute | solution.py:566
  161.6 3.7 %owned1.1 = bf16[2,2,64,64,128]{4,3,2,1,0:T(8,128)(2,1)} custom-call(bf16[16,2,4,64,128]{4,3,2,1,0:T(8,128)(2,1)} %all-to-all-done.4.refs_0_, bf16[16,112,256]{2,1,0:T(8,128)(2,1)S(1)} %all-to-all-done.5.refs_0_.refs_1_, bf16[2,2,64,64,128]{4,3,2,1,0:T(8,128)(2,1)} %owned0.1.refs_2_), custom_call_target="tpu_custom_call", output_to_operand_aliasing={{}: (2, {})} | custom-call | tf_op jit(solution)/shard_map/owned1/pallas_call | solution.py:431
  165.4 0.6 copy.40
  (28 shorter events, 0.1 us)
Async XLA Ops:
  7.2 19.8 %copy-start.11 = (s32[4,2]{0,1:T(2,128)S(1)}, s32[4,2]{0,1:T(2,128)}, u32[]{:S(2)}) copy-start(s32[4,2]{0,1:T(2,128)} %param.35) | copy-start | bytes 100
  7.2 20.0 %copy-start.16 = (s32[8]{0:T(128)S(1)}, s32[8]{0:T(128)}, u32[]{:S(2)}) copy-start(s32[8]{0:T(128)} %param.34) | copy-start | bytes 100
  7.2 20.0 %copy-start.15 = (s32[8]{0:T(128)S(1)}, s32[8]{0:T(128)}, u32[]{:S(2)}) copy-start(s32[8]{0:T(128)} %param.33) | copy-start | bytes 100
  7.2 46.4 %all-gather.5.cloned.1.call-start = ((), (), s32[]{:S(2)}) async-start(), calls=%async_computation.6 | async-start | bytes 5308416 | tf_op jit(solution)/shard_map/all_gather | solution.py:538
  7.2 8.4 %collective-permute-start = (bf16[64,256]{1,0:T(8,128)(2,1)}, bf16[64,256]{1,0:T(8,128)(2,1)S(1)}, u32[]{:S(2)}, u32[]{:S(2)}) collective-permute-start(bf16[64,256]{1,0:T(8,128)(2,1)} %param.18), channel_id=1, source_target_pairs={{0,0},{1,8},{2,16},{3,24},{4,32},{5,40},{6,48},{7,56},{8,64},{9,72... | collective-permute-start | bytes 98312 | tf_op jit(solution)/shard_map/ppermute | solution.py:529
  16.6 19.5 %all-to-all-start = ((bf16[16,64,256]{2,1,0:T(8,128)(2,1)}), bf16[16,64,256]{2,1,0:T(8,128)(2,1)S(1)}, u32[]{:S(2)}, u32[]{:S(2)}) async-start(bf16[16,64,256]{2,1,0:T(8,128)(2,1)} %broadcast_in_dim.4), calls=%async_computation | async-start | bytes 1048576 | tf_op jit(solution)/shard_map/all_to_all | solution.py:490
  26.9 86.9 %all-gather.7.cloned.1.call-start = ((), (), s32[]{:S(2)}) async-start(), calls=%async_computation.7 | async-start | bytes 5308416 | tf_op jit(solution)/shard_map/all_gather | solution.py:544
  33.8 9.5 %copy-start.9 = (bf16[2,8,3,256]{3,1,2,0:T(8,128)(2,1)S(1)}, bf16[2,8,3,256]{3,1,2,0:T(8,128)(2,1)}, u32[]{:S(2)}) copy-start(bf16[2,8,3,256]{3,1,2,0:T(8,128)(2,1)} %param.30) | copy-start | bytes 73732
  33.8 10.2 %copy-start.10 = (bf16[2,8,3,256]{3,1,2,0:T(8,128)(2,1)S(1)}, bf16[2,8,3,256]{3,1,2,0:T(8,128)(2,1)}, u32[]{:S(2)}) copy-start(bf16[2,8,3,256]{3,1,2,0:T(8,128)(2,1)} %param.31) | copy-start | bytes 73732
  33.8 10.8 %copy-start.12 = (f32[2,4]{1,0:T(2,128)S(1)}, f32[2,4]{1,0:T(2,128)}, u32[]{:S(2)}) copy-start(f32[2,4]{1,0:T(2,128)} %param.27) | copy-start | bytes 100
  33.8 10.8 %copy-start.13 = (f32[2,4]{1,0:T(2,128)S(1)}, f32[2,4]{1,0:T(2,128)}, u32[]{:S(2)}) copy-start(f32[2,4]{1,0:T(2,128)} %param.26) | copy-start | bytes 100
  33.8 10.8 %copy-start.14 = (f32[2,4]{1,0:T(2,128)S(1)}, f32[2,4]{1,0:T(2,128)}, u32[]{:S(2)}) copy-start(f32[2,4]{1,0:T(2,128)} %param.25) | copy-start | bytes 100
  36.0 17.6 %copy-start.8 = (bf16[16,64,256]{2,1,0:T(8,128)(2,1)}, bf16[16,64,256]{2,1,0:T(8,128)(2,1)S(1)}, u32[]{:S(2)}) copy-start(bf16[16,64,256]{2,1,0:T(8,128)(2,1)S(1)} %all-to-all-done.refs_2_) | copy-start | bytes 1572868
  36.1 34.0 %all-to-all-start.1 = ((bf16[16,2,4,64,128]{4,3,2,1,0:T(8,128)(2,1)}), bf16[16,2,4,64,128]{4,3,2,1,0:T(8,128)(2,1)}, u32[]{:S(2)}, u32[]{:S(2)}) async-start(bf16[16,2,4,64,128]{4,3,2,1,0:T(8,128)(2,1)} %starts0.1), calls=%async_computation.1 | async-start | bytes 4194304 | tf_op jit(solution)/shard_map/all_to_all | solution.py:490
  53.6 22.2 %copy-start = (f32[2,8,4,64,128]{4,3,2,1,0:T(8,128)S(1)}, f32[2,8,4,64,128]{4,3,2,1,0:T(8,128)}, u32[]{:S(2)}) copy-start(f32[2,8,4,64,128]{4,3,2,1,0:T(8,128)} %state_ref.7) | copy-start | bytes 6291460
  70.1 18.7 %all-to-all-start.2 = ((bf16[16,112,256]{2,1,0:T(8,128)(2,1)}), bf16[16,112,256]{2,1,0:T(8,128)(2,1)S(1)}, u32[]{:S(2)}, u32[]{:S(2)}) async-start(bf16[16,112,256]{2,1,0:T(8,128)(2,1)} %get-tuple-element.49), calls=%async_computation.2 | async-start | bytes 1835008 | tf_op jit(solution)/shard_map/all_to_all | solution.py:490
  75.9 1.0 copy-start.3
  76.8 0.9 copy-start.5
  77.7 0.8 copy-start.7
  103.5 32.8 %all-to-all-start.4 = ((bf16[16,2,4,64,128]{4,3,2,1,0:T(8,128)(2,1)}), bf16[16,2,4,64,128]{4,3,2,1,0:T(8,128)(2,1)}, u32[]{:S(2)}, u32[]{:S(2)}) async-start(bf16[16,2,4,64,128]{4,3,2,1,0:T(8,128)(2,1)} %starts1.1), calls=%async_computation.4 | async-start | bytes 4194304 | tf_op jit(solution)/shard_map/all_to_all | solution.py:490
  113.8 28.7 %copy-start.1 = (f32[2,8,4,64,128]{4,3,2,1,0:T(8,128)S(1)}, f32[2,8,4,64,128]{4,3,2,1,0:T(8,128)}, u32[]{:S(2)}) copy-start(f32[2,8,4,64,128]{4,3,2,1,0:T(8,128)} %state_ref.7) | copy-start | bytes 6291460
  136.3 19.0 %all-to-all-start.5 = ((bf16[16,112,256]{2,1,0:T(8,128)(2,1)}), bf16[16,112,256]{2,1,0:T(8,128)(2,1)S(1)}, u32[]{:S(2)}, u32[]{:S(2)}) async-start(bf16[16,112,256]{2,1,0:T(8,128)(2,1)} %get-tuple-element.61), calls=%async_computation.5 | async-start | bytes 1835008 | tf_op jit(solution)/shard_map/all_to_all | solution.py:490
  142.5 1.0 copy-start.2
  143.5 0.9 copy-start.4
  144.4 0.8 copy-start.6
  155.5 9.9 %collective-permute-start.1 = (bf16[64,256]{1,0:T(8,128)(2,1)S(1)}, bf16[64,256]{1,0:T(8,128)(2,1)S(1)}, u32[]{:S(2)}, u32[]{:S(2)}) collective-permute-start(bf16[64,256]{1,0:T(8,128)(2,1)S(1)} %update_last.1), channel_id=1, source_target_pairs={{0,0},{8,1},{16,2},{24,3},{32,4},{40,5},{48,6},{56,7},{64,8},{72,9... | collective-permute-start | bytes 98312 | tf_op jit(solution)/shard_map/ppermute | solution.py:566
Sparse Core Ops, SparseCore 0:
  15.8 37.7 all-gather.4
  55.3 34.2 all-gather.6

commit v7 on v6

--- a/solution.py
+++ b/solution.py
@@ -342,26 +342,27 @@
 
 def starts_body(ints_ref, state_ref, send_ref):
     send_ref[...] = jnp.zeros(send_ref.shape, BF)
-    requests = state_ref.shape[0]
+    layers, requests = state_ref.shape[:2]
     for q in range(requests):
         live, owner, rank = route(q, ints_ref, requests)
 
         @pl.when(live)
         def _put():
-            send_ref[owner, rank] = state_ref[q].astype(BF)
-
-
-def starts(layer, ints, state):
-    shape = (COLS, SEND_CAP) + state.shape[2:]
+            for layer in range(layers):
+                send_ref[owner, layer, rank] = state_ref[layer, q].astype(BF)
+
+
+def starts(ints, state):
+    shape = (COLS, state.shape[0], SEND_CAP) + state.shape[2:]
     return pl.pallas_call(
         starts_body,
-        name="starts%d" % layer,
+        name="starts",
         grid=(1,),
         in_specs=[
             pl.BlockSpec(memory_space=pltpu.SMEM),
-            pl.BlockSpec((None,) + state.shape[1:], lambda i: (layer, 0, 0, 0, 0)),
+            pl.BlockSpec(state.shape, lambda i: (0, 0, 0, 0, 0)),
         ],
-        out_specs=pl.BlockSpec(shape, lambda i: (0, 0, 0, 0, 0)),
+        out_specs=pl.BlockSpec(shape, lambda i: (0, 0, 0, 0, 0, 0)),
         out_shape=jax.ShapeDtypeStruct(shape, BF),
         compiler_params=pltpu.CompilerParams(
             dimension_semantics=("arbitrary",), vmem_limit_bytes=VMEM_BYTES
@@ -369,10 +370,20 @@
     )(ints, state)
 
 
-def owned_body(layer, starts_ref, received_ref, *rest):
-    out_ref, stage, b_s, sems = rest[-4:]
+def owned_body(layer, begun_ref, received_ref, *rest):
+    out_ref, starts_ref, stage, b_s, sems, in_sems = rest[-6:]
     cols, slots, heads, head_size, state_size = starts_ref.shape
     group = 4
+    arrivals = [
+        pltpu.make_async_copy(
+            begun_ref.at[pl.ds(i * group, group), layer],
+            starts_ref.at[pl.ds(i * group, group)],
+            in_sems.at[i],
+        )
+        for i in range(cols // group)
+    ]
+    for arrival in arrivals:
+        arrival.start()
     dx_rows = slots * S
     misc_at = received_ref.shape[1] - SUM_ROWS
     dx_at = misc_at - dx_rows
@@ -393,6 +404,7 @@
             [received_ref[i * group + g, dx_at:misc_at, :] for g in range(group)], axis=1
         )
         added = lax.dot_general(dx, b_all, (((0,), (0,)), ((), ())), preferred_element_type=F32)
+        arrivals[i].wait()
         for slot in range(slots):
             for g in range(group):
                 c = i * group + g
@@ -420,7 +432,7 @@
     layers, _, heads, head_size, state_size = state.shape
     resident = pl.BlockSpec(memory_space=pltpu.VMEM)
     anywhere = pl.BlockSpec(memory_space=pl.ANY)
-    in_specs = [resident, resident]
+    in_specs = [anywhere, resident]
     operands = [begun, received]
     aliases = {}
     if previous is not None:
@@ -437,9 +449,11 @@
             (SEND_CAP, layers, all_heads, head_size, state_size), BF
         ),
         scratch_shapes=[
+            pltpu.VMEM((COLS, SEND_CAP, heads, head_size, state_size), BF),
             pltpu.VMEM((SEND_CAP, all_heads, head_size, state_size), BF),
             pltpu.VMEM((SEND_CAP * S, SEND_CAP * state_size), F32),
             pltpu.SemaphoreType.DMA((SEND_CAP * COLS // 4,)),
+            pltpu.SemaphoreType.DMA((COLS // 4,)),
         ],
         input_output_aliases=aliases,
         compiler_params=pltpu.CompilerParams(vmem_limit_bytes=SMALL_VMEM_BYTES),
@@ -537,13 +551,12 @@
     first, block = lax.optimization_barrier((pack(0, *raw), block))
     weights = [lax.all_gather(first, "row", axis=0)]
     everything = swap(jnp.broadcast_to(block[None], (COLS,) + block.shape))
-    sends = [starts(layer, ints, state_cache) for layer in range(layer_count)]
-    sends, raw = lax.optimization_barrier((sends, raw))
+    send = starts(ints, state_cache)
+    send, raw = lax.optimization_barrier((send, raw))
     second = pack(1, *raw)
-    everything, sends, second = lax.optimization_barrier((everything, sends, second))
+    everything, send, second = lax.optimization_barrier((everything, send, second))
     weights.append(lax.all_gather(second, "row", axis=0))
-    begun = swap(sends[0])
-    send = sends[1]
+    begun = swap(send)
 
     steps = None
     owned = None
@@ -553,7 +566,7 @@
             layer, ints, floats, everything, weights[layer], inner_kernel, proj_kernel,
             norm_gain, inner_cache, proj_cache, state_cache,
         )
-        part, begun, owned = lax.optimization_barrier((part, begun, owned))
+        part, begun = lax.optimization_barrier((part, begun))
         received = swap(part)
         steps = states(layer, dx, b_conv, decay, state_cache, steps)
         received, steps = lax.optimization_barrier((received, steps))
@@ -561,8 +574,8 @@
         owned = owned_states(layer, state_cache, begun, received, owned)
         if not last:
             block = fresh[0]
-            everything, send = lax.optimization_barrier((swap(fresh[1]), send))
-            begun = swap(send)
+            everything = swap(fresh[1])
+            everything, owned = lax.optimization_barrier((everything, owned))
     hidden = lax.ppermute(fresh[0], ("row", "col"), back)
     owned_block = owned[None, None]
     return (hidden, steps, owned_block)

time: 176 us -> 175 us (level)
  waiting for transfers between devices: 40.5 us -> 56.1 us
  blocking collectives: 14.5 us -> 0 us
  starting transfers between devices: 45.4 us -> 43.1 us
    all_to_all x5, waiting for transfers between devices: 30.7 us -> 45.7 us  [swap(): return lax.all_to_all(x, 'col', 0, 0, tiled=True)]
    all_to_all x1 -> x0, blocking collectives: 14.5 us -> none  [swap(): return lax.all_to_all(x, 'col', 0, 0, tiled=True)]
    pallas_call x2 -> x1, Pallas kernels: 6 us -> 4.5 us  [starts(): pl.pallas_call(starts_body, name='starts', grid=(1,), in_specs=[pl.BlockS...]
    unnamed x39 -> x41, local copies, waits for them, and re-layouts: 9.29 us -> 10.8 us
  transfers between devices with their start and end apart: 9 -> 9, of which waited for: 6 -> 6; matrix products, arithmetic and copies ran while one was open for 3% -> 3% of each run, Pallas kernels for 27% -> 23%
where the time goes in v7:
time: 175 us; the launch traced here: 172 us
  waiting for transfers between devices  56.1 us (32%)
  Pallas kernels  45.7 us (26%)
  starting transfers between devices  43.1 us (25%)
  between operations  14.2 us (8%)
  local copies, waits for them, and re-layouts  12.4 us (7%)
    all_to_all x5, waiting for transfers between devices, swap(): return lax.all_to_all(x, 'col', 0, 0, tiled=True)  45.7 us
    all_to_all x5, starting transfers between devices, swap(): return lax.all_to_all(x, 'col', 0, 0, tiled=True)  34.5 us
    pallas_call x2, Pallas kernels, states(): pl.pallas_call(states_body, name='states%d' % layer, grid=(requests,), in...  15.6 us
    pallas_call x2, Pallas kernels, front(): pl.pallas_call(lambda *refs: front_body(layer, *refs), name='front%d' % l...  12.9 us
    unnamed x41, local copies, waits for them, and re-layouts  10.8 us
    all_gather x1, waiting for transfers between devices, local(): weights = [lax.all_gather(first, 'row', axis=0)]  9.07 us
    pallas_call x2, Pallas kernels, owned_states(): pl.pallas_call(lambda *refs: owned_body(layer, *refs), name='owned%d' % l...  7.23 us
    ppermute x1, starting transfers between devices, local(): hidden = lax.ppermute(fresh[0], ('row', 'col'), back)  5.57 us
  transfers between devices with their start and end apart: 9, of which 6 were waited for; matrix products, arithmetic and copies ran while one was open for 3% of the time, Pallas kernels for 23%

profile of v7, /device:TPU:32, one launch (start us, length us, event | category | flops | bytes accessed | tf_op | source)
XLA Modules:
  0.0 172.2 jit_solution(1699289475008869383)
XLA Ops:
  7.2 0.0 all-gather.5.cloned.1.call-start
  7.2 3.0 %collective-permute-start = (bf16[64,256]{1,0:T(8,128)(2,1)}, bf16[64,256]{1,0:T(8,128)(2,1)S(1)}, u32[]{:S(2)}, u32[]{:S(2)}) collective-permute-start(bf16[64,256]{1,0:T(8,128)(2,1)} %param.18), channel_id=1, source_target_pairs={{0,0},{1,8},{2,16},{3,24},{4,32},{5,40},{6,48},{7,56},{8,64},{9,72... | collective-permute-start | bytes 98312 | tf_op jit(solution)/shard_map/ppermute | solution.py:543
  10.3 1.9 %copy.36 = bf16[2,256,2,256]{3,1,2,0:T(8,128)(2,1)} copy(bf16[2,256,2,256]{3,2,1,0:T(2,128)(2,1)} %param.20) | data formatting | bytes 1048576 | tf_op args[2]
  12.2 2.1 %pack0.1 = bf16[256,1152]{1,0:T(8,128)(2,1)} custom-call(bf16[2,2,256,256]{3,2,1,0:T(8,128)(2,1)} %bitcast.12, bf16[2,256,256]{2,1,0:T(8,128)(2,1)} %refs_1_.2, bf16[2,4,256]{2,1,0:T(4,128)(2,1)} %bitcast.14, f32[2,256]{1,0:T(2,128)} %refs_3_.2, bf16[2,256,256]{2,1,0:T(8,128)(2,1)} %refs_4_.4), custom_call_target="tpu_custom_call" | custom-call | tf_op jit(solution)/shard_map/pack0/pallas_call | solution.py:49
  14.3 1.3 collective-permute-done.refs_2_
  15.7 0.0 all-gather.5.cloned.1.call-update
  15.7 0.9 broadcast_in_dim.4
  16.5 10.4 %all-to-all-start = ((bf16[16,64,256]{2,1,0:T(8,128)(2,1)}), bf16[16,64,256]{2,1,0:T(8,128)(2,1)S(1)}, u32[]{:S(2)}, u32[]{:S(2)}) async-start(bf16[16,64,256]{2,1,0:T(8,128)(2,1)} %broadcast_in_dim.4), calls=%async_computation | async-start | bytes 1048576 | tf_op jit(solution)/shard_map/all_to_all | solution.py:504
  26.9 0.0 all-gather.7.cloned.1.call-start
  27.0 0.1 copy.29
  27.1 0.1 reshape.18
  27.2 0.7 concatenate.6.ints_ref.refs_0_
  27.8 4.5 %starts.1 = bf16[16,2,2,4,64,128]{5,4,3,2,1,0:T(8,128)(2,1)} custom-call(s32[26]{0:T(128)} %concatenate.6.ints_ref.refs_0_, f32[2,8,4,64,128]{4,3,2,1,0:T(8,128)} %state_ref.5), custom_call_target="tpu_custom_call" | custom-call | tf_op jit(solution)/shard_map/starts/pallas_call | solution.py:357
  32.3 2.2 %pack1.1 = bf16[256,1152]{1,0:T(8,128)(2,1)} custom-call(bf16[2,2,256,256]{3,2,1,0:T(8,128)(2,1)} %bitcast.13, bf16[2,256,256]{2,1,0:T(8,128)(2,1)} %refs_1_.2, bf16[2,4,256]{2,1,0:T(4,128)(2,1)} %bitcast.15, f32[2,256]{1,0:T(2,128)} %refs_3_.2, bf16[2,256,256]{2,1,0:T(8,128)(2,1)} %refs_4_.4), custom_call_target="tpu_custom_call" | custom-call | tf_op jit(solution)/shard_map/pack1/pallas_call | solution.py:49
  34.5 0.9 all-to-all-done.refs_2_
  35.4 0.0 all-gather.7.cloned.1.call-update
  35.4 0.0 copy-start.10
  35.4 0.0 copy-start.11
  35.4 0.0 copy-start.14
  35.5 0.7 copy-done.8
  36.1 6.6 %all-to-all-start.1 = ((bf16[16,2,2,4,64,128]{5,4,3,2,1,0:T(8,128)(2,1)}), bf16[16,2,2,4,64,128]{5,4,3,2,1,0:T(8,128)(2,1)}, u32[]{:S(2)}, u32[]{:S(2)}) async-start(bf16[16,2,2,4,64,128]{5,4,3,2,1,0:T(8,128)(2,1)} %starts.1), calls=%async_computation.1 | async-start | bytes 8388608 | tf_op jit(solution)/shard_map/all_to_all | solution.py:504
  42.7 0.6 copy.31.refs_7_
  43.4 0.6 copy.32.refs_8_
  44.0 0.6 pad_maximum_fusion.refs_1_
  44.6 9.1 %all-gather.5.cloned.1.call-done = bf16[2048,1152]{1,0:T(8,128)(2,1)} async-done(((bf16[256,1152]{1,0:T(8,128)(2,1)}), bf16[2048,1152]{1,0:T(8,128)(2,1)}) %all-gather.5.cloned.1.call-update) | async-done | bytes 4718608 | tf_op jit(solution)/shard_map/all_gather | solution.py:552
  53.6 6.4 %front0.1 = (bf16[16,112,256]{2,1,0:T(8,128)(2,1)}, f32[128,256]{1,0:T(8,128)}, f32[128,128]{1,0:T(8,128)}, f32[128,512]{1,0:T(8,128)}) custom-call(s32[26]{0:T(128)} %concatenate.6.ints_ref.refs_0_, f32[2,12]{1,0:T(2,128)} %pad_maximum_fusion.refs_1_, bf16[16,64,256]{2,1,0:T(8,128)(2,1)} %copy-done.8, bf16[8,256,1152]{2,1,0:T(8,128)(2,1)} %bitcast.11, ...), custom_call_target="tpu_custom_call" | custom-call | tf_op jit(solution)/shard_map/front0/pallas_call | solution.py:266
  60.1 40.0 %all-to-all-done.1.refs_0_ = bf16[16,2,2,4,64,128]{5,4,3,2,1,0:T(8,128)(2,1)} async-done(((bf16[16,2,2,4,64,128]{5,4,3,2,1,0:T(8,128)(2,1)}), bf16[16,2,2,4,64,128]{5,4,3,2,1,0:T(8,128)(2,1)}, u32[]{:S(2)}, u32[]{:S(2)}) %all-to-all-start.1) | async-done | bytes 4194336 | tf_op jit(solution)/shard_map/all_to_all | solution.py:504
  100.1 5.0 %all-to-all-start.2 = ((bf16[16,112,256]{2,1,0:T(8,128)(2,1)}), bf16[16,112,256]{2,1,0:T(8,128)(2,1)S(1)}, u32[]{:S(2)}, u32[]{:S(2)}) async-start(bf16[16,112,256]{2,1,0:T(8,128)(2,1)} %get-tuple-element.45), calls=%async_computation.2 | async-start | bytes 1835008 | tf_op jit(solution)/shard_map/all_to_all | solution.py:504
  105.1 0.9 copy-done.2
  106.1 0.9 copy-done.4
  107.0 0.8 copy-done.6
  107.8 7.8 %states0.1.rest_0_ = bf16[2,8,16,4,64,128]{5,4,3,2,1,0:T(8,128)(2,1)} custom-call(f32[128,256]{1,0:T(8,128)S(1)} %copy-done.4, f32[128,128]{1,0:T(8,128)S(1)} %copy-done.6, f32[128,512]{1,0:T(8,128)S(1)} %copy-done.2, f32[2,8,4,64,128]{4,3,2,1,0:T(8,128)S(1)} %copy-done), custom_call_target="tpu_custom_call" | custom-call | tf_op jit(solution)/shard_map/states0/pallas_call | solution.py:325
  115.6 0.4 all-to-all-done.2.refs_0_.refs_1_
  116.0 1.0 update_spread.1
  117.0 6.8 %all-to-all-start.3 = ((bf16[16,64,256]{2,1,0:T(8,128)(2,1)}), bf16[16,64,256]{2,1,0:T(8,128)(2,1)S(1)}, u32[]{:S(2)}, u32[]{:S(2)}) async-start(bf16[16,64,256]{2,1,0:T(8,128)(2,1)} %get-tuple-element.50), calls=%async_computation.3 | async-start | bytes 1048576 | tf_op jit(solution)/shard_map/all_to_all | solution.py:504
  123.9 3.6 %owned0.1.refs_2_ = bf16[2,2,64,64,128]{4,3,2,1,0:T(8,128)(2,1)} custom-call(bf16[16,2,2,4,64,128]{5,4,3,2,1,0:T(8,128)(2,1)} %all-to-all-done.1.refs_0_, bf16[16,112,256]{2,1,0:T(8,128)(2,1)S(1)} %all-to-all-done.2.refs_0_.refs_1_), custom_call_target="tpu_custom_call" | custom-call | tf_op jit(solution)/shard_map/owned0/pallas_call | solution.py:443
  127.5 4.4 %all-to-all-done.3.refs_2_ = bf16[16,64,256]{2,1,0:T(8,128)(2,1)S(1)} async-done(((bf16[16,64,256]{2,1,0:T(8,128)(2,1)}), bf16[16,64,256]{2,1,0:T(8,128)(2,1)S(1)}, u32[]{:S(2)}, u32[]{:S(2)}) %all-to-all-start.3) | async-done | bytes 524320 | tf_op jit(solution)/shard_map/all_to_all | solution.py:504
  131.9 0.8 copy-done.9
  132.7 6.4 %front1.1 = (bf16[16,112,256]{2,1,0:T(8,128)(2,1)}, f32[128,256]{1,0:T(8,128)}, f32[128,128]{1,0:T(8,128)}, f32[128,512]{1,0:T(8,128)}) custom-call(s32[26]{0:T(128)} %concatenate.6.ints_ref.refs_0_, f32[2,12]{1,0:T(2,128)} %pad_maximum_fusion.refs_1_, bf16[16,64,256]{2,1,0:T(8,128)(2,1)} %copy-done.9, bf16[8,256,1152]{2,1,0:T(8,128)(2,1)} %bitcast.10, ...), custom_call_target="tpu_custom_call" | custom-call | tf_op jit(solution)/shard_map/front1/pallas_call | solution.py:266
  139.1 5.7 %all-to-all-start.4 = ((bf16[16,112,256]{2,1,0:T(8,128)(2,1)}), bf16[16,112,256]{2,1,0:T(8,128)(2,1)S(1)}, u32[]{:S(2)}, u32[]{:S(2)}) async-start(bf16[16,112,256]{2,1,0:T(8,128)(2,1)} %get-tuple-element.55), calls=%async_computation.4 | async-start | bytes 1835008 | tf_op jit(solution)/shard_map/all_to_all | solution.py:504
  144.8 0.9 copy-done.3
  145.7 0.9 copy-done.5
  146.6 0.8 copy-done.7
  147.5 7.8 %states1.1 = bf16[2,8,16,4,64,128]{5,4,3,2,1,0:T(8,128)(2,1)} custom-call(f32[128,256]{1,0:T(8,128)S(1)} %copy-done.5, f32[128,128]{1,0:T(8,128)S(1)} %copy-done.7, f32[128,512]{1,0:T(8,128)S(1)} %copy-done.3, f32[2,8,4,64,128]{4,3,2,1,0:T(8,128)S(1)} %copy-done.1, bf16[2,8,16,4,64,128]{5,4,3,2,1,0:T(8,128)(2,1)} %states0.1.rest_0_), custom_call_target="tpu_custom_call", output_to_operand_aliasing={{}: (4, {})} | custom-call | tf_op jit(solution)/shard_map/states1/pallas_call | solution.py:325
  155.3 0.2 update_last.1
  155.5 5.6 %collective-permute-start.1 = (bf16[64,256]{1,0:T(8,128)(2,1)S(1)}, bf16[64,256]{1,0:T(8,128)(2,1)S(1)}, u32[]{:S(2)}, u32[]{:S(2)}) collective-permute-start(bf16[64,256]{1,0:T(8,128)(2,1)S(1)} %update_last.1), channel_id=1, source_target_pairs={{0,0},{8,1},{16,2},{24,3},{32,4},{40,5},{48,6},{56,7},{64,8},{72,9... | collective-permute-start | bytes 98312 | tf_op jit(solution)/shard_map/ppermute | solution.py:579
  161.1 3.6 %owned1.1 = bf16[2,2,64,64,128]{4,3,2,1,0:T(8,128)(2,1)} custom-call(bf16[16,2,2,4,64,128]{5,4,3,2,1,0:T(8,128)(2,1)} %all-to-all-done.1.refs_0_, bf16[16,112,256]{2,1,0:T(8,128)(2,1)S(1)} %all-to-all-done.4.refs_0_.refs_1_, bf16[2,2,64,64,128]{4,3,2,1,0:T(8,128)(2,1)} %owned0.1.refs_2_), custom_call_target="tpu_custom_call", output_to_operand_aliasing={{}: (2, {})} | custom-call | tf_op jit(solution)/shard_map/owned1/pallas_call | solution.py:443
  164.7 0.6 copy.40
  (28 shorter events, 0.1 us)
Async XLA Ops:
  7.2 19.8 %copy-start.12 = (s32[4,2]{0,1:T(2,128)S(1)}, s32[4,2]{0,1:T(2,128)}, u32[]{:S(2)}) copy-start(s32[4,2]{0,1:T(2,128)} %param.35) | copy-start | bytes 100
  7.2 20.0 %copy-start.17 = (s32[8]{0:T(128)S(1)}, s32[8]{0:T(128)}, u32[]{:S(2)}) copy-start(s32[8]{0:T(128)} %param.34) | copy-start | bytes 100
  7.2 20.0 %copy-start.16 = (s32[8]{0:T(128)S(1)}, s32[8]{0:T(128)}, u32[]{:S(2)}) copy-start(s32[8]{0:T(128)} %param.33) | copy-start | bytes 100
  7.2 46.4 %all-gather.5.cloned.1.call-start = ((), (), s32[]{:S(2)}) async-start(), calls=%async_computation.5 | async-start | bytes 5308416 | tf_op jit(solution)/shard_map/all_gather | solution.py:552
  7.2 8.4 %collective-permute-start = (bf16[64,256]{1,0:T(8,128)(2,1)}, bf16[64,256]{1,0:T(8,128)(2,1)S(1)}, u32[]{:S(2)}, u32[]{:S(2)}) collective-permute-start(bf16[64,256]{1,0:T(8,128)(2,1)} %param.18), channel_id=1, source_target_pairs={{0,0},{1,8},{2,16},{3,24},{4,32},{5,40},{6,48},{7,56},{8,64},{9,72... | collective-permute-start | bytes 98312 | tf_op jit(solution)/shard_map/ppermute | solution.py:543
  16.5 18.8 %all-to-all-start = ((bf16[16,64,256]{2,1,0:T(8,128)(2,1)}), bf16[16,64,256]{2,1,0:T(8,128)(2,1)S(1)}, u32[]{:S(2)}, u32[]{:S(2)}) async-start(bf16[16,64,256]{2,1,0:T(8,128)(2,1)} %broadcast_in_dim.4), calls=%async_computation | async-start | bytes 1048576 | tf_op jit(solution)/shard_map/all_to_all | solution.py:504
  26.9 105.0 %all-gather.7.cloned.1.call-start = ((), (), s32[]{:S(2)}) async-start(), calls=%async_computation.6 | async-start | bytes 5308416 | tf_op jit(solution)/shard_map/all_gather | solution.py:558
  35.4 0.8 copy-start.8
  35.4 7.3 %copy-start.10 = (bf16[2,8,3,256]{3,1,2,0:T(8,128)(2,1)S(1)}, bf16[2,8,3,256]{3,1,2,0:T(8,128)(2,1)}, u32[]{:S(2)}) copy-start(bf16[2,8,3,256]{3,1,2,0:T(8,128)(2,1)} %param.30) | copy-start | bytes 73732
  35.4 7.9 %copy-start.11 = (bf16[2,8,3,256]{3,1,2,0:T(8,128)(2,1)S(1)}, bf16[2,8,3,256]{3,1,2,0:T(8,128)(2,1)}, u32[]{:S(2)}) copy-start(bf16[2,8,3,256]{3,1,2,0:T(8,128)(2,1)} %param.31) | copy-start | bytes 73732
  35.4 8.6 %copy-start.13 = (f32[2,4]{1,0:T(2,128)S(1)}, f32[2,4]{1,0:T(2,128)}, u32[]{:S(2)}) copy-start(f32[2,4]{1,0:T(2,128)} %param.27) | copy-start | bytes 100
  35.4 8.5 %copy-start.14 = (f32[2,4]{1,0:T(2,128)S(1)}, f32[2,4]{1,0:T(2,128)}, u32[]{:S(2)}) copy-start(f32[2,4]{1,0:T(2,128)} %param.26) | copy-start | bytes 100
  35.4 8.5 %copy-start.15 = (f32[2,4]{1,0:T(2,128)S(1)}, f32[2,4]{1,0:T(2,128)}, u32[]{:S(2)}) copy-start(f32[2,4]{1,0:T(2,128)} %param.25) | copy-start | bytes 100
  36.1 64.0 %all-to-all-start.1 = ((bf16[16,2,2,4,64,128]{5,4,3,2,1,0:T(8,128)(2,1)}), bf16[16,2,2,4,64,128]{5,4,3,2,1,0:T(8,128)(2,1)}, u32[]{:S(2)}, u32[]{:S(2)}) async-start(bf16[16,2,2,4,64,128]{5,4,3,2,1,0:T(8,128)(2,1)} %starts.1), calls=%async_computation.1 | async-start | bytes 8388608 | tf_op jit(solution)/shard_map/all_to_all | solution.py:504
  53.6 51.5 %copy-start = (f32[2,8,4,64,128]{4,3,2,1,0:T(8,128)S(1)}, f32[2,8,4,64,128]{4,3,2,1,0:T(8,128)}, u32[]{:S(2)}) copy-start(f32[2,8,4,64,128]{4,3,2,1,0:T(8,128)} %state_ref.5) | copy-start | bytes 6291460
  100.1 15.9 %all-to-all-start.2 = ((bf16[16,112,256]{2,1,0:T(8,128)(2,1)}), bf16[16,112,256]{2,1,0:T(8,128)(2,1)S(1)}, u32[]{:S(2)}, u32[]{:S(2)}) async-start(bf16[16,112,256]{2,1,0:T(8,128)(2,1)} %get-tuple-element.45), calls=%async_computation.2 | async-start | bytes 1835008 | tf_op jit(solution)/shard_map/all_to_all | solution.py:504
  105.1 1.0 copy-start.2
  106.1 0.9 copy-start.4
  107.0 0.8 copy-start.6
  117.0 14.9 %all-to-all-start.3 = ((bf16[16,64,256]{2,1,0:T(8,128)(2,1)}), bf16[16,64,256]{2,1,0:T(8,128)(2,1)S(1)}, u32[]{:S(2)}, u32[]{:S(2)}) async-start(bf16[16,64,256]{2,1,0:T(8,128)(2,1)} %get-tuple-element.50), calls=%async_computation.3 | async-start | bytes 1048576 | tf_op jit(solution)/shard_map/all_to_all | solution.py:504
  131.9 0.8 copy-start.9
  132.7 12.1 %copy-start.1 = (f32[2,8,4,64,128]{4,3,2,1,0:T(8,128)S(1)}, f32[2,8,4,64,128]{4,3,2,1,0:T(8,128)}, u32[]{:S(2)}) copy-start(f32[2,8,4,64,128]{4,3,2,1,0:T(8,128)} %state_ref.5) | copy-start | bytes 6291460
  139.1 16.2 %all-to-all-start.4 = ((bf16[16,112,256]{2,1,0:T(8,128)(2,1)}), bf16[16,112,256]{2,1,0:T(8,128)(2,1)S(1)}, u32[]{:S(2)}, u32[]{:S(2)}) async-start(bf16[16,112,256]{2,1,0:T(8,128)(2,1)} %get-tuple-element.55), calls=%async_computation.4 | async-start | bytes 1835008 | tf_op jit(solution)/shard_map/all_to_all | solution.py:504
  144.8 1.0 copy-start.3
  145.7 0.9 copy-start.5
  146.6 0.8 copy-start.7
  155.5 9.2 %collective-permute-start.1 = (bf16[64,256]{1,0:T(8,128)(2,1)S(1)}, bf16[64,256]{1,0:T(8,128)(2,1)S(1)}, u32[]{:S(2)}, u32[]{:S(2)}) collective-permute-start(bf16[64,256]{1,0:T(8,128)(2,1)S(1)} %update_last.1), channel_id=1, source_target_pairs={{0,0},{8,1},{16,2},{24,3},{32,4},{40,5},{48,6},{56,7},{64,8},{72,9... | collective-permute-start | bytes 98312 | tf_op jit(solution)/shard_map/ppermute | solution.py:579
Sparse Core Ops, SparseCore 0:
  15.8 37.7 all-gather.4
  55.3 34.2 all-gather.6

commit v8 on v6

--- a/solution.py
+++ b/solution.py
@@ -12,7 +12,7 @@
 COLS = 16
 BF = jnp.bfloat16
 F32 = jnp.float32
-SUM_ROWS = 16
+SUM_ROWS = 8
 VMEM_BYTES = 58 * 1024 * 1024
 SMALL_VMEM_BYTES = 12 * 1024 * 1024
 
@@ -40,7 +40,8 @@
 
 
 def pack(layer, inner, proj, step, gain, out):
-    rows, width = inner.shape[2:]
+    planes = jnp.transpose(inner[layer], (1, 0, 2))
+    rows, width = planes.shape[1:]
     cols = 2 * width + proj.shape[2] + 128 + out.shape[2]
 
     def layer_of(shape):
@@ -51,7 +52,7 @@
         name="pack%d" % layer,
         grid=(1,),
         in_specs=[
-            layer_of(inner.shape),
+            pl.BlockSpec(planes.shape, lambda i: (0, 0, 0)),
             layer_of(proj.shape),
             layer_of(step.shape),
             pl.BlockSpec(gain.shape, lambda i: (0, 0)),
@@ -62,7 +63,7 @@
         compiler_params=pltpu.CompilerParams(
             dimension_semantics=("arbitrary",), vmem_limit_bytes=VMEM_BYTES
         ),
-    )(inner, proj, step, gain, out)
+    )(planes, proj, step, gain, out)
 
 
 def route(q, ints_ref, requests):
@@ -528,7 +529,7 @@
 
     block = lax.ppermute(hidden_states, ("row", "col"), there)
     raw = (
-        jnp.transpose(inner_weight, (0, 2, 1, 3)),
+        inner_weight,
         proj_weight,
         jnp.transpose(step_weight, (0, 2, 1)),
         input_gain,

time: 176 us -> 174 us (0.989)
    unnamed x39 -> x41, local copies, waits for them, and re-layouts: 9.29 us -> 8.13 us
  transfers between devices with their start and end apart: 9 -> 9, of which waited for: 6 -> 6; matrix products, arithmetic and copies ran while one was open for 3% -> 4% of each run, Pallas kernels for 27% -> 27%
where the time goes in v8:
time: 174 us; the launch traced here: 172 us
  Pallas kernels  46.6 us (27%)
  starting transfers between devices  44.5 us (26%)
  waiting for transfers between devices  39.8 us (23%)
  blocking collectives  14.6 us (8%)
  between operations  14.2 us (8%)
  local copies, waits for them, and re-layouts  11.7 us (7%)
    all_to_all x5, starting transfers between devices, swap(): return lax.all_to_all(x, 'col', 0, 0, tiled=True)  36 us
    all_to_all x5, waiting for transfers between devices, swap(): return lax.all_to_all(x, 'col', 0, 0, tiled=True)  30.8 us
    pallas_call x2, Pallas kernels, states(): pl.pallas_call(states_body, name='states%d' % layer, grid=(requests,), in...  15.6 us
    all_to_all x1, blocking collectives, swap(): return lax.all_to_all(x, 'col', 0, 0, tiled=True)  14.6 us
    pallas_call x2, Pallas kernels, front(): pl.pallas_call(lambda *refs: front_body(layer, *refs), name='front%d' % l...  12.8 us
    unnamed x41, local copies, waits for them, and re-layouts  8.13 us
    all_gather x1, waiting for transfers between devices, local(): weights = [lax.all_gather(first, 'row', axis=0)]  7.55 us
    pallas_call x2, Pallas kernels, owned_states(): pl.pallas_call(lambda *refs: owned_body(layer, *refs), name='owned%d' % l...  7.44 us
  transfers between devices with their start and end apart: 9, of which 6 were waited for; matrix products, arithmetic and copies ran while one was open for 4% of the time, Pallas kernels for 27%

profile of v8, /device:TPU:32, one launch (start us, length us, event | category | flops | bytes accessed | tf_op | source)
XLA Modules:
  0.0 172.0 jit_solution(1087727567431138281)
XLA Ops:
  7.2 0.0 all-gather.5.cloned.1.call-start
  7.2 3.0 %collective-permute-start = (bf16[64,256]{1,0:T(8,128)(2,1)}, bf16[64,256]{1,0:T(8,128)(2,1)S(1)}, u32[]{:S(2)}, u32[]{:S(2)}) collective-permute-start(bf16[64,256]{1,0:T(8,128)(2,1)} %param.18), channel_id=1, source_target_pairs={{0,0},{1,8},{2,16},{3,24},{4,32},{5,40},{6,48},{7,56},{8,64},{9,72... | collective-permute-start | bytes 98312 | tf_op jit(solution)/shard_map/ppermute | solution.py:530
  10.3 1.1 slice.6
  11.4 0.7 copy.39
  12.1 2.1 %pack0.1 = bf16[256,1152]{1,0:T(8,128)(2,1)} custom-call(bf16[2,256,256]{2,1,0:T(8,128)(2,1)} %bitcast.18, bf16[2,256,256]{2,1,0:T(8,128)(2,1)} %refs_1_.2, bf16[2,4,256]{2,1,0:T(4,128)(2,1)} %bitcast.19, f32[2,256]{1,0:T(2,128)} %refs_3_.2, bf16[2,256,256]{2,1,0:T(8,128)(2,1)} %refs_4_.4), custom_call_target="tpu_custom_call" | custom-call | tf_op jit(solution)/shard_map/pack0/pallas_call | solution.py:50
  14.3 1.4 collective-permute-done.refs_2_
  15.7 0.9 broadcast_in_dim.4
  16.5 10.4 %all-to-all-start = ((bf16[16,64,256]{2,1,0:T(8,128)(2,1)}), bf16[16,64,256]{2,1,0:T(8,128)(2,1)S(1)}, u32[]{:S(2)}, u32[]{:S(2)}) async-start(bf16[16,64,256]{2,1,0:T(8,128)(2,1)} %broadcast_in_dim.4), calls=%async_computation | async-start | bytes 1048576 | tf_op jit(solution)/shard_map/all_to_all | solution.py:491
  26.9 0.0 all-gather.7.cloned.1.call-start
  27.0 0.1 copy.30
  27.1 0.1 reshape.18
  27.2 0.7 concatenate.6.ints_ref.refs_0_
  27.8 3.1 %starts1.1 = bf16[16,2,4,64,128]{4,3,2,1,0:T(8,128)(2,1)} custom-call(s32[26]{0:T(128)} %concatenate.6.ints_ref.refs_0_, f32[2,8,4,64,128]{4,3,2,1,0:T(8,128)} %state_ref.7), custom_call_target="tpu_custom_call" | custom-call | tf_op jit(solution)/shard_map/starts1/pallas_call | solution.py:357
  30.9 3.0 %starts0.1 = bf16[16,2,4,64,128]{4,3,2,1,0:T(8,128)(2,1)} custom-call(s32[26]{0:T(128)} %concatenate.6.ints_ref.refs_0_, f32[2,8,4,64,128]{4,3,2,1,0:T(8,128)} %state_ref.7), custom_call_target="tpu_custom_call" | custom-call | tf_op jit(solution)/shard_map/starts0/pallas_call | solution.py:357
  34.0 0.1 copy.32
  34.0 0.7 slice_bitcast_fusion.refs_0_
  34.8 2.2 %pack1.1 = bf16[256,1152]{1,0:T(8,128)(2,1)} custom-call(bf16[2,256,256]{2,1,0:T(8,128)(2,1)} %slice_bitcast_fusion.refs_0_, bf16[2,256,256]{2,1,0:T(8,128)(2,1)} %refs_1_.2, bf16[2,4,256]{2,1,0:T(4,128)(2,1)} %bitcast.20, f32[2,256]{1,0:T(2,128)} %refs_3_.2, bf16[2,256,256]{2,1,0:T(8,128)(2,1)} %refs_4_.4), custom_call_target="tpu_custom_call" | custom-call | tf_op jit(solution)/shard_map/pack1/pallas_call | solution.py:50
  36.9 0.0 all-gather.7.cloned.1.call-update
  37.0 7.2 %all-to-all-start.1 = ((bf16[16,2,4,64,128]{4,3,2,1,0:T(8,128)(2,1)}), bf16[16,2,4,64,128]{4,3,2,1,0:T(8,128)(2,1)}, u32[]{:S(2)}, u32[]{:S(2)}) async-start(bf16[16,2,4,64,128]{4,3,2,1,0:T(8,128)(2,1)} %starts0.1), calls=%async_computation.1 | async-start | bytes 4194304 | tf_op jit(solution)/shard_map/all_to_all | solution.py:491
  44.2 0.6 copy.33.refs_7_
  44.8 0.6 copy.34.refs_8_
  45.5 0.6 pad_maximum_fusion.refs_1_
  46.1 7.5 %all-gather.5.cloned.1.call-done = bf16[2048,1152]{1,0:T(8,128)(2,1)} async-done(((bf16[256,1152]{1,0:T(8,128)(2,1)}), bf16[2048,1152]{1,0:T(8,128)(2,1)}) %all-gather.5.cloned.1.call-update) | async-done | bytes 4718608 | tf_op jit(solution)/shard_map/all_gather | solution.py:539
  53.6 6.4 %front0.1 = (bf16[16,104,256]{2,1,0:T(8,128)(2,1)}, f32[128,256]{1,0:T(8,128)}, f32[128,128]{1,0:T(8,128)}, f32[128,512]{1,0:T(8,128)}) custom-call(s32[26]{0:T(128)} %concatenate.6.ints_ref.refs_0_, f32[2,12]{1,0:T(2,128)} %pad_maximum_fusion.refs_1_, bf16[16,64,256]{2,1,0:T(8,128)(2,1)} %copy-done.8, bf16[8,256,1152]{2,1,0:T(8,128)(2,1)} %bitcast.16, ...), custom_call_target="tpu_custom_call" | custom-call | tf_op jit(solution)/shard_map/front0/pallas_call | solution.py:267
  60.0 10.9 %all-to-all-done.1.refs_0_ = bf16[16,2,4,64,128]{4,3,2,1,0:T(8,128)(2,1)} async-done(((bf16[16,2,4,64,128]{4,3,2,1,0:T(8,128)(2,1)}), bf16[16,2,4,64,128]{4,3,2,1,0:T(8,128)(2,1)}, u32[]{:S(2)}, u32[]{:S(2)}) %all-to-all-start.1) | async-done | bytes 2097184 | tf_op jit(solution)/shard_map/all_to_all | solution.py:491
  70.9 5.8 %all-to-all-start.2 = ((bf16[16,104,256]{2,1,0:T(8,128)(2,1)}), bf16[16,104,256]{2,1,0:T(8,128)(2,1)S(1)}, u32[]{:S(2)}, u32[]{:S(2)}) async-start(bf16[16,104,256]{2,1,0:T(8,128)(2,1)} %get-tuple-element.49), calls=%async_computation.2 | async-start | bytes 1703936 | tf_op jit(solution)/shard_map/all_to_all | solution.py:491
  76.7 0.9 copy-done.3
  77.7 0.9 copy-done.5
  78.6 0.8 copy-done.7
  79.4 7.8 %states0.1.rest_0_ = bf16[2,8,16,4,64,128]{5,4,3,2,1,0:T(8,128)(2,1)} custom-call(f32[128,256]{1,0:T(8,128)S(1)} %copy-done.5, f32[128,128]{1,0:T(8,128)S(1)} %copy-done.7, f32[128,512]{1,0:T(8,128)S(1)} %copy-done.3, f32[2,8,4,64,128]{4,3,2,1,0:T(8,128)S(1)} %copy-done), custom_call_target="tpu_custom_call" | custom-call | tf_op jit(solution)/shard_map/states0/pallas_call | solution.py:326
  87.2 1.6 all-to-all-done.2.refs_0_.refs_1_
  88.9 0.2 update_spread.1
  89.1 14.6 %all_to_all.30.refs_2_ = bf16[16,64,256]{2,1,0:T(8,128)(2,1)} all-to-all(bf16[16,64,256]{2,1,0:T(8,128)(2,1)S(1)} %get-tuple-element.54), channel_id=1, replica_groups=mesh['row'=8,'col'=16] {'col'}, dimensions={0} | all-to-all | bytes 1048576 | tf_op jit(solution)/shard_map/all_to_all | solution.py:491
  103.6 6.7 %all-to-all-start.4 = ((bf16[16,2,4,64,128]{4,3,2,1,0:T(8,128)(2,1)}), bf16[16,2,4,64,128]{4,3,2,1,0:T(8,128)(2,1)}, u32[]{:S(2)}, u32[]{:S(2)}) async-start(bf16[16,2,4,64,128]{4,3,2,1,0:T(8,128)(2,1)} %starts1.1), calls=%async_computation.4 | async-start | bytes 4194304 | tf_op jit(solution)/shard_map/all_to_all | solution.py:491
  110.3 3.7 %owned0.1.refs_2_ = bf16[2,2,64,64,128]{4,3,2,1,0:T(8,128)(2,1)} custom-call(bf16[16,2,4,64,128]{4,3,2,1,0:T(8,128)(2,1)} %all-to-all-done.1.refs_0_, bf16[16,104,256]{2,1,0:T(8,128)(2,1)S(1)} %all-to-all-done.2.refs_0_.refs_1_), custom_call_target="tpu_custom_call" | custom-call | tf_op jit(solution)/shard_map/owned0/pallas_call | solution.py:432
  114.0 0.0 all-gather.7.cloned.1.call-done
  114.1 6.4 %front1.1 = (bf16[16,104,256]{2,1,0:T(8,128)(2,1)}, f32[128,256]{1,0:T(8,128)}, f32[128,128]{1,0:T(8,128)}, f32[128,512]{1,0:T(8,128)}) custom-call(s32[26]{0:T(128)} %concatenate.6.ints_ref.refs_0_, f32[2,12]{1,0:T(2,128)} %pad_maximum_fusion.refs_1_, bf16[16,64,256]{2,1,0:T(8,128)(2,1)} %all_to_all.30.refs_2_, bf16[8,256,1152]{2,1,0:T(8,128)(2,1)} %bitcast.17, ...), custom_call_target="tpu_custom_call" | custom-call | tf_op jit(solution)/shard_map/front1/pallas_call | solution.py:267
  120.4 16.7 %all-to-all-done.4.refs_0_ = bf16[16,2,4,64,128]{4,3,2,1,0:T(8,128)(2,1)} async-done(((bf16[16,2,4,64,128]{4,3,2,1,0:T(8,128)(2,1)}), bf16[16,2,4,64,128]{4,3,2,1,0:T(8,128)(2,1)}, u32[]{:S(2)}, u32[]{:S(2)}) %all-to-all-start.4) | async-done | bytes 2097184 | tf_op jit(solution)/shard_map/all_to_all | solution.py:491
  137.1 5.9 %all-to-all-start.5 = ((bf16[16,104,256]{2,1,0:T(8,128)(2,1)}), bf16[16,104,256]{2,1,0:T(8,128)(2,1)S(1)}, u32[]{:S(2)}, u32[]{:S(2)}) async-start(bf16[16,104,256]{2,1,0:T(8,128)(2,1)} %get-tuple-element.61), calls=%async_computation.5 | async-start | bytes 1703936 | tf_op jit(solution)/shard_map/all_to_all | solution.py:491
  143.0 0.9 copy-done.2
  144.0 0.9 copy-done.4
  144.9 0.8 copy-done.6
  145.7 7.8 %states1.1 = bf16[2,8,16,4,64,128]{5,4,3,2,1,0:T(8,128)(2,1)} custom-call(f32[128,256]{1,0:T(8,128)S(1)} %copy-done.4, f32[128,128]{1,0:T(8,128)S(1)} %copy-done.6, f32[128,512]{1,0:T(8,128)S(1)} %copy-done.2, f32[2,8,4,64,128]{4,3,2,1,0:T(8,128)S(1)} %copy-done.1, bf16[2,8,16,4,64,128]{5,4,3,2,1,0:T(8,128)(2,1)} %states0.1.rest_0_), custom_call_target="tpu_custom_call", output_to_operand_aliasing={{}: (4, {})} | custom-call | tf_op jit(solution)/shard_map/states1/pallas_call | solution.py:326
  153.5 1.7 all-to-all-done.5.refs_0_.refs_1_
  155.2 0.2 update_last.1
  155.4 5.4 %collective-permute-start.1 = (bf16[64,256]{1,0:T(8,128)(2,1)S(1)}, bf16[64,256]{1,0:T(8,128)(2,1)S(1)}, u32[]{:S(2)}, u32[]{:S(2)}) collective-permute-start(bf16[64,256]{1,0:T(8,128)(2,1)S(1)} %update_last.1), channel_id=1, source_target_pairs={{0,0},{8,1},{16,2},{24,3},{32,4},{40,5},{48,6},{56,7},{64,8},{72,9... | collective-permute-start | bytes 98312 | tf_op jit(solution)/shard_map/ppermute | solution.py:567
  160.8 3.7 %owned1.1 = bf16[2,2,64,64,128]{4,3,2,1,0:T(8,128)(2,1)} custom-call(bf16[16,2,4,64,128]{4,3,2,1,0:T(8,128)(2,1)} %all-to-all-done.4.refs_0_, bf16[16,104,256]{2,1,0:T(8,128)(2,1)S(1)} %all-to-all-done.5.refs_0_.refs_1_, bf16[2,2,64,64,128]{4,3,2,1,0:T(8,128)(2,1)} %owned0.1.refs_2_), custom_call_target="tpu_custom_call", output_to_operand_aliasing={{}: (2, {})} | custom-call | tf_op jit(solution)/shard_map/owned1/pallas_call | solution.py:432
  164.6 0.6 copy.43
  (33 shorter events, 0.1 us)
Async XLA Ops:
  7.2 19.8 %copy-start.12 = (s32[4,2]{0,1:T(2,128)S(1)}, s32[4,2]{0,1:T(2,128)}, u32[]{:S(2)}) copy-start(s32[4,2]{0,1:T(2,128)} %param.35) | copy-start | bytes 100
  7.2 20.0 %copy-start.17 = (s32[8]{0:T(128)S(1)}, s32[8]{0:T(128)}, u32[]{:S(2)}) copy-start(s32[8]{0:T(128)} %param.34) | copy-start | bytes 100
  7.2 20.0 %copy-start.16 = (s32[8]{0:T(128)S(1)}, s32[8]{0:T(128)}, u32[]{:S(2)}) copy-start(s32[8]{0:T(128)} %param.33) | copy-start | bytes 100
  7.2 46.4 %all-gather.5.cloned.1.call-start = ((), (), s32[]{:S(2)}) async-start(), calls=%async_computation.6 | async-start | bytes 5308416 | tf_op jit(solution)/shard_map/all_gather | solution.py:539
  7.2 8.4 %collective-permute-start = (bf16[64,256]{1,0:T(8,128)(2,1)}, bf16[64,256]{1,0:T(8,128)(2,1)S(1)}, u32[]{:S(2)}, u32[]{:S(2)}) collective-permute-start(bf16[64,256]{1,0:T(8,128)(2,1)} %param.18), channel_id=1, source_target_pairs={{0,0},{1,8},{2,16},{3,24},{4,32},{5,40},{6,48},{7,56},{8,64},{9,72... | collective-permute-start | bytes 98312 | tf_op jit(solution)/shard_map/ppermute | solution.py:530
  16.5 20.4 %all-to-all-start = ((bf16[16,64,256]{2,1,0:T(8,128)(2,1)}), bf16[16,64,256]{2,1,0:T(8,128)(2,1)S(1)}, u32[]{:S(2)}, u32[]{:S(2)}) async-start(bf16[16,64,256]{2,1,0:T(8,128)(2,1)} %broadcast_in_dim.4), calls=%async_computation | async-start | bytes 1048576 | tf_op jit(solution)/shard_map/all_to_all | solution.py:491
  26.9 87.1 %all-gather.7.cloned.1.call-start = ((), (), s32[]{:S(2)}) async-start(), calls=%async_computation.7 | async-start | bytes 5308416 | tf_op jit(solution)/shard_map/all_gather | solution.py:545
  27.8 6.1 %copy-start.9 = (bf16[2,256,2,256]{3,2,1,0:T(2,128)(2,1)S(1)}, bf16[2,256,2,256]{3,2,1,0:T(2,128)(2,1)}, u32[]{:S(2)}) copy-start(bf16[2,256,2,256]{3,2,1,0:T(2,128)(2,1)} %param.20) | copy-start | bytes 1572868
  33.9 10.3 %copy-start.10 = (bf16[2,8,3,256]{3,1,2,0:T(8,128)(2,1)S(1)}, bf16[2,8,3,256]{3,1,2,0:T(8,128)(2,1)}, u32[]{:S(2)}) copy-start(bf16[2,8,3,256]{3,1,2,0:T(8,128)(2,1)} %param.30) | copy-start | bytes 73732
  33.9 10.9 %copy-start.11 = (bf16[2,8,3,256]{3,1,2,0:T(8,128)(2,1)S(1)}, bf16[2,8,3,256]{3,1,2,0:T(8,128)(2,1)}, u32[]{:S(2)}) copy-start(bf16[2,8,3,256]{3,1,2,0:T(8,128)(2,1)} %param.31) | copy-start | bytes 73732
  33.9 11.5 %copy-start.13 = (f32[2,4]{1,0:T(2,128)S(1)}, f32[2,4]{1,0:T(2,128)}, u32[]{:S(2)}) copy-start(f32[2,4]{1,0:T(2,128)} %param.27) | copy-start | bytes 100
  33.9 11.5 %copy-start.14 = (f32[2,4]{1,0:T(2,128)S(1)}, f32[2,4]{1,0:T(2,128)}, u32[]{:S(2)}) copy-start(f32[2,4]{1,0:T(2,128)} %param.26) | copy-start | bytes 100
  34.0 11.5 %copy-start.15 = (f32[2,4]{1,0:T(2,128)S(1)}, f32[2,4]{1,0:T(2,128)}, u32[]{:S(2)}) copy-start(f32[2,4]{1,0:T(2,128)} %param.25) | copy-start | bytes 100
  36.9 16.7 %copy-start.8 = (bf16[16,64,256]{2,1,0:T(8,128)(2,1)}, bf16[16,64,256]{2,1,0:T(8,128)(2,1)S(1)}, u32[]{:S(2)}) copy-start(bf16[16,64,256]{2,1,0:T(8,128)(2,1)S(1)} %all-to-all-done.refs_2_) | copy-start | bytes 1572868
  37.0 33.9 %all-to-all-start.1 = ((bf16[16,2,4,64,128]{4,3,2,1,0:T(8,128)(2,1)}), bf16[16,2,4,64,128]{4,3,2,1,0:T(8,128)(2,1)}, u32[]{:S(2)}, u32[]{:S(2)}) async-start(bf16[16,2,4,64,128]{4,3,2,1,0:T(8,128)(2,1)} %starts0.1), calls=%async_computation.1 | async-start | bytes 4194304 | tf_op jit(solution)/shard_map/all_to_all | solution.py:491
  53.6 23.1 %copy-start = (f32[2,8,4,64,128]{4,3,2,1,0:T(8,128)S(1)}, f32[2,8,4,64,128]{4,3,2,1,0:T(8,128)}, u32[]{:S(2)}) copy-start(f32[2,8,4,64,128]{4,3,2,1,0:T(8,128)} %state_ref.7) | copy-start | bytes 6291460
  70.9 18.0 %all-to-all-start.2 = ((bf16[16,104,256]{2,1,0:T(8,128)(2,1)}), bf16[16,104,256]{2,1,0:T(8,128)(2,1)S(1)}, u32[]{:S(2)}, u32[]{:S(2)}) async-start(bf16[16,104,256]{2,1,0:T(8,128)(2,1)} %get-tuple-element.49), calls=%async_computation.2 | async-start | bytes 1703936 | tf_op jit(solution)/shard_map/all_to_all | solution.py:491
  76.7 1.0 copy-start.3
  77.7 0.9 copy-start.5
  78.6 0.8 copy-start.7
  103.6 33.5 %all-to-all-start.4 = ((bf16[16,2,4,64,128]{4,3,2,1,0:T(8,128)(2,1)}), bf16[16,2,4,64,128]{4,3,2,1,0:T(8,128)(2,1)}, u32[]{:S(2)}, u32[]{:S(2)}) async-start(bf16[16,2,4,64,128]{4,3,2,1,0:T(8,128)(2,1)} %starts1.1), calls=%async_computation.4 | async-start | bytes 4194304 | tf_op jit(solution)/shard_map/all_to_all | solution.py:491
  114.1 29.0 %copy-start.1 = (f32[2,8,4,64,128]{4,3,2,1,0:T(8,128)S(1)}, f32[2,8,4,64,128]{4,3,2,1,0:T(8,128)}, u32[]{:S(2)}) copy-start(f32[2,8,4,64,128]{4,3,2,1,0:T(8,128)} %state_ref.7) | copy-start | bytes 6291460
  137.1 18.1 %all-to-all-start.5 = ((bf16[16,104,256]{2,1,0:T(8,128)(2,1)}), bf16[16,104,256]{2,1,0:T(8,128)(2,1)S(1)}, u32[]{:S(2)}, u32[]{:S(2)}) async-start(bf16[16,104,256]{2,1,0:T(8,128)(2,1)} %get-tuple-element.61), calls=%async_computation.5 | async-start | bytes 1703936 | tf_op jit(solution)/shard_map/all_to_all | solution.py:491
  143.0 1.0 copy-start.2
  144.0 0.9 copy-start.4
  144.9 0.8 copy-start.6
  155.4 9.2 %collective-permute-start.1 = (bf16[64,256]{1,0:T(8,128)(2,1)S(1)}, bf16[64,256]{1,0:T(8,128)(2,1)S(1)}, u32[]{:S(2)}, u32[]{:S(2)}) collective-permute-start(bf16[64,256]{1,0:T(8,128)(2,1)S(1)} %update_last.1), channel_id=1, source_target_pairs={{0,0},{8,1},{16,2},{24,3},{32,4},{40,5},{48,6},{56,7},{64,8},{72,9... | collective-permute-start | bytes 98312 | tf_op jit(solution)/shard_map/ppermute | solution.py:567
Sparse Core Ops, SparseCore 0:
  15.8 37.7 all-gather.4
  55.3 34.2 all-gather.6

commit v9 on v8

--- a/solution.py
+++ b/solution.py
@@ -373,7 +373,7 @@
 def owned_body(layer, starts_ref, received_ref, *rest):
     out_ref, stage, b_s, sems = rest[-4:]
     cols, slots, heads, head_size, state_size = starts_ref.shape
-    group = 4
+    group = 2
     dx_rows = slots * S
     misc_at = received_ref.shape[1] - SUM_ROWS
     dx_at = misc_at - dx_rows
@@ -440,7 +440,7 @@
         scratch_shapes=[
             pltpu.VMEM((SEND_CAP, all_heads, head_size, state_size), BF),
             pltpu.VMEM((SEND_CAP * S, SEND_CAP * state_size), F32),
-            pltpu.SemaphoreType.DMA((SEND_CAP * COLS // 4,)),
+            pltpu.SemaphoreType.DMA((SEND_CAP * COLS // 2,)),
         ],
         input_output_aliases=aliases,
         compiler_params=pltpu.CompilerParams(vmem_limit_bytes=SMALL_VMEM_BYTES),

time: 174 us -> 175 us (level)
  no operation moved by 1% of the time
where the time goes in v9:
time: 175 us; the launch traced here: 172 us
  Pallas kernels  46.4 us (27%)
  starting transfers between devices  44.6 us (25%)
  waiting for transfers between devices  39.9 us (23%)
  blocking collectives  14.6 us (8%)
  between operations  14.2 us (8%)
  local copies, waits for them, and re-layouts  11.7 us (7%)
    all_to_all x5, starting transfers between devices, swap(): return lax.all_to_all(x, 'col', 0, 0, tiled=True)  36 us
    all_to_all x5, waiting for transfers between devices, swap(): return lax.all_to_all(x, 'col', 0, 0, tiled=True)  30.9 us
    pallas_call x2, Pallas kernels, states(): pl.pallas_call(states_body, name='states%d' % layer, grid=(requests,), in...  15.6 us
    all_to_all x1, blocking collectives, swap(): return lax.all_to_all(x, 'col', 0, 0, tiled=True)  14.6 us
    pallas_call x2, Pallas kernels, front(): pl.pallas_call(lambda *refs: front_body(layer, *refs), name='front%d' % l...  12.8 us
    unnamed x41, local copies, waits for them, and re-layouts  8.13 us
    all_gather x1, waiting for transfers between devices, local(): weights = [lax.all_gather(first, 'row', axis=0)]  7.54 us
    pallas_call x2, Pallas kernels, owned_states(): pl.pallas_call(lambda *refs: owned_body(layer, *refs), name='owned%d' % l...  7.18 us
  transfers between devices with their start and end apart: 9, of which 6 were waited for; matrix products, arithmetic and copies ran while one was open for 4% of the time, Pallas kernels for 27%

profile of v9, /device:TPU:32, one launch (start us, length us, event | category | flops | bytes accessed | tf_op | source)
XLA Modules:
  0.0 171.9 jit_solution(10966432890119799229)
XLA Ops:
  7.2 0.0 all-gather.5.cloned.1.call-start
  7.2 3.0 %collective-permute-start = (bf16[64,256]{1,0:T(8,128)(2,1)}, bf16[64,256]{1,0:T(8,128)(2,1)S(1)}, u32[]{:S(2)}, u32[]{:S(2)}) collective-permute-start(bf16[64,256]{1,0:T(8,128)(2,1)} %param.18), channel_id=1, source_target_pairs={{0,0},{1,8},{2,16},{3,24},{4,32},{5,40},{6,48},{7,56},{8,64},{9,72... | collective-permute-start | bytes 98312 | tf_op jit(solution)/shard_map/ppermute | solution.py:530
  10.3 1.1 slice.6
  11.4 0.7 copy.39
  12.1 2.1 %pack0.1 = bf16[256,1152]{1,0:T(8,128)(2,1)} custom-call(bf16[2,256,256]{2,1,0:T(8,128)(2,1)} %bitcast.18, bf16[2,256,256]{2,1,0:T(8,128)(2,1)} %refs_1_.2, bf16[2,4,256]{2,1,0:T(4,128)(2,1)} %bitcast.19, f32[2,256]{1,0:T(2,128)} %refs_3_.2, bf16[2,256,256]{2,1,0:T(8,128)(2,1)} %refs_4_.4), custom_call_target="tpu_custom_call" | custom-call | tf_op jit(solution)/shard_map/pack0/pallas_call | solution.py:50
  14.3 1.4 collective-permute-done.refs_2_
  15.7 0.9 broadcast_in_dim.4
  16.5 10.4 %all-to-all-start = ((bf16[16,64,256]{2,1,0:T(8,128)(2,1)}), bf16[16,64,256]{2,1,0:T(8,128)(2,1)S(1)}, u32[]{:S(2)}, u32[]{:S(2)}) async-start(bf16[16,64,256]{2,1,0:T(8,128)(2,1)} %broadcast_in_dim.4), calls=%async_computation | async-start | bytes 1048576 | tf_op jit(solution)/shard_map/all_to_all | solution.py:491
  26.9 0.0 all-gather.7.cloned.1.call-start
  27.0 0.1 copy.30
  27.1 0.1 reshape.18
  27.2 0.7 concatenate.6.ints_ref.refs_0_
  27.8 3.1 %starts1.1 = bf16[16,2,4,64,128]{4,3,2,1,0:T(8,128)(2,1)} custom-call(s32[26]{0:T(128)} %concatenate.6.ints_ref.refs_0_, f32[2,8,4,64,128]{4,3,2,1,0:T(8,128)} %state_ref.7), custom_call_target="tpu_custom_call" | custom-call | tf_op jit(solution)/shard_map/starts1/pallas_call | solution.py:357
  30.9 3.0 %starts0.1 = bf16[16,2,4,64,128]{4,3,2,1,0:T(8,128)(2,1)} custom-call(s32[26]{0:T(128)} %concatenate.6.ints_ref.refs_0_, f32[2,8,4,64,128]{4,3,2,1,0:T(8,128)} %state_ref.7), custom_call_target="tpu_custom_call" | custom-call | tf_op jit(solution)/shard_map/starts0/pallas_call | solution.py:357
  34.0 0.1 copy.32
  34.1 0.7 slice_bitcast_fusion.refs_0_
  34.8 2.2 %pack1.1 = bf16[256,1152]{1,0:T(8,128)(2,1)} custom-call(bf16[2,256,256]{2,1,0:T(8,128)(2,1)} %slice_bitcast_fusion.refs_0_, bf16[2,256,256]{2,1,0:T(8,128)(2,1)} %refs_1_.2, bf16[2,4,256]{2,1,0:T(4,128)(2,1)} %bitcast.20, f32[2,256]{1,0:T(2,128)} %refs_3_.2, bf16[2,256,256]{2,1,0:T(8,128)(2,1)} %refs_4_.4), custom_call_target="tpu_custom_call" | custom-call | tf_op jit(solution)/shard_map/pack1/pallas_call | solution.py:50
  37.0 0.0 all-gather.7.cloned.1.call-update
  37.0 7.2 %all-to-all-start.1 = ((bf16[16,2,4,64,128]{4,3,2,1,0:T(8,128)(2,1)}), bf16[16,2,4,64,128]{4,3,2,1,0:T(8,128)(2,1)}, u32[]{:S(2)}, u32[]{:S(2)}) async-start(bf16[16,2,4,64,128]{4,3,2,1,0:T(8,128)(2,1)} %starts0.1), calls=%async_computation.1 | async-start | bytes 4194304 | tf_op jit(solution)/shard_map/all_to_all | solution.py:491
  44.2 0.6 copy.33.refs_7_
  44.9 0.6 copy.34.refs_8_
  45.5 0.6 pad_maximum_fusion.refs_1_
  46.1 7.5 %all-gather.5.cloned.1.call-done = bf16[2048,1152]{1,0:T(8,128)(2,1)} async-done(((bf16[256,1152]{1,0:T(8,128)(2,1)}), bf16[2048,1152]{1,0:T(8,128)(2,1)}) %all-gather.5.cloned.1.call-update) | async-done | bytes 4718608 | tf_op jit(solution)/shard_map/all_gather | solution.py:539
  53.6 6.4 %front0.1 = (bf16[16,104,256]{2,1,0:T(8,128)(2,1)}, f32[128,256]{1,0:T(8,128)}, f32[128,128]{1,0:T(8,128)}, f32[128,512]{1,0:T(8,128)}) custom-call(s32[26]{0:T(128)} %concatenate.6.ints_ref.refs_0_, f32[2,12]{1,0:T(2,128)} %pad_maximum_fusion.refs_1_, bf16[16,64,256]{2,1,0:T(8,128)(2,1)} %copy-done.8, bf16[8,256,1152]{2,1,0:T(8,128)(2,1)} %bitcast.16, ...), custom_call_target="tpu_custom_call" | custom-call | tf_op jit(solution)/shard_map/front0/pallas_call | solution.py:267
  60.0 10.8 %all-to-all-done.1.refs_0_ = bf16[16,2,4,64,128]{4,3,2,1,0:T(8,128)(2,1)} async-done(((bf16[16,2,4,64,128]{4,3,2,1,0:T(8,128)(2,1)}), bf16[16,2,4,64,128]{4,3,2,1,0:T(8,128)(2,1)}, u32[]{:S(2)}, u32[]{:S(2)}) %all-to-all-start.1) | async-done | bytes 2097184 | tf_op jit(solution)/shard_map/all_to_all | solution.py:491
  70.9 5.8 %all-to-all-start.2 = ((bf16[16,104,256]{2,1,0:T(8,128)(2,1)}), bf16[16,104,256]{2,1,0:T(8,128)(2,1)S(1)}, u32[]{:S(2)}, u32[]{:S(2)}) async-start(bf16[16,104,256]{2,1,0:T(8,128)(2,1)} %get-tuple-element.49), calls=%async_computation.2 | async-start | bytes 1703936 | tf_op jit(solution)/shard_map/all_to_all | solution.py:491
  76.7 0.9 copy-done.3
  77.7 0.9 copy-done.5
  78.6 0.8 copy-done.7
  79.4 7.8 %states0.1.rest_0_ = bf16[2,8,16,4,64,128]{5,4,3,2,1,0:T(8,128)(2,1)} custom-call(f32[128,256]{1,0:T(8,128)S(1)} %copy-done.5, f32[128,128]{1,0:T(8,128)S(1)} %copy-done.7, f32[128,512]{1,0:T(8,128)S(1)} %copy-done.3, f32[2,8,4,64,128]{4,3,2,1,0:T(8,128)S(1)} %copy-done), custom_call_target="tpu_custom_call" | custom-call | tf_op jit(solution)/shard_map/states0/pallas_call | solution.py:326
  87.2 1.6 all-to-all-done.2.refs_0_.refs_1_
  88.8 0.2 update_spread.1
  89.1 14.6 %all_to_all.30.refs_2_ = bf16[16,64,256]{2,1,0:T(8,128)(2,1)} all-to-all(bf16[16,64,256]{2,1,0:T(8,128)(2,1)S(1)} %get-tuple-element.54), channel_id=1, replica_groups=mesh['row'=8,'col'=16] {'col'}, dimensions={0} | all-to-all | bytes 1048576 | tf_op jit(solution)/shard_map/all_to_all | solution.py:491
  103.6 6.7 %all-to-all-start.4 = ((bf16[16,2,4,64,128]{4,3,2,1,0:T(8,128)(2,1)}), bf16[16,2,4,64,128]{4,3,2,1,0:T(8,128)(2,1)}, u32[]{:S(2)}, u32[]{:S(2)}) async-start(bf16[16,2,4,64,128]{4,3,2,1,0:T(8,128)(2,1)} %starts1.1), calls=%async_computation.4 | async-start | bytes 4194304 | tf_op jit(solution)/shard_map/all_to_all | solution.py:491
  110.3 3.6 %owned0.1.refs_2_ = bf16[2,2,64,64,128]{4,3,2,1,0:T(8,128)(2,1)} custom-call(bf16[16,2,4,64,128]{4,3,2,1,0:T(8,128)(2,1)} %all-to-all-done.1.refs_0_, bf16[16,104,256]{2,1,0:T(8,128)(2,1)S(1)} %all-to-all-done.2.refs_0_.refs_1_), custom_call_target="tpu_custom_call" | custom-call | tf_op jit(solution)/shard_map/owned0/pallas_call | solution.py:432
  113.9 0.0 all-gather.7.cloned.1.call-done
  113.9 6.4 %front1.1 = (bf16[16,104,256]{2,1,0:T(8,128)(2,1)}, f32[128,256]{1,0:T(8,128)}, f32[128,128]{1,0:T(8,128)}, f32[128,512]{1,0:T(8,128)}) custom-call(s32[26]{0:T(128)} %concatenate.6.ints_ref.refs_0_, f32[2,12]{1,0:T(2,128)} %pad_maximum_fusion.refs_1_, bf16[16,64,256]{2,1,0:T(8,128)(2,1)} %all_to_all.30.refs_2_, bf16[8,256,1152]{2,1,0:T(8,128)(2,1)} %bitcast.17, ...), custom_call_target="tpu_custom_call" | custom-call | tf_op jit(solution)/shard_map/front1/pallas_call | solution.py:267
  120.3 16.8 %all-to-all-done.4.refs_0_ = bf16[16,2,4,64,128]{4,3,2,1,0:T(8,128)(2,1)} async-done(((bf16[16,2,4,64,128]{4,3,2,1,0:T(8,128)(2,1)}), bf16[16,2,4,64,128]{4,3,2,1,0:T(8,128)(2,1)}, u32[]{:S(2)}, u32[]{:S(2)}) %all-to-all-start.4) | async-done | bytes 2097184 | tf_op jit(solution)/shard_map/all_to_all | solution.py:491
  137.1 5.9 %all-to-all-start.5 = ((bf16[16,104,256]{2,1,0:T(8,128)(2,1)}), bf16[16,104,256]{2,1,0:T(8,128)(2,1)S(1)}, u32[]{:S(2)}, u32[]{:S(2)}) async-start(bf16[16,104,256]{2,1,0:T(8,128)(2,1)} %get-tuple-element.61), calls=%async_computation.5 | async-start | bytes 1703936 | tf_op jit(solution)/shard_map/all_to_all | solution.py:491
  143.0 0.9 copy-done.2
  144.0 0.9 copy-done.4
  144.9 0.8 copy-done.6
  145.7 7.8 %states1.1 = bf16[2,8,16,4,64,128]{5,4,3,2,1,0:T(8,128)(2,1)} custom-call(f32[128,256]{1,0:T(8,128)S(1)} %copy-done.4, f32[128,128]{1,0:T(8,128)S(1)} %copy-done.6, f32[128,512]{1,0:T(8,128)S(1)} %copy-done.2, f32[2,8,4,64,128]{4,3,2,1,0:T(8,128)S(1)} %copy-done.1, bf16[2,8,16,4,64,128]{5,4,3,2,1,0:T(8,128)(2,1)} %states0.1.rest_0_), custom_call_target="tpu_custom_call", output_to_operand_aliasing={{}: (4, {})} | custom-call | tf_op jit(solution)/shard_map/states1/pallas_call | solution.py:326
  153.5 1.7 all-to-all-done.5.refs_0_.refs_1_
  155.2 0.2 update_last.1
  155.4 5.4 %collective-permute-start.1 = (bf16[64,256]{1,0:T(8,128)(2,1)S(1)}, bf16[64,256]{1,0:T(8,128)(2,1)S(1)}, u32[]{:S(2)}, u32[]{:S(2)}) collective-permute-start(bf16[64,256]{1,0:T(8,128)(2,1)S(1)} %update_last.1), channel_id=1, source_target_pairs={{0,0},{8,1},{16,2},{24,3},{32,4},{40,5},{48,6},{56,7},{64,8},{72,9... | collective-permute-start | bytes 98312 | tf_op jit(solution)/shard_map/ppermute | solution.py:567
  160.8 3.6 %owned1.1 = bf16[2,2,64,64,128]{4,3,2,1,0:T(8,128)(2,1)} custom-call(bf16[16,2,4,64,128]{4,3,2,1,0:T(8,128)(2,1)} %all-to-all-done.4.refs_0_, bf16[16,104,256]{2,1,0:T(8,128)(2,1)S(1)} %all-to-all-done.5.refs_0_.refs_1_, bf16[2,2,64,64,128]{4,3,2,1,0:T(8,128)(2,1)} %owned0.1.refs_2_), custom_call_target="tpu_custom_call", output_to_operand_aliasing={{}: (2, {})} | custom-call | tf_op jit(solution)/shard_map/owned1/pallas_call | solution.py:432
  164.4 0.6 copy.43
  (33 shorter events, 0.1 us)
Async XLA Ops:
  7.2 19.8 %copy-start.12 = (s32[4,2]{0,1:T(2,128)S(1)}, s32[4,2]{0,1:T(2,128)}, u32[]{:S(2)}) copy-start(s32[4,2]{0,1:T(2,128)} %param.35) | copy-start | bytes 100
  7.2 20.0 %copy-start.17 = (s32[8]{0:T(128)S(1)}, s32[8]{0:T(128)}, u32[]{:S(2)}) copy-start(s32[8]{0:T(128)} %param.34) | copy-start | bytes 100
  7.2 20.0 %copy-start.16 = (s32[8]{0:T(128)S(1)}, s32[8]{0:T(128)}, u32[]{:S(2)}) copy-start(s32[8]{0:T(128)} %param.33) | copy-start | bytes 100
  7.2 46.4 %all-gather.5.cloned.1.call-start = ((), (), s32[]{:S(2)}) async-start(), calls=%async_computation.6 | async-start | bytes 5308416 | tf_op jit(solution)/shard_map/all_gather | solution.py:539
  7.2 8.4 %collective-permute-start = (bf16[64,256]{1,0:T(8,128)(2,1)}, bf16[64,256]{1,0:T(8,128)(2,1)S(1)}, u32[]{:S(2)}, u32[]{:S(2)}) collective-permute-start(bf16[64,256]{1,0:T(8,128)(2,1)} %param.18), channel_id=1, source_target_pairs={{0,0},{1,8},{2,16},{3,24},{4,32},{5,40},{6,48},{7,56},{8,64},{9,72... | collective-permute-start | bytes 98312 | tf_op jit(solution)/shard_map/ppermute | solution.py:530
  16.5 20.4 %all-to-all-start = ((bf16[16,64,256]{2,1,0:T(8,128)(2,1)}), bf16[16,64,256]{2,1,0:T(8,128)(2,1)S(1)}, u32[]{:S(2)}, u32[]{:S(2)}) async-start(bf16[16,64,256]{2,1,0:T(8,128)(2,1)} %broadcast_in_dim.4), calls=%async_computation | async-start | bytes 1048576 | tf_op jit(solution)/shard_map/all_to_all | solution.py:491
  26.9 87.0 %all-gather.7.cloned.1.call-start = ((), (), s32[]{:S(2)}) async-start(), calls=%async_computation.7 | async-start | bytes 5308416 | tf_op jit(solution)/shard_map/all_gather | solution.py:545
  27.8 6.1 %copy-start.9 = (bf16[2,256,2,256]{3,2,1,0:T(2,128)(2,1)S(1)}, bf16[2,256,2,256]{3,2,1,0:T(2,128)(2,1)}, u32[]{:S(2)}) copy-start(bf16[2,256,2,256]{3,2,1,0:T(2,128)(2,1)} %param.20) | copy-start | bytes 1572868
  33.9 10.3 %copy-start.10 = (bf16[2,8,3,256]{3,1,2,0:T(8,128)(2,1)S(1)}, bf16[2,8,3,256]{3,1,2,0:T(8,128)(2,1)}, u32[]{:S(2)}) copy-start(bf16[2,8,3,256]{3,1,2,0:T(8,128)(2,1)} %param.30) | copy-start | bytes 73732
  33.9 10.9 %copy-start.11 = (bf16[2,8,3,256]{3,1,2,0:T(8,128)(2,1)S(1)}, bf16[2,8,3,256]{3,1,2,0:T(8,128)(2,1)}, u32[]{:S(2)}) copy-start(bf16[2,8,3,256]{3,1,2,0:T(8,128)(2,1)} %param.31) | copy-start | bytes 73732
  33.9 11.5 %copy-start.13 = (f32[2,4]{1,0:T(2,128)S(1)}, f32[2,4]{1,0:T(2,128)}, u32[]{:S(2)}) copy-start(f32[2,4]{1,0:T(2,128)} %param.27) | copy-start | bytes 100
  33.9 11.5 %copy-start.14 = (f32[2,4]{1,0:T(2,128)S(1)}, f32[2,4]{1,0:T(2,128)}, u32[]{:S(2)}) copy-start(f32[2,4]{1,0:T(2,128)} %param.26) | copy-start | bytes 100
  34.0 11.5 %copy-start.15 = (f32[2,4]{1,0:T(2,128)S(1)}, f32[2,4]{1,0:T(2,128)}, u32[]{:S(2)}) copy-start(f32[2,4]{1,0:T(2,128)} %param.25) | copy-start | bytes 100
  37.0 16.7 %copy-start.8 = (bf16[16,64,256]{2,1,0:T(8,128)(2,1)}, bf16[16,64,256]{2,1,0:T(8,128)(2,1)S(1)}, u32[]{:S(2)}) copy-start(bf16[16,64,256]{2,1,0:T(8,128)(2,1)S(1)} %all-to-all-done.refs_2_) | copy-start | bytes 1572868
  37.0 33.9 %all-to-all-start.1 = ((bf16[16,2,4,64,128]{4,3,2,1,0:T(8,128)(2,1)}), bf16[16,2,4,64,128]{4,3,2,1,0:T(8,128)(2,1)}, u32[]{:S(2)}, u32[]{:S(2)}) async-start(bf16[16,2,4,64,128]{4,3,2,1,0:T(8,128)(2,1)} %starts0.1), calls=%async_computation.1 | async-start | bytes 4194304 | tf_op jit(solution)/shard_map/all_to_all | solution.py:491
  53.6 23.1 %copy-start = (f32[2,8,4,64,128]{4,3,2,1,0:T(8,128)S(1)}, f32[2,8,4,64,128]{4,3,2,1,0:T(8,128)}, u32[]{:S(2)}) copy-start(f32[2,8,4,64,128]{4,3,2,1,0:T(8,128)} %state_ref.7) | copy-start | bytes 6291460
  70.9 18.0 %all-to-all-start.2 = ((bf16[16,104,256]{2,1,0:T(8,128)(2,1)}), bf16[16,104,256]{2,1,0:T(8,128)(2,1)S(1)}, u32[]{:S(2)}, u32[]{:S(2)}) async-start(bf16[16,104,256]{2,1,0:T(8,128)(2,1)} %get-tuple-element.49), calls=%async_computation.2 | async-start | bytes 1703936 | tf_op jit(solution)/shard_map/all_to_all | solution.py:491
  76.7 1.0 copy-start.3
  77.7 0.9 copy-start.5
  78.6 0.8 copy-start.7
  103.6 33.5 %all-to-all-start.4 = ((bf16[16,2,4,64,128]{4,3,2,1,0:T(8,128)(2,1)}), bf16[16,2,4,64,128]{4,3,2,1,0:T(8,128)(2,1)}, u32[]{:S(2)}, u32[]{:S(2)}) async-start(bf16[16,2,4,64,128]{4,3,2,1,0:T(8,128)(2,1)} %starts1.1), calls=%async_computation.4 | async-start | bytes 4194304 | tf_op jit(solution)/shard_map/all_to_all | solution.py:491
  113.9 29.1 %copy-start.1 = (f32[2,8,4,64,128]{4,3,2,1,0:T(8,128)S(1)}, f32[2,8,4,64,128]{4,3,2,1,0:T(8,128)}, u32[]{:S(2)}) copy-start(f32[2,8,4,64,128]{4,3,2,1,0:T(8,128)} %state_ref.7) | copy-start | bytes 6291460
  137.1 18.1 %all-to-all-start.5 = ((bf16[16,104,256]{2,1,0:T(8,128)(2,1)}), bf16[16,104,256]{2,1,0:T(8,128)(2,1)S(1)}, u32[]{:S(2)}, u32[]{:S(2)}) async-start(bf16[16,104,256]{2,1,0:T(8,128)(2,1)} %get-tuple-element.61), calls=%async_computation.5 | async-start | bytes 1703936 | tf_op jit(solution)/shard_map/all_to_all | solution.py:491
  143.0 1.0 copy-start.2
  144.0 0.9 copy-start.4
  144.9 0.8 copy-start.6
  155.4 9.0 %collective-permute-start.1 = (bf16[64,256]{1,0:T(8,128)(2,1)S(1)}, bf16[64,256]{1,0:T(8,128)(2,1)S(1)}, u32[]{:S(2)}, u32[]{:S(2)}) collective-permute-start(bf16[64,256]{1,0:T(8,128)(2,1)S(1)} %update_last.1), channel_id=1, source_target_pairs={{0,0},{8,1},{16,2},{24,3},{32,4},{40,5},{48,6},{56,7},{64,8},{72,9... | collective-permute-start | bytes 98312 | tf_op jit(solution)/shard_map/ppermute | solution.py:567
Sparse Core Ops, SparseCore 0:
  15.8 37.7 all-gather.4
  55.3 34.2 all-gather.6
